TPU v7x, 32 devices: a whole 2x2x4 slice. The times are simulated.
32 devices in a mesh: dp: 8 (over y, x, core), mp: 4 (over z).
Axes of the slice: x: 2, y: 2, z: 4, core: 2. Of those that a mesh axis runs over, the one named last changes fastest.
Arguments:
- hidden_in: bfloat16 [8, 2048, 1024], P('dp', 'mp'), may hold values from -6 to 6
- segment_ids: int32 [8, 2048], P('dp'), may hold values from 0 to 6, as said below
- first_values: bfloat16 [8, 2048, 1024], P('dp', None, 'mp'), may hold values from -20 to 20
- grad_out: bfloat16 [8, 2048, 1024], P('dp', 'mp'), may hold values from -6 to 6
- input_proj: float32 [3, 1024, 1024], P(None, 'dp', 'mp'), may hold values from -0.1875 to 0.1875
- output_proj: float32 [1024, 1024], P('mp', 'dp'), may hold values from -3 to 3
- expand_proj: float32 [2, 1024, 2816], P(None, 'dp', 'mp'), may hold values from -0.1875 to 0.1875
- reduce_proj: float32 [2816, 1024], P('mp', 'dp'), may hold values from -0.1875 to 0.1875
- norm_gains: float32 [2, 1024], P(None, 'dp'), may hold values from 0.5 to 1.5
- old_moment_input: float32 [3, 1024, 1024], P(None, 'dp', 'mp'), may hold values from -1536 to 1536
- old_moment_output: float32 [1024, 1024], P('mp', 'dp'), may hold values from -96 to 96
- old_moment_expand: float32 [2, 1024, 2816], P(None, 'dp', 'mp'), may hold values from -512 to 512
- old_moment_reduce: float32 [2816, 1024], P('mp', 'dp'), may hold values from -448 to 448
- old_moment_gains: float32 [2, 1024], P(None, 'dp'), may hold values from -1280 to 1280
- old_square_input: float32 [3, 1024, 1024], P(None, 'dp', 'mp'), may hold values from 63717.918 to 254871.67
- old_square_output: float32 [1024, 1024], P('mp', 'dp'), may hold values from 248.48643 to 993.94574
- old_square_expand: float32 [2, 1024, 2816], P(None, 'dp', 'mp'), may hold values from 6434.444 to 25737.775
- old_square_reduce: float32 [2816, 1024], P('mp', 'dp'), may hold values from 5898.24 to 23592.96
- old_square_gains: float32 [2, 1024], P(None, 'dp'), may hold values from 47349.76 to 189399.05
Outputs:
- layer_output: bfloat16 [8, 2048, 1024], P('dp', 'mp')
- input_grad: float32 [8, 2048, 1024], P('dp', 'mp')
- values_grad: float32 [8, 2048, 1024], P('dp', None, 'mp')
- value_norms: float32 [2], replicated
- updated_input: float32 [3, 1024, 1024], P(None, 'dp', 'mp')
- updated_output: float32 [1024, 1024], P('mp', 'dp')
- updated_expand: float32 [2, 1024, 2816], P(None, 'dp', 'mp')
- updated_reduce: float32 [2816, 1024], P('mp', 'dp')
- updated_gains: float32 [2, 1024], P(None, 'dp')
- moment_input: float32 [3, 1024, 1024], P(None, 'dp', 'mp')
- moment_output: float32 [1024, 1024], P('mp', 'dp')
- moment_expand: float32 [2, 1024, 2816], P(None, 'dp', 'mp')
- moment_reduce: float32 [2816, 1024], P('mp', 'dp')
- moment_gains: float32 [2, 1024], P(None, 'dp')
- square_input: float32 [3, 1024, 1024], P(None, 'dp', 'mp')
- square_output: float32 [1024, 1024], P('mp', 'dp')
- square_expand: float32 [2, 1024, 2816], P(None, 'dp', 'mp')
- square_reduce: float32 [2816, 1024], P('mp', 'dp')
- square_gains: float32 [2, 1024], P(None, 'dp')
Inputs may be any that keep to these rules, and one draw needn't show every extreme that they name: `segment_ids`: along each row the ids start at 0, never fall and end at 6 (seven documents); in every row one document begins within the first 512 positions and ends within the last 512.
All inputs are finite; a program needn't handle non-finite values.
Results may differ from a plain program's by a relative error of at most 0.023.
Values may be sent and summed in bfloat16 or wider, within the bound.
A program may use at most 192 MiB of HBM per device.

v0:
```python
import math

import jax
import jax.numpy as jnp
from jax import lax
from jax.sharding import PartitionSpec as P

D = 1024
HEADS = 16
HD = 64
FF = 2816
LEN = 2048
STEP = 5


def rope_tables(seg_row, head_size):
    length = seg_row.shape[0]
    places = jnp.arange(length, dtype=jnp.int32)
    is_fresh = jnp.concatenate([jnp.ones((1,), jnp.bool_), seg_row[1:] != seg_row[:-1]])
    begins = lax.cummax(jnp.where(is_fresh, places, 0), axis=0)
    offset = (places - begins).astype(jnp.float32)
    inverse_rates = 10000.0 ** (-2.0 * jnp.arange(head_size // 2, dtype=jnp.float32) / head_size)
    angles = offset[:, None] * inverse_rates[None, :]
    return (jnp.cos(angles)[:, None, :], jnp.sin(angles)[:, None, :])


def rotate(values, cosine, sine_part, forward):
    half_size = values.shape[-1] // 2
    first_half = values[..., :half_size]
    second_half = values[..., half_size:]
    if forward:
        return jnp.concatenate(
            [
                first_half * cosine - second_half * sine_part,
                second_half * cosine + first_half * sine_part,
            ],
            axis=-1,
        )
    return jnp.concatenate(
        [
            first_half * cosine + second_half * sine_part,
            second_half * cosine - first_half * sine_part,
        ],
        axis=-1,
    )


def rms_factor(values):
    return lax.rsqrt(jnp.mean(values * values, axis=-1, keepdims=True) + 1e-06)


def norm_back(values, factor, gain_row, incoming):
    scaled = incoming * gain_row
    value_grad = factor * scaled - values * factor**3 * jnp.mean(
        scaled * values, axis=-1, keepdims=True
    )
    gain_grad = jnp.sum(incoming * values * factor, axis=0)
    return (value_grad, gain_grad)


def visible_block(seg_row, first_row, block_rows):
    length = seg_row.shape[0]
    query_seg = lax.dynamic_slice_in_dim(seg_row, first_row, block_rows, 0)
    query_places = first_row + jnp.arange(block_rows, dtype=jnp.int32)
    key_places = jnp.arange(length, dtype=jnp.int32)
    return (query_seg[:, None] == seg_row[None, :]) & (query_places[:, None] >= key_places[None, :])


def block_scores(queries, keys_rot, seg_row, first_row, block_rows, score_scale):
    query_block = lax.dynamic_slice_in_dim(queries, first_row, block_rows, 0)
    visible = visible_block(seg_row, first_row, block_rows)
    scores = (
        jnp.einsum("qhd,khd->hqk", query_block, keys_rot, preferred_element_type=jnp.float32)
        * score_scale
    )
    return (query_block, jnp.where(visible[None], scores, -1e30))


def attend(queries, keys_rot, mixed_values, seg_row, score_scale):
    length = queries.shape[0]
    block_rows = min(512, length)

    def one_block(block_index):
        first_row = block_index * block_rows
        query_block, scores = block_scores(
            queries, keys_rot, seg_row, first_row, block_rows, score_scale
        )
        top_score = jnp.max(scores, axis=-1, keepdims=True)
        raised = jnp.exp(scores - top_score)
        totals = jnp.sum(raised, axis=-1, keepdims=True)
        shares = (raised / totals).astype(jnp.bfloat16)
        combined = jnp.einsum(
            "hqk,khd->qhd", shares, mixed_values, preferred_element_type=jnp.float32
        )
        return (combined, (top_score + jnp.log(totals))[..., 0])

    combined, log_totals = lax.map(one_block, jnp.arange(length // block_rows, dtype=jnp.int32))
    return (combined.reshape(length, -1), log_totals)


def attend_back(queries, keys_rot, mixed_values, out_grad, log_totals, seg_row, score_scale):
    length = queries.shape[0]
    block_rows = min(512, length)

    def one_block(running, operands):
        key_sum, value_sum = running
        block_index, block_totals = operands
        first_row = block_index * block_rows
        query_block, scores = block_scores(
            queries, keys_rot, seg_row, first_row, block_rows, score_scale
        )
        grad_block = lax.dynamic_slice_in_dim(out_grad, first_row, block_rows, 0)
        shares = jnp.exp(scores - block_totals[..., None])
        share_grad = jnp.einsum(
            "qhd,khd->hqk", grad_block, mixed_values, preferred_element_type=jnp.float32
        )
        inner = jnp.sum(shares * share_grad, axis=-1, keepdims=True)
        score_grad = (shares * (share_grad - inner)).astype(jnp.bfloat16)
        query_grad = (
            jnp.einsum("hqk,khd->qhd", score_grad, keys_rot, preferred_element_type=jnp.float32)
            * score_scale
        )
        key_sum = (
            key_sum
            + jnp.einsum(
                "hqk,qhd->khd", score_grad, query_block, preferred_element_type=jnp.float32
            )
            * score_scale
        )
        value_sum = value_sum + jnp.einsum(
            "hqk,qhd->khd",
            shares.astype(jnp.bfloat16),
            grad_block,
            preferred_element_type=jnp.float32,
        )
        return ((key_sum, value_sum), query_grad)

    empty_sum = jnp.zeros(keys_rot.shape, jnp.float32)
    (key_grad, value_grad), query_grad = lax.scan(
        one_block,
        (empty_sum, empty_sum),
        (jnp.arange(length // block_rows, dtype=jnp.int32), log_totals),
    )
    return (query_grad.reshape(keys_rot.shape), key_grad, value_grad)


def adamw(master, gradient, moment, square, step_rate, decay):
    new_moment = 0.5 * moment + 0.5 * gradient
    new_square = 0.5 * square + 0.5 * gradient * gradient
    correct = 1.0 - 0.5**STEP
    update = new_moment / correct / (jnp.sqrt(new_square / correct) + 1e-08)
    return (master - step_rate * (update + decay * master), new_moment, new_square)


def shards(
    hidden_in,
    segment_ids,
    first_values,
    grad_out,
    input_proj,
    output_proj,
    expand_proj,
    reduce_proj,
    norm_gains,
    old_moment_input,
    old_moment_output,
    old_moment_expand,
    old_moment_reduce,
    old_moment_gains,
    old_square_input,
    old_square_output,
    old_square_expand,
    old_square_reduce,
    old_square_gains,
):
    attn_weight, out_weight, expand_weight, reduce_weight, gains_low = (
        lax.all_gather(input_proj.astype(jnp.bfloat16), "dp", axis=1, tiled=True),
        lax.all_gather(output_proj.astype(jnp.bfloat16), "dp", axis=1, tiled=True),
        lax.all_gather(expand_proj.astype(jnp.bfloat16), "dp", axis=1, tiled=True),
        lax.all_gather(reduce_proj.astype(jnp.bfloat16), "dp", axis=1, tiled=True),
        lax.all_gather(norm_gains.astype(jnp.bfloat16), "dp", axis=1, tiled=True),
    )
    gains = gains_low.astype(jnp.float32)
    hidden = hidden_in[0].astype(jnp.float32)
    seg_row = segment_ids[0]
    length = seg_row.shape[0]
    first_in = first_values[0].astype(jnp.float32)
    local_heads = attn_weight.shape[2] // HD
    score_scale = 1.0 / math.sqrt(HD)
    factor_one = rms_factor(hidden)
    normed_one = (hidden * factor_one * gains[0]).astype(jnp.bfloat16)
    all_normed, all_grad_out = (
        lax.all_gather(normed_one, "mp", axis=0, tiled=True),
        lax.all_gather(grad_out[0], "mp", axis=0, tiled=True),
    )
    projected = jnp.einsum(
        "td,cde->cte", all_normed, attn_weight, preferred_element_type=jnp.float32
    )
    cosine, sine_part = rope_tables(seg_row, HD)
    queries = rotate(projected[0].reshape(length, local_heads, HD), cosine, sine_part, True).astype(
        jnp.bfloat16
    )
    keys_rot = rotate(
        projected[1].reshape(length, local_heads, HD), cosine, sine_part, True
    ).astype(jnp.bfloat16)
    blended = 0.5 * projected[2] + 0.5 * first_in
    mixed_values = blended.astype(jnp.bfloat16).reshape(length, local_heads, HD)
    square_terms = jnp.stack([jnp.sum(first_in * first_in), jnp.sum(blended * blended)])
    attended, log_totals = attend(queries, keys_rot, mixed_values, seg_row, score_scale)
    attended_low = attended.astype(jnp.bfloat16)
    rows_part = attended_low
    branch = lax.psum_scatter(
        jnp.dot(rows_part, out_weight, preferred_element_type=jnp.float32),
        "mp",
        scatter_dimension=0,
        tiled=True,
    )
    middle = hidden + branch
    factor_two = rms_factor(middle)
    normed_two = (middle * factor_two * gains[1]).astype(jnp.bfloat16)
    all_normed_two = lax.all_gather(normed_two, "mp", axis=0, tiled=True)
    gate_up = jnp.einsum(
        "td,cdf->ctf", all_normed_two, expand_weight, preferred_element_type=jnp.float32
    )
    gate_sig = jax.nn.sigmoid(gate_up[0])
    gate_act = gate_up[0] * gate_sig
    activated = (gate_act * gate_up[1]).astype(jnp.bfloat16)
    rows_part = activated
    feed_out = lax.psum_scatter(
        jnp.dot(rows_part, reduce_weight, preferred_element_type=jnp.float32).astype(jnp.bfloat16),
        "mp",
        scatter_dimension=0,
        tiled=True,
    ).astype(jnp.float32)
    layer_output = (middle + feed_out).astype(jnp.bfloat16)[None]
    hidden_grad = jnp.einsum(
        "td,fd->tf", all_grad_out, reduce_weight, preferred_element_type=jnp.float32
    )
    reduce_grad = jnp.einsum(
        "tf,td->fd", activated, all_grad_out, preferred_element_type=jnp.float32
    )
    gate_grad = hidden_grad * gate_up[1] * gate_sig * (1.0 + gate_up[0] * (1.0 - gate_sig))
    up_grad = hidden_grad * gate_act
    pair_grad = jnp.stack([gate_grad, up_grad]).astype(jnp.bfloat16)
    expand_grad = jnp.einsum(
        "ctf,td->cdf", pair_grad, all_normed_two, preferred_element_type=jnp.float32
    )
    rows_part = pair_grad
    normed_two_grad = lax.psum_scatter(
        jnp.einsum(
            "ctf,cdf->td", rows_part, expand_weight, preferred_element_type=jnp.float32
        ).astype(jnp.bfloat16),
        "mp",
        scatter_dimension=0,
        tiled=True,
    ).astype(jnp.float32)
    middle_part, gain_two_grad = norm_back(middle, factor_two, gains[1], normed_two_grad)
    middle_grad = grad_out[0].astype(jnp.float32) + middle_part
    branch_low = middle_grad.astype(jnp.bfloat16)
    all_branch = lax.all_gather(branch_low, "mp", axis=0, tiled=True)
    out_grad = jnp.einsum("te,td->ed", attended_low, all_branch, preferred_element_type=jnp.float32)
    attended_grad = jnp.einsum(
        "td,ed->te", all_branch, out_weight, preferred_element_type=jnp.float32
    ).astype(jnp.bfloat16)
    query_grad, key_grad, mix_grad = attend_back(
        queries,
        keys_rot,
        mixed_values,
        attended_grad.reshape(length, local_heads, HD),
        log_totals,
        seg_row,
        score_scale,
    )
    query_grad = rotate(query_grad, cosine, sine_part, False).reshape(length, -1)
    key_grad = rotate(key_grad, cosine, sine_part, False).reshape(length, -1)
    mix_grad = mix_grad.reshape(length, -1)
    values_grad = (0.5 * mix_grad)[None]
    proj_grad = jnp.stack([query_grad, key_grad, 0.5 * mix_grad]).astype(jnp.bfloat16)
    attn_grad = jnp.einsum("cte,td->cde", proj_grad, all_normed, preferred_element_type=jnp.float32)
    rows_part = proj_grad
    normed_one_grad = lax.psum_scatter(
        jnp.einsum(
            "cte,cde->td", rows_part, attn_weight, preferred_element_type=jnp.float32
        ).astype(jnp.bfloat16),
        "mp",
        scatter_dimension=0,
        tiled=True,
    ).astype(jnp.float32)
    input_part, gain_one_grad = norm_back(hidden, factor_one, gains[0], normed_one_grad)
    input_grad = (middle_grad + input_part)[None]
    attn_total, out_total, expand_total, reduce_total = (
        lax.psum_scatter(
            attn_grad.astype(jnp.bfloat16), "dp", scatter_dimension=1, tiled=True
        ).astype(jnp.float32),
        lax.psum_scatter(
            out_grad.astype(jnp.bfloat16), "dp", scatter_dimension=1, tiled=True
        ).astype(jnp.float32),
        lax.psum_scatter(
            expand_grad.astype(jnp.bfloat16), "dp", scatter_dimension=1, tiled=True
        ).astype(jnp.float32),
        lax.psum_scatter(
            reduce_grad.astype(jnp.bfloat16), "dp", scatter_dimension=1, tiled=True
        ).astype(jnp.float32),
    )
    gain_totals, square_sums = lax.psum(
        (jnp.stack([gain_one_grad, gain_two_grad]), square_terms), ("dp", "mp")
    )
    gain_width = norm_gains.shape[1]
    gain_total = lax.dynamic_slice_in_dim(
        gain_totals, lax.axis_index("dp") * gain_width, gain_width, 1
    )
    value_norms = jnp.sqrt(square_sums / (lax.axis_size("dp") * length * D))
    new_input = adamw(input_proj, attn_total, old_moment_input, old_square_input, D ** (-0.5), 0.1)
    new_output = adamw(
        output_proj,
        out_total,
        old_moment_output,
        old_square_output,
        max(1, 8 * HEADS * HD // LEN) ** (-0.5),
        0.1,
    )
    new_expand = adamw(
        expand_proj, expand_total, old_moment_expand, old_square_expand, D ** (-0.5), 0.1
    )
    new_reduce = adamw(
        reduce_proj, reduce_total, old_moment_reduce, old_square_reduce, (FF // 3) ** (-0.5), 0.1
    )
    new_gains = adamw(norm_gains, gain_total, old_moment_gains, old_square_gains, 0.2, 0.0)
    return (
        layer_output,
        input_grad,
        values_grad,
        value_norms,
        new_input[0],
        new_output[0],
        new_expand[0],
        new_reduce[0],
        new_gains[0],
        new_input[1],
        new_output[1],
        new_expand[1],
        new_reduce[1],
        new_gains[1],
        new_input[2],
        new_output[2],
        new_expand[2],
        new_reduce[2],
        new_gains[2],
    )


def solution(mesh):
    return jax.shard_map(
        shards,
        mesh=mesh,
        in_specs=(
            P("dp", "mp", None),
            P("dp", None),
            P("dp", None, "mp"),
            P("dp", "mp", None),
            P(None, "dp", "mp"),
            P("mp", "dp"),
            P(None, "dp", "mp"),
            P("mp", "dp"),
            P(None, "dp"),
            P(None, "dp", "mp"),
            P("mp", "dp"),
            P(None, "dp", "mp"),
            P("mp", "dp"),
            P(None, "dp"),
            P(None, "dp", "mp"),
            P("mp", "dp"),
            P(None, "dp", "mp"),
            P("mp", "dp"),
            P(None, "dp"),
        ),
        out_specs=(
            P("dp", "mp", None),
            P("dp", "mp", None),
            P("dp", None, "mp"),
            P(),
            P(None, "dp", "mp"),
            P("mp", "dp"),
            P(None, "dp", "mp"),
            P("mp", "dp"),
            P(None, "dp"),
            P(None, "dp", "mp"),
            P("mp", "dp"),
            P(None, "dp", "mp"),
            P("mp", "dp"),
            P(None, "dp"),
            P(None, "dp", "mp"),
            P("mp", "dp"),
            P(None, "dp", "mp"),
            P("mp", "dp"),
            P(None, "dp"),
        ),
        check_vma=False,
    )
```

profile of v0, /device:TPU:0, one launch (start us, length us, event | category | flops | bytes accessed | tf_op | source)
XLA Modules:
  0.0 1261.3 jit_solution(11477510304041689263)
XLA Ops:
  9.9 10.2 all_gather.27
  26.9 13.0 %all_gather.30 = bf16[256,1024]{1,0:T(8,128)(2,1)} all-gather(bf16[256,128]{1,0:T(8,128)(2,1)S(1)} %convert_element_type.144), channel_id=1, replica_groups=mesh['dp'=8,'mp'=4] {'dp'}, dimensions={1}, use_global_device_ids=true | all-gather | bytes 589824 | tf_op jit(solution)/shard_map/all_gather | solution.py:178
  40.9 82.5 %all-gather.9.cloned.1.call-done = bf16[2048,1024]{1,0:T(8,128)(2,1)} async-done(((bf16[512,1024]{1,0:T(8,128)(2,1)}), bf16[2048,1024]{1,0:T(8,128)(2,1)}) %all-gather.9.cloned.1.call-update) | async-done | bytes 4194320 | tf_op jit(solution)/shard_map/all_gather | solution.py:193
  123.5 6.0 fusion.49
  132.4 64.0 %while.27 = (s32[]{:T(128)}, bf16[4,512,4,64]{1,3,2,0:T(8,128)(2,1)}, f32[4,4,512]{2,1,0:T(4,128)}, s32[4]{0:T(128)S(1)}, s32[2048]{0:T(1024)S(1)}, /*index=5*/s...) while((s32[]{:T(128)}, ...), condition=%wide.region_6.7_spmd, body=%wide.region_3.0_spmd.sunk | while | flops 1127217664 | bytes 65882380 | solution.py:97
  142.5 4.8 fusion.153
  207.0 141.2 %reduce-scatter.15.cloned.1.call-done = f32[512,1024]{1,0:T(8,128)} async-done(((f32[2048,1024]{1,0:T(8,128)}), f32[512,1024]{1,0:T(8,128)}) %reduce-scatter.15.cloned.1.call-update) | async-done | bytes 2097168 | tf_op jit(solution)/shard_map/reduce_scatter | solution.py:212
  353.3 29.7 %all-gather.15.cloned.1.call-done = bf16[2,1024,704]{1,2,0:T(8,128)(2,1)} async-done(((bf16[2,128,704]{1,2,0:T(8,128)(2,1)}), bf16[2,1024,704]{1,2,0:T(8,128)(2,1)}) %all-gather.15.cloned.1.call-update) | async-done | bytes 2883600 | tf_op jit(solution)/shard_map/all_gather | solution.py:179
  383.0 82.8 %all-gather.13.cloned.1.call-done = bf16[2048,1024]{1,0:T(8,128)(2,1)} async-done(((bf16[512,1024]{1,0:T(8,128)(2,1)}), bf16[2048,1024]{1,0:T(8,128)(2,1)}) %all-gather.13.cloned.1.call-update) | async-done | bytes 4194320 | tf_op jit(solution)/shard_map/all_gather | solution.py:221
  465.8 11.5 convolution_bitcast_fusion
  477.2 14.7 %all-gather.17.cloned.1.call-done = bf16[704,1024]{1,0:T(8,128)(2,1)} async-done(((bf16[704,128]{1,0:T(8,128)(2,1)}), bf16[704,1024]{1,0:T(8,128)(2,1)}) %all-gather.17.cloned.1.call-update) | async-done | bytes 1441808 | tf_op jit(solution)/shard_map/all_gather | solution.py:180
  491.9 82.4 %all-gather.21.cloned.1.call-done = bf16[1,2048,1024]{2,1,0:T(8,128)(2,1)} async-done(((bf16[1,512,1024]{2,1,0:T(8,128)(2,1)}), bf16[1,2048,1024]{2,1,0:T(8,128)(2,1)}) %all-gather.21.cloned.1.call-update) | async-done | bytes 4194320 | tf_op jit(solution)/shard_map/all_gather | solution.py:194
  574.3 11.3 fusion.53
  588.0 8.3 bitcast_convert_fusion.1
  596.5 75.2 %reduce-scatter.19.cloned.1.call-done = bf16[512,1024]{1,0:T(8,128)(2,1)} async-done(((bf16[2048,1024]{1,0:T(8,128)(2,1)}), bf16[512,1024]{1,0:T(8,128)(2,1)}) %reduce-scatter.19.cloned.1.call-update) | async-done | bytes 1048592 | tf_op jit(solution)/shard_map/reduce_scatter | solution.py:249
  676.2 6.2 fusion.79
  684.1 11.1 convert_bitcast_fusion
  695.2 8.8 copy.70
  704.0 7.6 reshape.342
  711.7 45.9 %all-gather.19.cloned.1.call-done = bf16[2048,1024]{1,0:T(8,128)(2,1)} async-done(((bf16[512,1024]{1,0:T(8,128)(2,1)}), bf16[2048,1024]{1,0:T(8,128)(2,1)}) %all-gather.19.cloned.1.call-update) | async-done | bytes 4194320 | tf_op jit(solution)/shard_map/all_gather | solution.py:260
  762.0 237.2 %while.28 = (s32[]{:T(128)}, f32[2048,4,64]{0,2,1:T(8,128)}, f32[2048,4,64]{0,2,1:T(8,128)}, f32[4,512,4,64]{1,0,3,2:T(4,128)}, s32[4]{0:T(128)S(1)}, /*index=5*...) while((s32[]{:T(128)}, f32[2048,4,64]{0,2,1:T(8,128)}, ...), condition=%wide.region_14.15_spmd.clone, body=%wide.region_12.14_spmd.clone.sunk | while | flops 2753165824 | bytes 183118192 | solution.py:139
  769.0 7.2 fusion.166
  776.2 11.5 multiply_reduce_fusion.4
  787.8 11.0 multiply_convert_fusion.6
  798.8 6.2 fusion.167
  809.4 11.2 dynamic_update_slice.19
  827.4 7.6 fusion.166
  835.0 11.5 multiply_reduce_fusion.4
  846.6 11.0 multiply_convert_fusion.6
  857.6 6.2 fusion.167
  868.9 11.1 dynamic_update_slice.19
  886.8 7.6 fusion.166
  894.5 11.5 multiply_reduce_fusion.4
  906.0 11.0 multiply_convert_fusion.6
  917.0 6.2 fusion.167
  928.4 11.1 dynamic_update_slice.19
  946.2 7.6 fusion.166
  953.9 11.5 multiply_reduce_fusion.4
  965.4 11.0 multiply_convert_fusion.6
  976.4 6.2 fusion.167
  987.8 11.1 dynamic_update_slice.19
  1021.3 6.4 bitcast_convert_fusion
  1029.2 6.8 fusion.82
  1036.2 7.7 convolution_convert_fusion
  1056.9 70.8 %reduce-scatter.21.cloned.1.call-done = bf16[512,1024]{1,0:T(8,128)(2,1)} async-done(((bf16[2048,1024]{1,0:T(8,128)(2,1)}), bf16[512,1024]{1,0:T(8,128)(2,1)}) %reduce-scatter.21.cloned.1.call-update) | async-done | bytes 1048592 | tf_op jit(solution)/shard_map/reduce_scatter | solution.py:281
  1131.7 38.7 %reduce-scatter.23.cloned.1.call-done = bf16[3,128,256]{2,1,0:T(8,128)(2,1)} async-done(((bf16[3,1024,256]{2,1,0:T(8,128)(2,1)}), bf16[3,128,256]{2,1,0:T(8,128)(2,1)}) %reduce-scatter.23.cloned.1.call-update) | async-done | bytes 196624 | tf_op jit(solution)/shard_map/reduce_scatter | solution.py:292
  1172.8 42.0 %all-reduce = (f32[2]{0:T(128)S(1)}, f32[2,1024]{1,0:T(2,128)S(1)}) all-reduce(f32[2]{0:T(128)} %pad_maximum_fusion.13, f32[2,1024]{1,0:T(2,128)} %pad_maximum_fusion.12), channel_id=1, replica_groups=mesh['dp'=8,'mp'=4] {'dp','mp'}, use_global_device_ids=true, to_apply=%region_19.20 | all-reduce | flops 2050 | bytes 16400 | tf_op jit(solution)/shard_map/psum | solution.py:305
  1217.3 33.0 %reduce-scatter.17.cloned.1.call-done = bf16[512,1024]{1,0:T(8,128)(2,1)} async-done(((bf16[2048,1024]{1,0:T(8,128)(2,1)}), bf16[512,1024]{1,0:T(8,128)(2,1)}) %reduce-scatter.17.cloned.1.call-update) | async-done | bytes 1048592 | tf_op jit(solution)/shard_map/reduce_scatter | solution.py:229
  (303 shorter events, 191.8 us)
Async XLA Ops:
  7.2 18.2 %copy-start.22 = (s32[1,2048]{1,0:T(1,128)S(1)}, s32[1,2048]{1,0:T(1,128)}, u32[]{:S(2)}) copy-start(s32[1,2048]{1,0:T(1,128)} %param.24) | copy-start | bytes 24580
  7.2 18.9 %copy-start.36 = (f32[256,128]{1,0:T(8,128)S(1)}, f32[256,128]{1,0:T(8,128)}, u32[]{:S(2)}) copy-start(f32[256,128]{1,0:T(8,128)} %param.28) | copy-start | bytes 393220
  7.2 18.9 %copy-start.28 = (bf16[1,2048,256]{2,1,0:T(8,128)(2,1)S(1)}, bf16[1,2048,256]{2,1,0:T(8,128)(2,1)}, u32[]{:S(2)}) copy-start(bf16[1,2048,256]{2,1,0:T(8,128)(2,1)} %param.25) | copy-start | bytes 3145732
  7.2 33.7 %all-gather.11.cloned.1.call-start = ((), (), s32[]{:S(2)}) async-start(), calls=%async_computation.9 | async-start | bytes 1769472 | tf_op jit(solution)/shard_map/all_gather | solution.py:177
  9.2 114.3 %all-gather.9.cloned.1.call-start = ((), (), s32[]{:S(2)}) async-start(), calls=%async_computation.8 | async-start | bytes 5242880 | tf_op jit(solution)/shard_map/all_gather | solution.py:193
  25.4 322.9 %reduce-scatter.15.cloned.1.call-start = ((), (), s32[]{:S(2)}) async-start(), calls=%async_computation.10 | async-start | bytes 10485760 | tf_op jit(solution)/shard_map/reduce_scatter | solution.py:212
  40.9 90.6 %copy-start.14 = (f32[2048,32]{0,1:T(8,128)}, f32[2048,32]{0,1:T(8,128)S(1)}, u32[]{:S(2)}) copy-start(f32[2048,32]{0,1:T(8,128)S(1)} %get-tuple-element.304) | copy-start | bytes 786436
  40.9 90.6 %copy-start.16 = (f32[2048,32]{0,1:T(8,128)}, f32[2048,32]{0,1:T(8,128)S(1)}, u32[]{:S(2)}) copy-start(f32[2048,32]{0,1:T(8,128)S(1)} %get-tuple-element.305) | copy-start | bytes 786436
  196.4 8.7 copy-start.5
  196.4 8.7 copy-start.7
  205.1 177.9 %all-gather.15.cloned.1.call-start = ((), (), s32[]{:S(2)}) async-start(), calls=%async_computation.12 | async-start | bytes 3244032 | tf_op jit(solution)/shard_map/all_gather | solution.py:179
  207.0 143.5 %copy-start.39 = (f32[1,1024]{1,0:T(1,128)S(1)}, f32[1,1024]{1,0:T(1,128)}, u32[]{:S(2)}) copy-start(f32[1,1024]{1,0:T(1,128)} %get-tuple-element.306) | copy-start | bytes 12292
  207.0 258.8 %all-gather.13.cloned.1.call-start = ((), (), s32[]{:S(2)}) async-start(), calls=%async_computation.11 | async-start | bytes 5242880 | tf_op jit(solution)/shard_map/all_gather | solution.py:221
  350.4 324.0 %copy-start.3 = (f32[512,1024]{1,0:T(8,128)}, f32[512,1024]{1,0:T(8,128)S(1)}, u32[]{:S(2)}) copy-start(f32[512,1024]{1,0:T(8,128)S(1)} %get-tuple-element.279) | copy-start | bytes 6291460
  350.5 324.0 %copy-start.43 = (f32[512]{0:T(512)}, f32[512]{0:T(512)S(1)}, u32[]{:S(2)}) copy-start(f32[512]{0:T(512)S(1)} %get-tuple-element.311) | copy-start | bytes 6148
  350.5 324.0 %copy-start.47 = (f32[512]{0:T(512)}, f32[512]{0:T(512)S(1)}, u32[]{:S(2)}) copy-start(f32[512]{0:T(512)S(1)} %get-tuple-element.310) | copy-start | bytes 6148
  351.7 140.2 %all-gather.17.cloned.1.call-start = ((), (), s32[]{:S(2)}) async-start(), calls=%async_computation.13 | async-start | bytes 1622016 | tf_op jit(solution)/shard_map/all_gather | solution.py:180
  352.5 221.8 %all-gather.21.cloned.1.call-start = ((), (), s32[]{:S(2)}) async-start(), calls=%async_computation.19 | async-start | bytes 5242880 | tf_op jit(solution)/shard_map/all_gather | solution.py:194
  353.3 318.5 %reduce-scatter.19.cloned.1.call-start = ((), (), s32[]{:S(2)}) async-start(), calls=%async_computation.15 | async-start | bytes 5242880 | tf_op jit(solution)/shard_map/reduce_scatter | solution.py:249
  574.3 13.7 %copy-start.49 = (bf16[2,1024,704]{1,2,0:T(8,128)(2,1)S(1)}, bf16[2,1024,704]{1,2,0:T(8,128)(2,1)}, u32[]{:S(2)}) copy-start(bf16[2,1024,704]{1,2,0:T(8,128)(2,1)} %all-gather.15.cloned.1.call-done) | copy-start | bytes 8650756
  596.3 161.2 %all-gather.19.cloned.1.call-start = ((), (), s32[]{:S(2)}) async-start(), calls=%async_computation.16 | async-start | bytes 5242880 | tf_op jit(solution)/shard_map/all_gather | solution.py:260
  676.1 370.0 %reduce-scatter.29.cloned.1.call-start = ((), (), s32[]{:S(2)}) async-start(), calls=%async_computation.22 | async-start | bytes 1769472
  684.0 364.3 %reduce-scatter.27.cloned.1.call-start = ((), (), s32[]{:S(2)}) async-start(), calls=%async_computation.21 | async-start | bytes 3244032
  711.6 46.0 %copy-start.19 = (bf16[256,1024]{1,0:T(8,128)(2,1)S(1)}, bf16[256,1024]{1,0:T(8,128)(2,1)}, u32[]{:S(2)}) copy-start(bf16[256,1024]{1,0:T(8,128)(2,1)} %all_gather.30) | copy-start | bytes 1572868
  711.6 341.7 %reduce-scatter.25.cloned.1.call-start = ((), (), s32[]{:S(2)}) async-start(), calls=%async_computation.20 | async-start | bytes 589824
  798.8 6.2 copy-start
  805.0 15.6 %copy-start.24 = (s32[1,2048]{1,0:T(1,128)S(1)}, s32[1,2048]{1,0:T(1,128)}, u32[]{:S(2)}) copy-start(s32[1,2048]{1,0:T(1,128)} %copy-done.23) | copy-start | bytes 24580 | tf_op jit(solution)/shard_map/while
  857.6 6.2 copy-start
  863.8 16.3 %copy-start.24 = (s32[1,2048]{1,0:T(1,128)S(1)}, s32[1,2048]{1,0:T(1,128)}, u32[]{:S(2)}) copy-start(s32[1,2048]{1,0:T(1,128)} %copy-done.23) | copy-start | bytes 24580 | tf_op jit(solution)/shard_map/while
  917.0 6.2 copy-start
  923.2 16.3 %copy-start.24 = (s32[1,2048]{1,0:T(1,128)S(1)}, s32[1,2048]{1,0:T(1,128)}, u32[]{:S(2)}) copy-start(s32[1,2048]{1,0:T(1,128)} %copy-done.23) | copy-start | bytes 24580 | tf_op jit(solution)/shard_map/while
  976.4 6.2 copy-start
  982.6 16.3 %copy-start.24 = (s32[1,2048]{1,0:T(1,128)S(1)}, s32[1,2048]{1,0:T(1,128)}, u32[]{:S(2)}) copy-start(s32[1,2048]{1,0:T(1,128)} %copy-done.23) | copy-start | bytes 24580 | tf_op jit(solution)/shard_map/while
  1003.0 4.7 copy-start.2
  1003.0 4.7 copy-start.15
  1015.5 112.2 %reduce-scatter.21.cloned.1.call-start = ((), (), s32[]{:S(2)}) async-start(), calls=%async_computation.17 | async-start | bytes 5242880 | tf_op jit(solution)/shard_map/reduce_scatter | solution.py:281
  1018.9 8.7 copy-start.10
  1027.6 142.8 %reduce-scatter.23.cloned.1.call-start = ((), (), s32[]{:S(2)}) async-start(), calls=%async_computation.18 | async-start | bytes 1769472 | tf_op jit(solution)/shard_map/reduce_scatter | solution.py:292
  1036.0 214.4 %reduce-scatter.17.cloned.1.call-start = ((), (), s32[]{:S(2)}) async-start(), calls=%async_computation.14 | async-start | bytes 5242880 | tf_op jit(solution)/shard_map/reduce_scatter | solution.py:229
  1044.0 6.3 copy-start.13
  1044.0 6.3 copy-start.35
  1050.4 77.3 %copy-start.6 = (bf16[1,512,1024]{2,1,0:T(8,128)(2,1)S(1)}, bf16[1,512,1024]{2,1,0:T(8,128)(2,1)}, u32[]{:S(2)}) copy-start(bf16[1,512,1024]{2,1,0:T(8,128)(2,1)} %param.23) | copy-start | bytes 3145732
  1050.4 77.3 %copy-start.42 = (f32[1,1024]{1,0:T(1,128)S(1)}, f32[1,1024]{1,0:T(1,128)}, u32[]{:S(2)}) copy-start(f32[1,1024]{1,0:T(1,128)} %copy-done.41) | copy-start | bytes 12292
  1050.4 77.3 %copy-start.46 = (f32[512]{0:T(512)S(1)}, f32[512]{0:T(512)}, u32[]{:S(2)}) copy-start(f32[512]{0:T(512)} %copy-done.45) | copy-start | bytes 6148
  1050.4 120.0 %copy-start.25 = (f32[3,128,256]{2,1,0:T(8,128)S(1)}, f32[3,128,256]{2,1,0:T(8,128)}, u32[]{:S(2)}) copy-start(f32[3,128,256]{2,1,0:T(8,128)} %param.27) | copy-start | bytes 1179652
  1053.3 197.1 %copy-start.4 = (f32[512,1024]{1,0:T(8,128)S(1)}, f32[512,1024]{1,0:T(8,128)}, u32[]{:S(2)}) copy-start(f32[512,1024]{1,0:T(8,128)} %copy-done.3) | copy-start | bytes 6291460
  1053.3 197.1 %copy-start.40 = (f32[1,1024]{1,0:T(1,128)S(1)}, f32[1,1024]{1,0:T(1,128)}, u32[]{:S(2)}) copy-start(f32[1,1024]{1,0:T(1,128)} %get-tuple-element.306) | copy-start | bytes 12292
  1053.3 197.1 %copy-start.44 = (f32[512]{0:T(512)S(1)}, f32[512]{0:T(512)}, u32[]{:S(2)}) copy-start(f32[512]{0:T(512)} %copy-done.43) | copy-start | bytes 6148
  (37 other events, 97.3 us)
Sparse Core Ops, SparseCore 0:
  10.5 29.9 all-gather.10
  42.7 80.7 all-gather.8
  205.2 142.9 reduce-scatter.14
  350.5 32.3 all-gather.14
  385.0 80.7 all-gather.12
  468.1 23.8 all-gather.16
  493.5 80.7 all-gather.20
  596.4 75.2 reduce-scatter.18
  676.2 81.2 all-gather.18
  761.1 36.9 reduce-scatter.28
  801.8 44.8 reduce-scatter.26
  1015.7 32.8 reduce-scatter.24
  1050.9 76.7 reduce-scatter.20
  1131.4 38.9 reduce-scatter.22
  1172.6 77.7 reduce-scatter.16
where the time goes:
time: 1270 us; the launch traced here: 1260 us
  waiting for transfers between devices  698 us (55%)
  matrix products  253 us (20%)
  other arithmetic  120 us (9%)
  local copies, waits for them, and re-layouts  103 us (8%)
  blocking collectives  65.1 us (5%)
  between operations  14.8 us (1%)
    reduce_scatter x1, waiting for transfers between devices, shards(): lax.psum_scatter(jnp.dot(rows_part, out_weight, preferred_element_type=jn...  141 us
    all_gather x1, waiting for transfers between devices, shards(): all_normed_two = lax.all_gather(normed_two, 'mp', axis=0, tiled=True)  82.8 us
    all_gather x1, waiting for transfers between devices, shards(): lax.all_gather(normed_one, 'mp', axis=0, tiled=True)  82.5 us
    all_gather x1, waiting for transfers between devices, shards(): lax.all_gather(grad_out[0], 'mp', axis=0, tiled=True)  82.4 us
    reduce_scatter x1, waiting for transfers between devices, shards(): lax.psum_scatter(jnp.einsum('ctf,cdf->td', rows_part, expand_weight, pref...  75.2 us
    reduce_scatter x1, waiting for transfers between devices, shards(): lax.psum_scatter(jnp.einsum('cte,cde->td', rows_part, attn_weight, prefer...  70.8 us
    dynamic_update_slice x8, local copies, waits for them, and re-layouts, attend(): lax.map(one_block, jnp.arange(length // block_rows, dtype=jnp.int32))  46.6 us
    dot_general x4, matrix products, one_block(): jnp.einsum('qhd,khd->hqk', grad_block, mixed_values, preferred_element_ty...  46.1 us
  transfers between devices with their start and end apart: 15, of which 11 were waited for; matrix products, arithmetic and copies ran while one was open for 29% of the time, Pallas kernels for 0%

commit v1 on v0

--- a/solution.py
+++ b/solution.py
@@ -1,8 +1,11 @@
+import functools
 import math
 
 import jax
 import jax.numpy as jnp
 from jax import lax
+from jax.experimental import pallas as pl
+from jax.experimental.pallas import tpu as pltpu
 from jax.sharding import PartitionSpec as P
 
 D = 1024
@@ -11,13 +14,35 @@
 FF = 2816
 LEN = 2048
 STEP = 5
+PLANES = 4
+PIECE = 128
+BLOCKS = 4
+ATTN_ROWS = 784
+VMEM_LIMIT = 56 << 20
+OPEN_COPIES = 66
+
+
+def arrivals(plane):
+    order = [(0, 0, plane)]
+    for hop in range(1, PLANES):
+        if plane + hop < PLANES:
+            order.append((0, hop, plane + hop))
+        if plane - hop >= 0:
+            order.append((1, hop, plane - hop))
+    return order
+
+
+SLOTS = [arrivals(plane) for plane in range(PLANES)]
+
+
+def cost(flops, moved):
+    return pl.CostEstimate(flops=flops, bytes_accessed=moved, transcendentals=0)
 
 
 def rope_tables(seg_row, head_size):
     length = seg_row.shape[0]
     places = jnp.arange(length, dtype=jnp.int32)
-    is_fresh = jnp.concatenate([jnp.ones((1,), jnp.bool_), seg_row[1:] != seg_row[:-1]])
-    begins = lax.cummax(jnp.where(is_fresh, places, 0), axis=0)
+    begins = jnp.sum((seg_row[None, :] < seg_row[:, None]).astype(jnp.int32), axis=1)
     offset = (places - begins).astype(jnp.float32)
     inverse_rates = 10000.0 ** (-2.0 * jnp.arange(head_size // 2, dtype=jnp.float32) / head_size)
     angles = offset[:, None] * inverse_rates[None, :]
@@ -349,9 +374,1038 @@
     )
 
 
+def tokens_dot(a, b, left, right):
+    return lax.dot_general(a, b, (((left,), (right,)), ((), ())), preferred_element_type=jnp.float32)
+
+
+def piece_columns(place, step):
+    start = jnp.bitwise_xor(place, step) * PIECE
+    return pl.ds(pl.multiple_of(start, PIECE), PIECE)
+
+
+def turn(values, cosine, sine_part, forward):
+    lane = lax.broadcasted_iota(jnp.int32, values.shape, 1)
+    swapped = jnp.where(
+        lax.rem(lane, HD) < HD // 2, pltpu.roll(values, 96, 1), pltpu.roll(values, 32, 1)
+    )
+    if forward:
+        return values * cosine + swapped * sine_part
+    return values * cosine - swapped * sine_part
+
+
+MESH = pl.DeviceIdType.MESH
+LOG2E = 1.4426950408889634
+
+
+def flip(place, bit):
+    return place + bit - 2 * bit * lax.rem(lax.div(place, bit), 2)
+
+
+def at_plane(depth, values):
+    found = 0
+    for plane, value in enumerate(values):
+        found = found + jnp.where(depth == plane, value, 0)
+    return found
+
+
+def slot_at(depth, way, hop):
+    return at_plane(
+        depth,
+        [
+            next((k for k, s in enumerate(SLOTS[plane]) if s[:2] == (way, hop)), 0)
+            for plane in range(PLANES)
+        ],
+    )
+
+
+def columns_of(piece, width=PIECE):
+    return pl.ds(pl.multiple_of(piece * width, width), width)
+
+
+class Links:
+    def __init__(self, send, recv):
+        self.send, self.recv, self.count, self.started = send, recv, 0, []
+        self.place, self.depth = lax.axis_index("dp"), lax.axis_index("mp")
+
+    def number(self, count=1):
+        self.count += count
+        return self.count - count
+
+    def copy(self, number, source, target, to):
+        return pltpu.make_async_remote_copy(
+            src_ref=source,
+            dst_ref=target,
+            send_sem=self.send.at[number],
+            recv_sem=self.recv.at[number],
+            device_id=to,
+            device_id_type=MESH,
+        )
+
+    def go(self, number, source, target, to, when=None):
+        copy = self.copy(number, source, target, to)
+        self.started.append((copy, when))
+        if when is None:
+            copy.start()
+        else:
+            pl.when(when)(copy.start)
+
+    def got(self, number, landed, when=None):
+        copy = self.copy(number, landed, landed, (flip(self.place, 1), self.depth))
+        if when is None:
+            copy.wait_recv()
+        else:
+            pl.when(when)(copy.wait_recv)
+
+    def drain(self):
+        for copy, when in self.started:
+            if when is None:
+                copy.wait_send()
+            else:
+                pl.when(when)(copy.wait_send)
+
+    def greet(self):
+        barrier = pltpu.get_barrier_semaphore()
+        others = [(flip(self.place, bit), self.depth) for bit in (1, 2, 4)]
+        others += [(self.place, lax.rem(self.depth + step, PLANES)) for step in range(1, PLANES)]
+        for other in others:
+            pl.semaphore_signal(barrier, inc=1, device_id=other, device_id_type=MESH)
+        pl.semaphore_wait(barrier, len(others))
+
+
+class Spread:
+    def __init__(self, links, own, spot, bits):
+        self.links, self.own, self.spot, self.bits = links, own, spot, bits
+        self.base = links.number(7)
+        place = links.place
+        self.first, self.second = flip(place, bits[0]), flip(place, bits[1])
+        self.both = flip(self.first, bits[1])
+
+    def to(self, bit):
+        return (flip(self.links.place, bit), self.links.depth)
+
+    def one(self):
+        links = self.links
+        links.go(self.base, self.own, self.spot(links.place), self.to(self.bits[0]))
+
+    def two(self):
+        links = self.links
+        to = self.to(self.bits[1])
+        links.go(self.base + 1, self.own, self.spot(links.place), to)
+        links.got(self.base, self.spot(self.first))
+        links.go(self.base + 2, self.spot(self.first), self.spot(self.first), to)
+
+    def three(self):
+        links = self.links
+        to = self.to(1)
+        links.go(self.base + 3, self.own, self.spot(links.place), to)
+        links.go(self.base + 4, self.spot(self.first), self.spot(self.first), to)
+        links.got(self.base + 1, self.spot(self.second))
+        links.go(self.base + 5, self.spot(self.second), self.spot(self.second), to)
+        links.got(self.base + 2, self.spot(self.both))
+        links.go(self.base + 6, self.spot(self.both), self.spot(self.both), to)
+
+    def end(self):
+        links = self.links
+        for index, piece in enumerate((links.place, self.first, self.second, self.both)):
+            links.got(self.base + 3 + index, self.spot(flip(piece, 1)))
+
+
+class Relay:
+    def __init__(self, links, own, put):
+        self.links, self.own, self.put = links, own, put
+        self.base = links.number(2 * (PLANES - 1))
+
+    def send(self, hop):
+        links, depth = self.links, self.links.depth
+        for way in range(2):
+            to = depth + (1 if way else -1)
+            when = (
+                (depth >= hop - 1) & (depth < PLANES - 1)
+                if way
+                else (depth <= PLANES - hop) & (depth > 0)
+            )
+            source = self.own if hop == 1 else self.put(depth, way, hop - 1)
+            links.go(
+                self.base + 2 * (hop - 1) + way,
+                source,
+                self.put(to, way, hop),
+                (links.place, jnp.clip(to, 0, PLANES - 1)),
+                when,
+            )
+
+    def take(self, hop):
+        links, depth = self.links, self.links.depth
+        for way in range(2):
+            when = depth >= hop if way else depth + hop < PLANES
+            links.got(self.base + 2 * (hop - 1) + way, self.put(depth, way, hop), when)
+
+
+def open_kernel(*refs):
+    hidden, attn_piece, out_piece, feed_piece, cos_ref, sin_ref, first_ref, begin_ref = refs[:8]
+    q_out, k_out, v_out, o_out, n_out, weight_out, out_weight_out, feed_all = refs[8:16]
+    gain_ref, square_ref, log_ref, middle_ref, normed_ref, attended_ref = refs[16:22]
+    held, q_ref, k_ref, v_ref, o_ref, n_ref, weight_ref, out_ref, send, recv, local = refs[22:]
+    links = Links(send, recv)
+    place, depth = links.place, links.depth
+    shard = hidden.shape[0]
+    stores = []
+
+    def store(source, target):
+        copy = pltpu.make_async_copy(source, target, local.at[len(stores)])
+        copy.start()
+        stores.append(copy)
+        return copy
+
+    block_at = lambda plane, way, hop: jnp.clip(plane + (-hop if way else hop), 0, PLANES - 1)
+    wide = Relay(links, hidden, lambda plane, way, hop: held.at[block_at(plane, way, hop)])
+    out_rows = lambda block: out_ref.at[
+        pl.ds(pl.multiple_of(block * 256, 256), 256), columns_of(place)
+    ]
+    thin = Relay(links, out_piece, lambda plane, way, hop: out_rows(block_at(plane, way, hop)))
+    feeds = Relay(
+        links,
+        feed_piece,
+        lambda plane, way, hop: feed_all.at[slot_at(plane, way, hop), place],
+    )
+    attn = Spread(links, attn_piece, lambda piece: weight_ref.at[:, columns_of(piece)], (2, 4))
+    outs = Spread(
+        links, out_ref.at[:, columns_of(place)], lambda piece: out_ref.at[:, columns_of(piece)], (2, 4)
+    )
+    slots = [
+        Spread(
+            links,
+            feed_piece if slot == 0 else feed_all.at[slot, place],
+            lambda piece, slot=slot: feed_all.at[slot, piece],
+            (2, 4) if slot % 2 == 0 else (4, 2),
+        )
+        for slot in range(PLANES)
+    ]
+    across = links.number(PLANES)
+
+    links.greet()
+    thin.send(1)
+    wide.send(1)
+    attn.one()
+    own_hidden = store(hidden, held.at[depth])
+    own_attn = store(attn_piece, weight_ref.at[:, columns_of(place)])
+    own_out = store(out_piece, out_rows(depth))
+    own_feed = store(feed_piece, feed_all.at[0, place])
+    square_ref[...] = jnp.zeros_like(square_ref)
+    attn.two()
+    attn.three()
+    slots[0].one()
+    attn.end()
+    for copy in (own_hidden, own_attn, own_out, own_feed):
+        copy.wait()
+    store(weight_ref, weight_out)
+    gain_ref[...] = weight_ref[pl.ds(768, 16), :].astype(jnp.float32)
+
+    def project(block):
+        rows = pl.ds(pl.multiple_of(block * shard, shard), shard)
+        values = held[block].astype(jnp.float32)
+        factor = lax.rsqrt(jnp.mean(values * values, axis=-1, keepdims=True) + 1e-06)
+        normed = (values * factor * gain_ref[0:1, :]).astype(jnp.bfloat16)
+        n_ref[rows, :] = normed
+        cosine, sine_part = cos_ref[rows, :], sin_ref[rows, :]
+        query = tokens_dot(normed, weight_ref[pl.ds(0, 256), :], 1, 1)
+        key = tokens_dot(normed, weight_ref[pl.ds(256, 256), :], 1, 1)
+        value = tokens_dot(normed, weight_ref[pl.ds(512, 256), :], 1, 1)
+        for half in range(2):
+            lanes = slice(half * 128, half * 128 + 128)
+            turned = turn(query[:, lanes], cosine, sine_part, True)
+            q_ref[rows, lanes] = (turned * (HD**-0.5 * LOG2E)).astype(jnp.bfloat16)
+            k_ref[rows, lanes] = turn(key[:, lanes], cosine, sine_part, True).astype(jnp.bfloat16)
+        first = first_ref[rows, :].astype(jnp.float32)
+        blended = 0.5 * value + 0.5 * first
+        v_ref[rows, :] = blended.astype(jnp.bfloat16)
+        square_ref[0:1, :] += jnp.sum(first * first, axis=0, keepdims=True)
+        square_ref[1:2, :] += jnp.sum(blended * blended, axis=0, keepdims=True)
+
+    def project_hop(hop):
+        def one(side, carried):
+            block = depth + hop * (2 * side - 1)
+            pl.when((block >= 0) & (block < PLANES))(lambda: project(block))
+            return carried
+
+        lax.fori_loop(0, 2, one, 0)
+
+    project(depth)
+    wide.take(1)
+    wide.send(2)
+    thin.take(1)
+    thin.send(2)
+    slots[0].two()
+    project_hop(1)
+    wide.take(2)
+    wide.send(3)
+    thin.take(2)
+    thin.send(3)
+    project_hop(2)
+    slots[0].three()
+    wide.take(3)
+    thin.take(3)
+    feeds.send(1)
+    outs.one()
+    project_hop(3)
+    store(n_ref, n_out)
+    store(q_ref, q_out)
+    store(k_ref, k_out)
+    store(v_ref, v_out)
+
+    lane = lax.broadcasted_iota(jnp.int32, (shard, 128), 1)
+    inside = lax.broadcasted_iota(jnp.int32, (shard, shard), 1)
+    down = lax.broadcasted_iota(jnp.int32, (shard, 1), 0)
+
+    def flash_pair(block, pair):
+        rows = pl.ds(pl.multiple_of(block * shard, shard), shard)
+        lanes = columns_of(pair)
+        query = q_ref[rows, lanes]
+        begin = begin_ref[rows, :]
+        parts = [
+            jnp.where((lane < HD) == (head == 0), query, jnp.zeros_like(query)) for head in range(2)
+        ]
+
+        def tile(index, carried, visible):
+            span = pl.ds(pl.multiple_of(index * shard, shard), shard)
+            keys, values = k_ref[span, lanes], v_ref[span, lanes]
+            after = []
+            for head in range(2):
+                top, total, summed = carried[3 * head : 3 * head + 3]
+                scores = jnp.where(visible, tokens_dot(parts[head], keys, 1, 1), -1e30)
+                raised_top = jnp.maximum(top, jnp.max(scores, axis=1, keepdims=True))
+                shrink = jnp.exp2(top - raised_top)
+                shares = jnp.exp2(scores - raised_top)
+                total = total * shrink + jnp.sum(shares, axis=1, keepdims=True)
+                summed = summed * shrink + tokens_dot(shares.astype(jnp.bfloat16), values, 1, 0)
+                after += [raised_top, total, summed]
+            return tuple(after)
+
+        fresh = (
+            jnp.full((shard, 1), -1e30, jnp.float32),
+            jnp.zeros((shard, 1), jnp.float32),
+            jnp.zeros((shard, 128), jnp.float32),
+        )
+        carried = tile(block, fresh + fresh, (inside >= begin - block * shard) & (inside <= down))
+        top0, total0, sum0, top1, total1, sum1 = lax.fori_loop(
+            0, block, lambda j, held: tile(j, held, inside >= begin - j * shard), carried
+        )
+        o_ref[rows, lanes] = jnp.where(lane < HD, sum0 / total0, sum1 / total1).astype(jnp.bfloat16)
+        turned = jnp.transpose(
+            jnp.where(lane < HD, top0 + jnp.log2(total0), top1 + jnp.log2(total1))
+        )
+        log_ref[pair, 0:1, rows] = turned[0:1]
+        log_ref[pair, 1:2, rows] = turned[HD : HD + 1]
+
+    own_columns = attended_ref.at[:, columns_of(depth, 256)]
+
+    def hand(step):
+        block = lax.rem(depth + step, PLANES)
+        rows = pl.ds(pl.multiple_of(block * shard, shard), shard)
+        return links.copy(across + step, o_ref.at[rows, :], own_columns, (place, block))
+
+    def flash(step):
+        block = lax.rem(depth + step, PLANES)
+
+        def one(pair, carried):
+            flash_pair(block, pair)
+            return carried
+
+        lax.fori_loop(0, 2, one, 0)
+
+    flash(3)
+    hand(3).start()
+    feeds.take(1)
+    feeds.send(2)
+    slots[1].one()
+    outs.two()
+    slots[0].end()
+
+    def middle_steps(index, carried):
+        step = 2 - index
+        flash(step)
+        hand(step).start()
+        return carried
+
+    lax.fori_loop(0, 2, middle_steps, 0)
+    feeds.take(2)
+    feeds.send(3)
+    slots[1].two()
+    slots[2].one()
+    outs.three()
+    flash(0)
+    own_rows = pl.ds(pl.multiple_of(depth * shard, shard), shard)
+    attended_ref[:, columns_of(depth, 256)] = o_ref[own_rows, :]
+    store(o_ref, o_out)
+    feeds.take(3)
+    slots[2].two()
+    slots[3].one()
+    slots[1].three()
+    outs.end()
+    store(out_ref, out_weight_out)
+    for step in range(1, PLANES):
+        source = lax.rem(depth - step + PLANES, PLANES)
+        links.got(across + step, attended_ref.at[:, columns_of(source, 256)])
+    half = shard // 2
+    for part in range(2):
+        rows = pl.ds(part * half, half)
+        middle = held[depth, rows, :].astype(jnp.float32) + tokens_dot(
+            attended_ref[rows, :], out_ref[...], 1, 0
+        )
+        middle_ref[rows, :] = middle
+        factor = lax.rsqrt(jnp.mean(middle * middle, axis=-1, keepdims=True) + 1e-06)
+        normed_ref[rows, :] = (middle * factor * gain_ref[1:2, :]).astype(jnp.bfloat16)
+    slots[2].three()
+    slots[1].end()
+    slots[3].two()
+    slots[2].end()
+    slots[3].three()
+    slots[3].end()
+    for step in range(1, PLANES):
+        hand(step).wait_send()
+    links.drain()
+    for copy in stores[4:]:
+        copy.wait()
+
+
+def opening(hidden, attn_piece, out_piece, feed_piece, cosine, sine_part, first_values, begin_column):
+    length, width = first_values.shape
+    rows = hidden.shape[0]
+    count = feed_piece.shape[0]
+    low, full = jnp.bfloat16, jnp.float32
+    any_spec, vmem = pl.BlockSpec(memory_space=pl.ANY), pl.BlockSpec(memory_space=pltpu.VMEM)
+    shape = jax.ShapeDtypeStruct
+    return pl.pallas_call(
+        open_kernel,
+        in_specs=[any_spec] * 4 + [vmem] * 4,
+        out_specs=[any_spec] * 8 + [vmem] * 6,
+        out_shape=[
+            shape((length, width), low),
+            shape((length, width), low),
+            shape((length, width), low),
+            shape((length, width), low),
+            shape((length, D), low),
+            shape((ATTN_ROWS, D), low),
+            shape((D, D), low),
+            shape((PLANES, 8, count, PIECE), low),
+            shape((16, D), full),
+            shape((8, width), full),
+            shape((width // 128, 8, length), full),
+            shape((rows, D), full),
+            shape((rows, D), low),
+            shape((rows, D), low),
+        ],
+        scratch_shapes=[
+            pltpu.VMEM((PLANES, rows, D), low),
+            pltpu.VMEM((length, width), low),
+            pltpu.VMEM((length, width), low),
+            pltpu.VMEM((length, width), low),
+            pltpu.VMEM((length, width), low),
+            pltpu.VMEM((length, D), low),
+            pltpu.VMEM((ATTN_ROWS, D), low),
+            pltpu.VMEM((D, D), low),
+            pltpu.SemaphoreType.DMA((OPEN_COPIES,)),
+            pltpu.SemaphoreType.DMA((OPEN_COPIES,)),
+            pltpu.SemaphoreType.DMA((12,)),
+        ],
+        compiler_params=pltpu.CompilerParams(
+            vmem_limit_bytes=VMEM_LIMIT, collective_id=1, has_side_effects=True
+        ),
+        name="opening",
+    )(hidden, attn_piece, out_piece, feed_piece, cosine, sine_part, first_values, begin_column)
+
+
+def feed_kernel(normed_ref, grad_ref, pieces, feed_ref, back_ref, made_out, weight, made, act, gate, up, sem, out_sem):
+    slot = pl.program_id(0)
+    place = lax.axis_index("dp")
+    now = lax.rem(slot, 2)
+
+    def load(which, buffer):
+        return [
+            pltpu.make_async_copy(
+                pieces.at[which, piece],
+                weight.at[buffer, :, pl.ds(piece * PIECE, PIECE)],
+                sem.at[buffer, piece],
+            )
+            for piece in range(8)
+        ]
+
+    def flush(which, buffer):
+        return [
+            pltpu.make_async_copy(
+                made.at[buffer, :, piece_columns(place, index)],
+                made_out.at[which, index & 1, index >> 1],
+                out_sem.at[buffer, index],
+            )
+            for index in range(8)
+        ]
+
+    @pl.when(slot == 0)
+    def _():
+        for copy in load(slot, now):
+            copy.start()
+        feed_ref[...] = jnp.zeros_like(feed_ref)
+        back_ref[...] = jnp.zeros_like(back_ref)
+
+    @pl.when(slot + 1 < PLANES)
+    def _():
+        for copy in load(slot + 1, 1 - now):
+            copy.start()
+
+    for copy in load(slot, now):
+        copy.wait()
+
+    @pl.when(slot >= 2)
+    def _():
+        for copy in flush(slot - 2, now):
+            copy.wait()
+
+    count = weight.shape[1] // 3
+    rows = normed_ref.shape[0]
+    spans = [pl.ds(index * count, count) for index in range(3)]
+    half = rows // 2
+    for tile in range(2):
+        at = pl.ds(tile * half, half)
+        normed, grad = normed_ref[at, :], grad_ref[at, :]
+        gates = tokens_dot(weight[now, spans[0], :], normed, 1, 1)
+        ups = tokens_dot(weight[now, spans[1], :], normed, 1, 1)
+        backs = tokens_dot(weight[now, spans[2], :], grad, 1, 1)
+        sig = jax.nn.sigmoid(gates)
+        active = gates * sig
+        act[:, at] = (active * ups).astype(jnp.bfloat16)
+        gate[:, at] = (backs * ups * sig * (1.0 + gates * (1.0 - sig))).astype(jnp.bfloat16)
+        up[:, at] = (backs * active).astype(jnp.bfloat16)
+
+    def columns(tile, carried):
+        lanes = columns_of(tile, 256)
+        normed, grad = normed_ref[:, lanes], grad_ref[:, lanes]
+        made[now, spans[0], lanes] = tokens_dot(gate[...], normed, 1, 0).astype(jnp.bfloat16)
+        made[now, spans[1], lanes] = tokens_dot(up[...], normed, 1, 0).astype(jnp.bfloat16)
+        made[now, spans[2], lanes] = tokens_dot(act[...], grad, 1, 0).astype(jnp.bfloat16)
+        feed_ref[:, lanes] += tokens_dot(act[...], weight[now, spans[2], lanes], 0, 0)
+        back_ref[:, lanes] += tokens_dot(gate[...], weight[now, spans[0], lanes], 0, 0) + tokens_dot(
+            up[...], weight[now, spans[1], lanes], 0, 0
+        )
+        return carried
+
+    lax.fori_loop(0, D // 256, columns, 0)
+    for copy in flush(slot, now):
+        copy.start()
+
+    @pl.when(slot == PLANES - 1)
+    def _():
+        for copy in flush(slot - 1, 1 - now) + flush(slot, now):
+            copy.wait()
+
+
+def feed(normed, grad, pieces):
+    rows = normed.shape[0]
+    count = pieces.shape[2]
+    any_spec = pl.BlockSpec(memory_space=pl.ANY)
+    whole = pl.BlockSpec((rows, D), lambda i: (0, 0))
+    total = jax.ShapeDtypeStruct((rows, D), jnp.float32)
+    narrow = pltpu.VMEM((count // 3, rows), jnp.bfloat16)
+    return pl.pallas_call(
+        feed_kernel,
+        grid=(PLANES,),
+        in_specs=[whole, whole, any_spec],
+        out_specs=[whole, whole, any_spec],
+        out_shape=[
+            total,
+            total,
+            jax.ShapeDtypeStruct((PLANES, 2, 4, count, PIECE), jnp.bfloat16),
+        ],
+        scratch_shapes=[
+            pltpu.VMEM((2, count, D), jnp.bfloat16),
+            pltpu.VMEM((2, count, D), jnp.bfloat16),
+            narrow,
+            narrow,
+            narrow,
+            pltpu.SemaphoreType.DMA((2, 8)),
+            pltpu.SemaphoreType.DMA((2, 8)),
+        ],
+        compiler_params=pltpu.CompilerParams(vmem_limit_bytes=VMEM_LIMIT),
+        cost_estimate=cost(24 * rows * D * count, 40 << 20),
+        name="feed",
+    )(normed, grad, pieces)
+
+
+def flash_back_kernel(*refs):
+    low_ref, q_ref, k_ref, v_ref, o_ref = refs[:5]
+    incoming = refs[5:9]
+    log_ref, begin_ref, cos_ref, sin_ref = refs[9:13]
+    dq_ref, dk_ref, dv_ref, first_ref = refs[13:17]
+    grad, inner, total, queries, grads, sem = refs[17:]
+    pair, block = pl.program_id(0), pl.program_id(1)
+    depth = lax.axis_index("mp")
+    length = q_ref.shape[0]
+    rows = length // BLOCKS
+    shard = length // PLANES
+    lane = lax.broadcasted_iota(jnp.int32, (rows, 128), 1)
+
+    @pl.when(block == 0)
+    def _():
+        copies = [
+            pltpu.make_async_copy(
+                piece.at[:, pl.ds(pl.multiple_of(pair * 128, 128), 128)],
+                grad.at[pl.ds(pl.multiple_of(lax.rem(depth - index + PLANES, PLANES) * shard, shard), shard)],
+                sem.at[index],
+            )
+            for index, piece in enumerate(incoming)
+        ]
+        for copy in copies:
+            copy.start()
+        for copy in copies:
+            copy.wait()
+        total[...] = jnp.zeros_like(total)
+        for index in range(BLOCKS):
+            span = pl.ds(index * rows, rows)
+            product = grad[span, :].astype(jnp.float32) * o_ref[span, :].astype(jnp.float32)
+            turned = jnp.transpose(product)
+            for head in range(2):
+                inner[head : head + 1, span] = jnp.sum(
+                    turned[head * HD : head * HD + HD], axis=0, keepdims=True
+                )
+                keep = (lane < HD) == (head == 0)
+                none = jnp.zeros((rows, 128), jnp.bfloat16)
+                queries[head, span, :] = jnp.where(keep, q_ref[span, :], none)
+                grads[head, span, :] = jnp.where(keep, grad[span, :], none)
+
+    start = pl.multiple_of(block * rows, rows)
+    keys, values = k_ref[pl.ds(start, rows), :], v_ref[pl.ds(start, rows), :]
+    keeps = [lane < HD, lane >= HD]
+    own_keys = [jnp.where(keep, keys, jnp.zeros_like(keys)) for keep in keeps]
+    seen = start + lax.broadcasted_iota(jnp.int32, (rows, rows), 0)
+    across = lax.broadcasted_iota(jnp.int32, (1, rows), 1)
+
+    def one(index, carried):
+        key_sum, value_sum = carried
+        at = pl.multiple_of(index * rows, rows)
+        span = pl.ds(at, rows)
+        visible = (seen >= begin_ref[0:1, span]) & (seen <= across + at)
+        query_sum = total[span, :]
+        for head in range(2):
+            query, out_grad = queries[head, span, :], grads[head, span, :]
+            scores = tokens_dot(keys, query, 1, 1)
+            shares = jnp.where(visible, jnp.exp2(scores - log_ref[0, head : head + 1, span]), 0.0)
+            share_grad = tokens_dot(values, out_grad, 1, 1)
+            score_grad = (shares * (share_grad - inner[head : head + 1, span])).astype(jnp.bfloat16)
+            value_sum = value_sum + tokens_dot(shares.astype(jnp.bfloat16), out_grad, 1, 0)
+            key_sum = key_sum + tokens_dot(score_grad, query, 1, 0)
+            query_sum = query_sum + tokens_dot(score_grad, own_keys[head], 0, 0)
+        total[span, :] = query_sum
+        return (key_sum, value_sum)
+
+    last = block + 1
+    for index in range(1, BLOCKS):
+        reaches = (index > block) & (low_ref[index] < start + rows)
+        last = last + jnp.where(reaches, 1, 0)
+    empty = jnp.zeros((rows, 128), jnp.float32)
+    key_sum, value_sum = lax.fori_loop(block, last, one, (empty, empty))
+    span = pl.ds(start, rows)
+    dk_ref[span, :] = turn(key_sum * (1 / LOG2E), cos_ref[span, :], sin_ref[span, :], False).astype(jnp.bfloat16)
+    dv_ref[span, :] = (0.5 * value_sum).astype(jnp.bfloat16)
+    first_ref[span, :] = 0.5 * value_sum
+    query_sum = total[span, :] * HD**-0.5
+    dq_ref[span, :] = turn(query_sum, cos_ref[span, :], sin_ref[span, :], False).astype(jnp.bfloat16)
+
+
+def flash_back(queries, keys, values, attended, incoming, logs, begin_row, cosine, sine_part, lows):
+    length, width = queries.shape
+    pairs = width // 128
+    column = pl.BlockSpec((length, 128), lambda p, j, low: (0, p))
+    table = pl.BlockSpec((length, 128), lambda p, j, low: (0, 0))
+    any_spec = pl.BlockSpec(memory_space=pl.ANY)
+    return pl.pallas_call(
+        flash_back_kernel,
+        grid_spec=pltpu.PrefetchScalarGridSpec(
+            num_scalar_prefetch=1,
+            grid=(pairs, BLOCKS),
+            in_specs=[column] * 4
+            + [any_spec] * 4
+            + [
+                pl.BlockSpec((1, 8, length), lambda p, j, low: (p, 0, 0)),
+                pl.BlockSpec((8, length), lambda p, j, low: (0, 0)),
+                table,
+                table,
+            ],
+            out_specs=[column] * 4,
+            scratch_shapes=[
+                pltpu.VMEM((length, 128), jnp.bfloat16),
+                pltpu.VMEM((8, length), jnp.float32),
+                pltpu.VMEM((length, 128), jnp.float32),
+                pltpu.VMEM((2, length, 128), jnp.bfloat16),
+                pltpu.VMEM((2, length, 128), jnp.bfloat16),
+                pltpu.SemaphoreType.DMA((PLANES,)),
+            ],
+        ),
+        out_shape=[jax.ShapeDtypeStruct((length, width), jnp.bfloat16)] * 3
+        + [jax.ShapeDtypeStruct((length, width), jnp.float32)],
+        compiler_params=pltpu.CompilerParams(vmem_limit_bytes=VMEM_LIMIT),
+        cost_estimate=cost(24 * length * length * width, 12 << 20),
+        name="flash_back",
+    )(lows, queries, keys, values, attended, *incoming, logs, begin_row, cosine, sine_part)
+
+
+def middle_back_kernel(*refs):
+    middle_ref, grad_ref, back_ref, weight_ref, gain_ref = refs[:5]
+    low_ref, dm_ref, gain_grad_ref = refs[5:8]
+    outs = refs[8:12]
+    depth = lax.axis_index("mp")
+    half = middle_ref.shape[0] // 2
+    gain = gain_ref[1:2, :]
+    gain_grad_ref[...] = jnp.zeros_like(gain_grad_ref)
+    for tile in range(2):
+        rows = pl.ds(tile * half, half)
+        middle, incoming = middle_ref[rows, :], back_ref[rows, :]
+        factor = lax.rsqrt(jnp.mean(middle * middle, axis=-1, keepdims=True) + 1e-06)
+        scaled = incoming * gain
+        mean = jnp.mean(scaled * middle, axis=-1, keepdims=True)
+        total = grad_ref[rows, :].astype(jnp.float32) + factor * scaled - middle * (factor**3 * mean)
+        gain_grad_ref[0:1, :] += jnp.sum(incoming * middle * factor, axis=0, keepdims=True)
+        dm_ref[rows, :] = total
+        low_ref[rows, :] = total.astype(jnp.bfloat16)
+    for index, out in enumerate(outs):
+        owner = lax.rem(depth + index, PLANES)
+        rows = pl.ds(pl.multiple_of(owner * 256, 256), 256)
+        out[...] = tokens_dot(low_ref[...], weight_ref[rows, :], 1, 1).astype(jnp.bfloat16)
+
+
+def middle_back(middle, grad, back, weight, gains):
+    rows = middle.shape[0]
+    return pl.pallas_call(
+        middle_back_kernel,
+        out_shape=[
+            jax.ShapeDtypeStruct((rows, D), jnp.bfloat16),
+            jax.ShapeDtypeStruct((rows, D), jnp.float32),
+            jax.ShapeDtypeStruct((8, D), jnp.float32),
+        ]
+        + [jax.ShapeDtypeStruct((rows, 256), jnp.bfloat16)] * PLANES,
+        compiler_params=pltpu.CompilerParams(vmem_limit_bytes=VMEM_LIMIT),
+        cost_estimate=cost(2 * rows * D * D, 12 << 20),
+        name="middle_back",
+    )(middle, grad, back, weight, gains)
+
+
+def grad_kernel(*refs):
+    wide, other_ref, out_ref, acc, sem = refs[:-4], refs[-4], refs[-3], refs[-2], refs[-1]
+    place = lax.axis_index("dp")
+    step = pl.program_id(0)
+    row = 0
+    for one in wide:
+        count = one.shape[1]
+        acc[pl.ds(row, count), :] = tokens_dot(one[...], other_ref[...], 0, 0).astype(jnp.bfloat16)
+        row += count
+    copies = []
+    for part in range(2):
+        at = jnp.bitwise_xor(place, 2 * step + part)
+        to = out_ref.at[lax.rem(at, 2), lax.div(at, 2)]
+        copies.append(pltpu.make_async_copy(acc.at[:, pl.ds(part * PIECE, PIECE)], to, sem.at[part]))
+    for copy in copies:
+        copy.start()
+    for copy in copies:
+        copy.wait()
+
+
+def weight_grad(wide, other, name):
+    rows = other.shape[0]
+    count = sum(one.shape[1] for one in wide)
+    return pl.pallas_call(
+        grad_kernel,
+        grid=(D // 256,),
+        in_specs=[pl.BlockSpec(one.shape, lambda i: (0, 0)) for one in wide]
+        + [pl.BlockSpec((rows, 256), lambda i: (0, i))],
+        out_specs=pl.BlockSpec(memory_space=pl.ANY),
+        out_shape=jax.ShapeDtypeStruct((2, 4, count, PIECE), jnp.bfloat16),
+        scratch_shapes=[pltpu.VMEM((count, 256), jnp.bfloat16), pltpu.SemaphoreType.DMA((2,))],
+        compiler_params=pltpu.CompilerParams(vmem_limit_bytes=VMEM_LIMIT),
+        cost_estimate=cost(2 * rows * D * count, 8 << 20),
+        name=name,
+    )(*wide, other)
+
+
+def input_back_kernel(dq_ref, dk_ref, dv_ref, weight_ref, n_ref, gain_ref, out_ref, gain_grad_ref):
+    @pl.when(pl.program_id(0) == 0)
+    def _():
+        gain_grad_ref[...] = jnp.zeros_like(gain_grad_ref)
+
+    incoming = (
+        tokens_dot(dq_ref[...], weight_ref[pl.ds(0, 256), :], 1, 0)
+        + tokens_dot(dk_ref[...], weight_ref[pl.ds(256, 256), :], 1, 0)
+        + tokens_dot(dv_ref[...], weight_ref[pl.ds(512, 256), :], 1, 0)
+    )
+    out_ref[0] = incoming.astype(jnp.bfloat16)
+    gain_grad_ref[0:1, :] += (
+        jnp.sum(incoming * n_ref[...].astype(jnp.float32), axis=0, keepdims=True) / gain_ref[0:1, :]
+    )
+
+
+def input_back(grads, weight, normed, gains):
+    length = normed.shape[0]
+    rows = length // PLANES
+    tile = pl.BlockSpec((rows, 256), lambda i: (i, 0))
+    whole = lambda *shape: pl.BlockSpec(shape, lambda i: (0,) * len(shape))
+    return pl.pallas_call(
+        input_back_kernel,
+        grid=(PLANES,),
+        in_specs=[tile] * 3
+        + [whole(ATTN_ROWS, D), pl.BlockSpec((rows, D), lambda i: (i, 0)), whole(16, D)],
+        out_specs=[pl.BlockSpec((1, rows, D), lambda i: (i, 0, 0)), whole(8, D)],
+        out_shape=[
+            jax.ShapeDtypeStruct((PLANES, rows, D), jnp.bfloat16),
+            jax.ShapeDtypeStruct((8, D), jnp.float32),
+        ],
+        compiler_params=pltpu.CompilerParams(vmem_limit_bytes=VMEM_LIMIT),
+        cost_estimate=cost(2 * length * D * 768, 12 << 20),
+        name="input_back",
+    )(*grads, weight, normed, gains)
+
+
+def permute(values, pairs):
+    return lax.ppermute(values, ("dp", "mp"), pairs)
+
+
+def swap(values, bit):
+    return permute(
+        values,
+        [
+            (place * PLANES + depth, (place ^ bit) * PLANES + depth)
+            for place in range(8)
+            for depth in range(PLANES)
+        ],
+    )
+
+
+def along(values, moves):
+    return permute(
+        values,
+        [(place * PLANES + a, place * PLANES + b) for place in range(8) for a, b in moves],
+    )
+
+
+def added(a, b):
+    return (a.astype(jnp.float32) + b.astype(jnp.float32)).astype(jnp.bfloat16)
+
+
+def fold(keep, send, bits):
+    got = swap(send, 1)
+    mine, theirs = added(keep[:2], got[:2]), added(keep[2:], got[2:])
+    got = swap(theirs, bits[0])
+    mine, theirs = added(mine[0], got[0]), added(mine[1], got[1])
+    return added(mine, swap(theirs, bits[1]))
+
+
+def fold_line(block, depth):
+    right = left = None
+    for step in range(1, PLANES):
+        there = block(jnp.minimum(depth + PLANES - step, PLANES - 1))
+        right = along(
+            there if right is None else added(there, right), [(a, a + 1) for a in range(step)]
+        )
+        there = block(jnp.maximum(depth - PLANES + step, 0))
+        left = along(
+            there if left is None else added(there, left),
+            [(a, a - 1) for a in range(PLANES - step, PLANES)],
+        )
+    return (
+        block(depth).astype(jnp.float32) + right.astype(jnp.float32) + left.astype(jnp.float32)
+    )
+
+
+def exchange(parts):
+    return [parts[0]] + [
+        along(parts[step], [(a, (a + step) % PLANES) for a in range(PLANES)])
+        for step in range(1, PLANES)
+    ]
+
+
+def fast_shards(
+    hidden_in,
+    segment_ids,
+    first_values,
+    grad_out,
+    input_proj,
+    output_proj,
+    expand_proj,
+    reduce_proj,
+    norm_gains,
+    old_moment_input,
+    old_moment_output,
+    old_moment_expand,
+    old_moment_reduce,
+    old_moment_gains,
+    old_square_input,
+    old_square_output,
+    old_square_expand,
+    old_square_reduce,
+    old_square_gains,
+):
+    place, depth = lax.axis_index("dp"), lax.axis_index("mp")
+    low = jnp.bfloat16
+    hidden, out_cotangent = hidden_in[0], grad_out[0]
+    seg_row = segment_ids[0]
+    length = seg_row.shape[0]
+    shard = hidden.shape[0]
+    ffs = reduce_proj.shape[0]
+
+    attn_piece = jnp.concatenate(
+        [
+            input_proj.astype(low).transpose(0, 2, 1).reshape(768, PIECE),
+            norm_gains.astype(low),
+            jnp.zeros((14, PIECE), low),
+        ]
+    )
+    feed_piece = jnp.concatenate(
+        [
+            expand_proj.astype(low).transpose(0, 2, 1).reshape(2 * ffs, PIECE),
+            reduce_proj.astype(low),
+        ]
+    )
+
+    begins = jnp.zeros_like(seg_row)
+    for number in range(1, 7):
+        start = jnp.sum((seg_row < number).astype(jnp.int32))
+        begins = jnp.where(seg_row == number, start, begins)
+    lows = begins[:: length // BLOCKS]
+    offset = (jnp.arange(length, dtype=jnp.int32) - begins).astype(jnp.float32)
+    inverse_rates = 10000.0 ** (-2.0 * jnp.arange(HD // 2, dtype=jnp.float32) / HD)
+    angles = offset[:, None] * inverse_rates[None, :]
+    cosine, sine = jnp.cos(angles), jnp.sin(angles)
+    cosine = jnp.concatenate([cosine] * 4, axis=1)
+    sine_part = jnp.concatenate([-sine, sine, -sine, sine], axis=1)
+
+    (
+        queries,
+        keys,
+        values,
+        attended,
+        normed,
+        attn_weight,
+        out_weight,
+        feed_all,
+        gains,
+        squares,
+        logs,
+        middle,
+        normed_two,
+        attended_own,
+    ) = opening(
+        hidden,
+        attn_piece,
+        output_proj.astype(low),
+        feed_piece,
+        cosine,
+        sine_part,
+        first_values[0],
+        begins[:, None],
+    )
+    feed_out, normed_two_grad, feed_parts = feed(normed_two, out_cotangent, feed_all)
+    made = [fold(feed_parts[slot, 0], feed_parts[slot, 1], (4, 2)) for slot in range(PLANES)]
+    layer_output = (middle + feed_out).astype(low)[None]
+    branch_low, middle_grad, gain_two, *out_grads = middle_back(
+        middle, out_cotangent, normed_two_grad, out_weight, gains
+    )
+    incoming = exchange(out_grads)
+    out_made = weight_grad([attended_own], branch_low, "output_grad")
+    out_made = fold(out_made[0], out_made[1], (4, 2))
+    feed_made = jnp.stack(made)
+
+    dq, dk, dv, values_grad = flash_back(
+        queries,
+        keys,
+        values,
+        attended,
+        incoming,
+        logs,
+        jnp.broadcast_to(begins[None], (8, length)),
+        cosine,
+        sine_part,
+        lows,
+    )
+    slot_table = jnp.array(
+        [[[s[2] for s in SLOTS[plane]].index(j) for j in range(PLANES)] for plane in range(PLANES)],
+        jnp.int32,
+    )[depth]
+    weight_total = fold_line(
+        lambda j: jnp.concatenate(
+            [
+                lax.dynamic_index_in_dim(feed_made, slot_table[j], 0, False),
+                lax.dynamic_slice_in_dim(out_made, j * 256, 256, 0),
+            ]
+        ),
+        depth,
+    )
+    input_partial, gain_one = input_back((dq, dk, dv), attn_weight, normed, gains)
+    attn_made = weight_grad([dq, dk, dv], normed, "input_grad")
+    normed_grad = fold_line(lambda j: lax.dynamic_index_in_dim(input_partial, j, 0, False), depth)
+    attn_total = fold(attn_made[0], attn_made[1], (4, 2)).astype(jnp.float32)
+
+    small = jnp.concatenate(
+        [
+            gain_one[0].reshape(8, PIECE),
+            gain_two[0].reshape(8, PIECE),
+            jnp.broadcast_to(jnp.sum(squares[:2], axis=1)[:, None], (2, PIECE)),
+            jnp.zeros((6, PIECE), jnp.float32),
+        ]
+    )
+    for bit in (1, 2, 4):
+        small = small + swap(small, bit)
+    for bit in (1, 2):
+        small = small + along(small, [(a, a ^ bit) for a in range(PLANES)])
+    value_norms = jnp.sqrt(small[16:18, 0] / (8 * length * D))
+    gain_total = lax.dynamic_index_in_dim(small[:16].reshape(2, 8, PIECE), place, 1, False)
+
+    hidden32 = hidden.astype(jnp.float32)
+    factor_one = rms_factor(hidden32)
+    input_part, _ = norm_back(hidden32, factor_one, gains[0], normed_grad)
+    input_grad = (middle_grad + input_part)[None]
+
+    expand_total = weight_total[: 2 * ffs].reshape(2, ffs, PIECE).transpose(0, 2, 1)
+    reduce_total = weight_total[2 * ffs : 3 * ffs]
+    out_total = weight_total[3 * ffs :]
+    attn_total = attn_total.reshape(3, 256, PIECE).transpose(0, 2, 1)
+    new_input = adamw(input_proj, attn_total, old_moment_input, old_square_input, D ** (-0.5), 0.1)
+    new_output = adamw(
+        output_proj,
+        out_total,
+        old_moment_output,
+        old_square_output,
+        max(1, 8 * HEADS * HD // LEN) ** (-0.5),
+        0.1,
+    )
+    new_expand = adamw(
+        expand_proj, expand_total, old_moment_expand, old_square_expand, D ** (-0.5), 0.1
+    )
+    new_reduce = adamw(
+        reduce_proj, reduce_total, old_moment_reduce, old_square_reduce, (FF // 3) ** (-0.5), 0.1
+    )
+    new_gains = adamw(norm_gains, gain_total, old_moment_gains, old_square_gains, 0.2, 0.0)
+    return (
+        layer_output,
+        input_grad,
+        values_grad[None],
+        value_norms,
+        new_input[0],
+        new_output[0],
+        new_expand[0],
+        new_reduce[0],
+        new_gains[0],
+        new_input[1],
+        new_output[1],
+        new_expand[1],
+        new_reduce[1],
+        new_gains[1],
+        new_input[2],
+        new_output[2],
+        new_expand[2],
+        new_reduce[2],
+        new_gains[2],
+    )
+
+
 def solution(mesh):
+    quick = mesh.shape["dp"] == 8 and mesh.shape["mp"] == PLANES
     return jax.shard_map(
-        shards,
+        fast_shards if quick else shards,
         mesh=mesh,
         in_specs=(
             P("dp", "mp", None),

time: 1270 us -> 630 us (0.50)
  waiting for transfers between devices: 698 us -> 161 us
  Pallas kernels: 0 us -> 315 us
  matrix products: 253 us -> 0 us
  local copies, waits for them, and re-layouts: 103 us -> 20.2 us
  blocking collectives: 65.1 us -> 0 us
  other arithmetic: 120 us -> 55.9 us
  starting transfers between devices: 0.96 us -> 55.3 us
    reduce_scatter x5 -> x0, waiting for transfers between devices: 359 us -> none  [the longest x1 141 us: shards(): lax.psum_scatter(jnp.dot(rows_part, out_weight, preferred_element_type=jn...]
    all_gather x7 -> x0, waiting for transfers between devices: 338 us -> none  [the longest x1 82.8 us: shards(): all_normed_two = lax.all_gather(normed_two, 'mp', axis=0, tiled=True)]
    pallas_call x0 -> x7, Pallas kernels: none -> 315 us  [the longest x1 198 us: opening(): pl.pallas_call(open_kernel, in_specs=[any_spec] * 4 + [vmem] * 4, out_spe...]
    dot_general x40 -> x0, matrix products: 253 us -> none  [the longest x4 46.1 us: one_block(): jnp.einsum('qhd,khd->hqk', grad_block, mixed_values, preferred_element_ty...]
    ppermute x0 -> x38, waiting for transfers between devices: none -> 161 us  [permute(): return lax.ppermute(values, ('dp', 'mp'), pairs)]
    ppermute x0 -> x38, starting transfers between devices: none -> 55.3 us  [permute(): return lax.ppermute(values, ('dp', 'mp'), pairs)]
    dynamic_update_slice x8 -> x0, local copies, waits for them, and re-layouts: 46.6 us -> none  [attend(): lax.map(one_block, jnp.arange(length // block_rows, dtype=jnp.int32))]
    psum x1 -> x0, blocking collectives: 42 us -> none  [shards(): lax.psum((jnp.stack([gain_one_grad, gain_two_grad]), square_terms), ('dp'...]
  transfers between devices with their start and end apart: 15 -> 38, of which waited for: 11 -> 15; matrix products, arithmetic and copies ran while one was open for 29% -> 8% of each run, Pallas kernels for 0% -> 3%
where the time goes in v1:
time: 630 us; the launch traced here: 622 us
  Pallas kernels  315 us (50%)
  waiting for transfers between devices  161 us (26%)
  other arithmetic  55.9 us (9%)
  starting transfers between devices  55.3 us (9%)
  local copies, waits for them, and re-layouts  20.2 us (3%)
  between operations  15.4 us (2%)
    pallas_call x1, Pallas kernels, opening(): pl.pallas_call(open_kernel, in_specs=[any_spec] * 4 + [vmem] * 4, out_spe...  198 us
    ppermute x38, waiting for transfers between devices, permute(): return lax.ppermute(values, ('dp', 'mp'), pairs)  161 us
    ppermute x38, starting transfers between devices, permute(): return lax.ppermute(values, ('dp', 'mp'), pairs)  55.3 us
    pallas_call x1, Pallas kernels, flash_back(): pl.pallas_call(flash_back_kernel, grid_spec=pltpu.PrefetchScalarGridSpec(...  45.9 us
    pallas_call x1, Pallas kernels, feed(): pl.pallas_call(feed_kernel, grid=(PLANES,), in_specs=[whole, whole, any_s...  40.4 us
    convert_element_type x18, other arithmetic, added(): return (a.astype(jnp.float32) + b.astype(jnp.float32)).astype(jnp.bfloat16)  19 us
    pallas_call x2, Pallas kernels, weight_grad(): pl.pallas_call(grad_kernel, grid=(D // 256,), in_specs=[pl.BlockSpec(one....  16.3 us
  transfers between devices with their start and end apart: 38, of which 15 were waited for; matrix products, arithmetic and copies ran while one was open for 8% of the time, Pallas kernels for 3%

profile of v1, /device:TPU:0, one launch (start us, length us, event | category | flops | bytes accessed | tf_op | source)
XLA Modules:
  0.0 622.5 jit_solution(5717526085745347427)
XLA Ops:
  0.7 1.5 fusion.55
  2.2 4.6 compare_select_fusion.5
  6.8 4.6 fusion.68
  14.4 3.7 fusion.46
  19.0 3.0 pad_maximum_fusion.1
  22.9 197.5 %opening.1 = (bf16[2048,256]{1,0:T(8,128)(2,1)}, bf16[2048,256]{1,0:T(8,128)(2,1)}, bf16[2048,256]{1,0:T(8,128)(2,1)}, bf16[2048,256]{1,0:T(8,128)(2,1)}, bf16[2...) custom-call(bf16[512,1024]{1,0:T(8,128)(2,1)} %bitcast.191, ...), custom_call_target="tpu_custom_call" | custom-call | tf_op jit(solution)/shard_map/opening/pallas_call | solution.py:777
  220.4 40.4 %feed.1 = (f32[512,1024]{1,0:T(8,128)}, f32[512,1024]{1,0:T(8,128)}, bf16[4,2,4,2112,128]{4,3,2,1,0:T(8,128)(2,1)}) custom-call(bf16[512,1024]{1,0:T(8,128)(2,1)} %get-tuple-element.50.normed_ref, bf16[512,1024]{1,0:T(8,128)(2,1)} %bitcast.195, bf16[4,8,2112,128]{3,2,1,0:T(8,128)(2,1)} %get-tuple-element.51.pieces), custom_call_target="tpu_custom_call" | custom-call | flops 26575110144 | bytes 41943040 | tf_op jit(solution)/shard_map/feed/pallas_call | solution.py:907
  260.9 6.5 %middle_back.1 = (bf16[512,1024]{1,0:T(8,128)(2,1)}, f32[512,1024]{1,0:T(8,128)}, f32[8,1024]{1,0:T(8,128)}, bf16[512,256]{1,0:T(8,128)(2,1)}, bf16[512,256]{1,0...) custom-call(f32[512,1024]{1,0:T(8,128)} %get-tuple-element.49.refs_0_, bf16[512,1024]{1,0:T(8,128)(2,1)} %bitcast.196, ...), custom_call_target="tpu_custom_call" | custom-call | flops 1073741824 | bytes 12582912 | tf_op jit(solution)/shard_map/middle_back/pallas_call | solution.py:1075
  267.4 3.8 collective-permute-start.2
  273.5 6.8 %output_grad.1 = bf16[2,4,1024,128]{3,2,1,0:T(8,128)(2,1)} custom-call(bf16[512,1024]{1,0:T(8,128)(2,1)} %get-tuple-element.77.refs_0_, bf16[512,1024]{1,0:T(8,128)(2,1)} %get-tuple-element.78.refs_1_), custom_call_target="tpu_custom_call" | custom-call | flops 1073741824 | bytes 8388608 | tf_op jit(solution)/shard_map/output_grad/pallas_call | solution.py:1112
  280.3 8.5 %collective-permute-done.1.refs_7_ = bf16[512,256]{1,0:T(8,128)(2,1)S(1)} collective-permute-done((bf16[512,256]{1,0:T(8,128)(2,1)}, bf16[512,256]{1,0:T(8,128)(2,1)S(1)}, u32[]{:S(2)}, u32[]{:S(2)}) %collective-permute-start.1) | collective-permute-done | bytes 262176 | tf_op jit(solution)/shard_map/ppermute | solution.py:1164
  289.7 45.9 %flash_back.1 = (bf16[2048,256]{1,0:T(8,128)(2,1)}, bf16[2048,256]{1,0:T(8,128)(2,1)}, bf16[2048,256]{1,0:T(8,128)(2,1)}, f32[2048,256]{1,0:T(8,128)}) custom-call(s32[4]{0:T(128)} %slice.222.refs_0_, bf16[2048,256]{1,0:T(8,128)(2,1)} %get-tuple-element.57.refs_1_, bf16[2048,256]{1,0:T(8,128)(2,1)} %get-tuple-element.58.refs_2_, ...), custom_call_target="tpu_custom_call" | custom-call | flops 25769803776 | bytes 12582912 | tf_op jit(solution)/shard_map/flash_back/pallas_call | solution.py:1018
  335.5 8.3 %input_back.1 = (bf16[4,512,1024]{2,1,0:T(8,128)(2,1)}, f32[8,1024]{1,0:T(8,128)}) custom-call(bf16[2048,256]{1,0:T(8,128)(2,1)} %get-tuple-element.66.dq_ref.refs_0_, bf16[2048,256]{1,0:T(8,128)(2,1)} %get-tuple-element.67.dk_ref.refs_1_, bf16[2048,256]{1,0:T(8,128)(2,1)} %get-tuple-element.68.dv_ref.refs_2_, ...), custom_call_target="tpu_custom_call" | custom-call | flops 3221225472 | bytes 12582912 | tf_op jit(solution)/shard_map/input_back/pallas_call | solution.py:1147
  347.8 9.5 %input_grad.1 = bf16[2,4,768,128]{3,2,1,0:T(8,128)(2,1)} custom-call(bf16[2048,256]{1,0:T(8,128)(2,1)} %get-tuple-element.66.dq_ref.refs_0_, bf16[2048,256]{1,0:T(8,128)(2,1)} %get-tuple-element.67.dk_ref.refs_1_, bf16[2048,256]{1,0:T(8,128)(2,1)} %get-tuple-element.68.dv_ref.refs_2_, bf16[2048,1024]{1,0:T(8,128)(2,1)} %get-tuple-element.70.n_ref.refs_3_), custom_call_target="tpu_custom_call" | custom-call | flops 3221225472 | bytes 8388608 | tf_op jit(solution)/shard_map/input_grad/pallas_call | solution.py:1112
  357.9 2.0 slice_bitcast_fusion.5
  361.1 5.7 collective-permute-start.12
  366.8 1.5 dynamic-slice_bitcast_fusion.1
  368.3 2.9 collective-permute-start.3
  371.2 6.3 %slice_bitcast_fusion.3 = (bf16[4,2112,128]{2,1,0:T(8,128)(2,1)}, bf16[4,2112,128]{2,1,0:T(8,128)(2,1)}, bf16[4,2112,128]{2,1,0:T(8,128)(2,1)}, bf16[4,2112,128]{2,1,0:T(8,128)(2,1)}) fusion(bf16[4,2,4,2112,128]{4,3,2,1,0:T(8,128)(2,1)} %get-tuple-element.76), kind=kLoop, calls=%fused_computation.23 | loop fusion | bytes 17301504 | tf_op jit(solution)/shard_map/squeeze | solution.py:1302
  393.6 3.0 fusion.24
  400.2 9.1 %collective-permute-done.15 = bf16[2,768,128]{2,1,0:T(8,128)(2,1)S(1)} collective-permute-done((bf16[2,768,128]{2,1,0:T(8,128)(2,1)S(1)}, bf16[2,768,128]{2,1,0:T(8,128)(2,1)S(1)}, u32[]{:S(2)}, u32[]{:S(2)}) %collective-permute-start.15) | collective-permute-done | bytes 393248 | tf_op jit(solution)/shard_map/ppermute | solution.py:1164
  411.4 2.9 fusion.16
  414.4 8.1 %collective-permute-done.30 = bf16[2,1024,128]{2,1,0:T(8,128)(2,1)S(1)} collective-permute-done((bf16[2,1024,128]{2,1,0:T(8,128)(2,1)S(1)}, bf16[2,1024,128]{2,1,0:T(8,128)(2,1)S(1)}, u32[]{:S(2)}, u32[]{:S(2)}) %collective-permute-start.30) | collective-permute-done | bytes 524320 | tf_op jit(solution)/shard_map/ppermute | solution.py:1164
  422.5 1.6 collective-permute-start.6
  424.9 2.5 collective-permute-start.4
  428.0 1.5 collective-permute-start.31
  429.5 7.0 %fusion.7 = (bf16[2,2112,128]{2,1,0:T(8,128)(2,1)}, bf16[2,2112,128]{2,1,0:T(8,128)(2,1)}, bf16[2,2112,128]{2,1,0:T(8,128)(2,1)}, bf16[2,2112,128]{2,1,0:T(8,128...) fusion(bf16[4,2112,128]{2,1,0:T(8,128)(2,1)} %collective-permut, ...), kind=kLoop, calls=%fused_computation.19 | loop fusion | flops 17301504 | bytes 25952256 | tf_op jit(solution)/shard_map/convert_element_type | solution.py:1186
  436.5 1.5 collective-permute-start.18
  439.0 2.7 multiply_subtract_fusion.1
  445.7 2.1 collective-permute-done.4
  447.9 2.5 fusion.17
  451.1 12.6 %collective-permute-done.18 = bf16[2,2112,128]{2,1,0:T(8,128)(2,1)} collective-permute-done((bf16[2,2112,128]{2,1,0:T(8,128)(2,1)}, bf16[2,2112,128]{2,1,0:T(8,128)(2,1)}, u32[]{:S(2)}, u32[]{:S(2)}) %collective-permute-start.18) | collective-permute-done | bytes 1081376 | tf_op jit(solution)/shard_map/ppermute | solution.py:1164
  463.7 5.2 collective-permute-start.5
  470.1 16.7 %collective-permute-done.21 = bf16[2,2112,128]{2,1,0:T(8,128)(2,1)S(1)} collective-permute-done((bf16[2,2112,128]{2,1,0:T(8,128)(2,1)}, bf16[2,2112,128]{2,1,0:T(8,128)(2,1)S(1)}, u32[]{:S(2)}, u32[]{:S(2)}) %collective-permute-start.21) | collective-permute-done | bytes 1081376 | tf_op jit(solution)/shard_map/ppermute | solution.py:1164
  487.4 22.5 %collective-permute-done.24 = bf16[2,2112,128]{2,1,0:T(8,128)(2,1)S(1)} collective-permute-done((bf16[2,2112,128]{2,1,0:T(8,128)(2,1)}, bf16[2,2112,128]{2,1,0:T(8,128)(2,1)S(1)}, u32[]{:S(2)}, u32[]{:S(2)}) %collective-permute-start.24) | collective-permute-done | bytes 1081376 | tf_op jit(solution)/shard_map/ppermute | solution.py:1164
  510.6 19.4 %collective-permute-done.27 = bf16[2,2112,128]{2,1,0:T(8,128)(2,1)S(1)} collective-permute-done((bf16[2,2112,128]{2,1,0:T(8,128)(2,1)}, bf16[2,2112,128]{2,1,0:T(8,128)(2,1)S(1)}, u32[]{:S(2)}, u32[]{:S(2)}) %collective-permute-start.27) | collective-permute-done | bytes 1081376 | tf_op jit(solution)/shard_map/ppermute | solution.py:1164
  530.6 1.6 collective-permute-start.28
  533.7 11.5 %collective-permute-done.25 = bf16[2112,128]{1,0:T(8,128)(2,1)S(1)} collective-permute-done((bf16[2112,128]{1,0:T(8,128)(2,1)S(1)}, bf16[2112,128]{1,0:T(8,128)(2,1)S(1)}, u32[]{:S(2)}, u32[]{:S(2)}) %collective-permute-start.25) | collective-permute-done | bytes 540704 | tf_op jit(solution)/shard_map/ppermute | solution.py:1164
  545.4 7.3 %collective-permute-done.28 = bf16[2112,128]{1,0:T(8,128)(2,1)S(1)} collective-permute-done((bf16[2112,128]{1,0:T(8,128)(2,1)S(1)}, bf16[2112,128]{1,0:T(8,128)(2,1)S(1)}, u32[]{:S(2)}, u32[]{:S(2)}) %collective-permute-start.28) | collective-permute-done | bytes 540704 | tf_op jit(solution)/shard_map/ppermute | solution.py:1164
  553.5 5.2 collective-permute-start.32
  561.2 6.6 %collective-permute-done.32 = bf16[2368,128]{1,0:T(8,128)(2,1)S(1)} collective-permute-done((bf16[2368,128]{1,0:T(8,128)(2,1)S(1)}, bf16[2368,128]{1,0:T(8,128)(2,1)S(1)}, u32[]{:S(2)}, u32[]{:S(2)}) %collective-permute-start.32) | collective-permute-done | bytes 606240 | tf_op jit(solution)/shard_map/ppermute | solution.py:1164
  568.0 4.6 collective-permute-start.33
  573.5 8.4 %collective-permute-done.8 = bf16[512,1024]{1,0:T(8,128)(2,1)S(1)} collective-permute-done((bf16[512,1024]{1,0:T(8,128)(2,1)S(1)}, bf16[512,1024]{1,0:T(8,128)(2,1)S(1)}, u32[]{:S(2)}, u32[]{:S(2)}) %collective-permute-start.8) | collective-permute-done | bytes 1048608 | tf_op jit(solution)/shard_map/ppermute | solution.py:1164
  582.9 3.5 collective-permute-start.34
  587.9 2.2 fusion.12
  590.1 3.9 collective-permute-done.34
  593.9 22.9 %collective-permute-done.37 = bf16[2368,128]{1,0:T(8,128)(2,1)S(1)} collective-permute-done((bf16[2368,128]{1,0:T(8,128)(2,1)S(1)}, bf16[2368,128]{1,0:T(8,128)(2,1)S(1)}, u32[]{:S(2)}, u32[]{:S(2)}) %collective-permute-start.37) | collective-permute-done | bytes 606240 | tf_op jit(solution)/shard_map/ppermute | solution.py:1164
  620.3 1.7 multiply_subtract_fusion
  (178 shorter events, 43.7 us)
Async XLA Ops:
  0.7 12.2 %copy-start.7 = (f32[2,128,704]{1,2,0:T(8,128)S(1)}, f32[2,128,704]{1,2,0:T(8,128)}, u32[]{:S(2)}) copy-start(f32[2,128,704]{1,2,0:T(8,128)} %param.26) | copy-start | bytes 2162692
  0.7 12.2 %copy-start.13 = (f32[704,128]{1,0:T(8,128)S(1)}, f32[704,128]{1,0:T(8,128)}, u32[]{:S(2)}) copy-start(f32[704,128]{1,0:T(8,128)} %param.27) | copy-start | bytes 1081348
  267.4 13.0 %collective-permute-start = (bf16[512,256]{1,0:T(8,128)(2,1)}, bf16[512,256]{1,0:T(8,128)(2,1)S(1)}, u32[]{:S(2)}, u32[]{:S(2)}) collective-permute-start(bf16[512,256]{1,0:T(8,128)(2,1)} %get-tuple-element.62), channel_id=1, source_target_pairs={{0,1},{1,2},{2,3},{3,0},{4,5},{5,6},{6,7},{7,4},{8,9},{9,10},{10,1... | collective-permute-start | bytes 786440 | tf_op jit(solution)/shard_map/ppermute | solution.py:1164
  267.4 21.5 %collective-permute-start.1 = (bf16[512,256]{1,0:T(8,128)(2,1)}, bf16[512,256]{1,0:T(8,128)(2,1)S(1)}, u32[]{:S(2)}, u32[]{:S(2)}) collective-permute-start(bf16[512,256]{1,0:T(8,128)(2,1)} %get-tuple-element.63), channel_id=1, source_target_pairs={{0,2},{1,3},{2,0},{3,1},{4,6},{5,7},{6,4},{7,5},{8,10},{9,11},{10,... | collective-permute-start | bytes 786440 | tf_op jit(solution)/shard_map/ppermute | solution.py:1164
  267.4 21.5 %collective-permute-start.2 = (bf16[512,256]{1,0:T(8,128)(2,1)}, bf16[512,256]{1,0:T(8,128)(2,1)S(1)}, u32[]{:S(2)}, u32[]{:S(2)}) collective-permute-start(bf16[512,256]{1,0:T(8,128)(2,1)} %get-tuple-element.64), channel_id=1, source_target_pairs={{0,3},{1,0},{2,1},{3,2},{4,7},{5,4},{6,5},{7,6},{8,11},{9,8},{10,9... | collective-permute-start | bytes 786440 | tf_op jit(solution)/shard_map/ppermute | solution.py:1164
  280.3 9.2 %copy-start.28 = (bf16[512,256]{1,0:T(8,128)(2,1)}, bf16[512,256]{1,0:T(8,128)(2,1)S(1)}, u32[]{:S(2)}) copy-start(bf16[512,256]{1,0:T(8,128)(2,1)S(1)} %collective-permute-done.refs_6_) | copy-start | bytes 786436
  335.5 9.1 %copy-start.4 = (bf16[2,4,1024,128]{3,2,1,0:T(8,128)(2,1)S(1)}, bf16[2,4,1024,128]{3,2,1,0:T(8,128)(2,1)}, u32[]{:S(2)}) copy-start(bf16[2,4,1024,128]{3,2,1,0:T(8,128)(2,1)} %output_grad.1) | copy-start | bytes 6291460
  344.6 1.6 collective-permute-start.9
  345.7 47.4 %collective-permute-start.29 = (bf16[4,1024,128]{2,1,0:T(8,128)(2,1)}, bf16[4,1024,128]{2,1,0:T(8,128)(2,1)S(1)}, u32[]{:S(2)}, u32[]{:S(2)}) collective-permute-start(bf16[4,1024,128]{2,1,0:T(8,128)(2,1)} %slice_bitcast_fusion.4), channel_id=1, source_target_pairs={{0,4},{1,5},{2,6},{3,7},{4,0},{5,1},{6,2},{7,3},{8,12},{9,13},{10,... | collective-permute-start | bytes 3145736 | tf_op jit(solution)/shard_map/ppermute | solution.py:1164
  346.3 11.0 %collective-permute-start.10 = (f32[24,128]{1,0:T(8,128)S(1)}, f32[24,128]{1,0:T(8,128)S(1)}, u32[]{:S(2)}, u32[]{:S(2)}) collective-permute-start(f32[24,128]{1,0:T(8,128)S(1)} %fusion.61), channel_id=1, source_target_pairs={{0,8},{1,9},{2,10},{3,11},{4,12},{5,13},{6,14},{7,15},{8,0},{9,1},... | collective-permute-start | bytes 36872 | tf_op jit(solution)/shard_map/ppermute | solution.py:1164
  347.8 19.0 %copy-start = (bf16[4,512,1024]{2,1,0:T(8,128)(2,1)S(1)}, bf16[4,512,1024]{2,1,0:T(8,128)(2,1)}, u32[]{:S(2)}) copy-start(bf16[4,512,1024]{2,1,0:T(8,128)(2,1)} %get-tuple-element.71) | copy-start | bytes 12582916
  357.3 3.8 collective-permute-start.11
  359.9 33.3 %collective-permute-start.14 = (bf16[4,768,128]{2,1,0:T(8,128)(2,1)}, bf16[4,768,128]{2,1,0:T(8,128)(2,1)}, u32[]{:S(2)}, u32[]{:S(2)}) collective-permute-start(bf16[4,768,128]{2,1,0:T(8,128)(2,1)} %slice_bitcast_fusion.5), channel_id=1, source_target_pairs={{0,4},{1,5},{2,6},{3,7},{4,0},{5,1},{6,2},{7,3},{8,12},{9,13},{10,... | collective-permute-start | bytes 2359304 | tf_op jit(solution)/shard_map/ppermute | solution.py:1164
  361.1 10.1 %collective-permute-start.12 = (f32[24,128]{1,0:T(8,128)S(1)}, f32[24,128]{1,0:T(8,128)S(1)}, u32[]{:S(2)}, u32[]{:S(2)}) collective-permute-start(f32[24,128]{1,0:T(8,128)S(1)} %add.386), channel_id=1, source_target_pairs={{0,1},{1,0},{2,3},{3,2},{4,5},{5,4},{6,7},{7,6},{8,9},{9,8},{10,11... | collective-permute-start | bytes 36872 | tf_op jit(solution)/shard_map/ppermute | solution.py:1164
  368.3 29.8 %collective-permute-start.3 = (bf16[512,1024]{1,0:T(8,128)(2,1)}, bf16[512,1024]{1,0:T(8,128)(2,1)}, u32[]{:S(2)}, u32[]{:S(2)}) collective-permute-start(bf16[512,1024]{1,0:T(8,128)(2,1)} %get-tuple-element.122), channel_id=1, source_target_pairs={{0,1},{4,5},{8,9},{12,13},{16,17},{20,21},{24,25},{28,29}} | collective-permute-start | bytes 3145736 | tf_op jit(solution)/shard_map/ppermute | solution.py:1164
  371.2 21.4 %collective-permute-start.13 = (f32[24,128]{1,0:T(8,128)S(1)}, f32[24,128]{1,0:T(8,128)S(1)}, u32[]{:S(2)}, u32[]{:S(2)}) collective-permute-start(f32[24,128]{1,0:T(8,128)S(1)} %add.387), channel_id=1, source_target_pairs={{0,2},{1,3},{2,0},{3,1},{4,6},{5,7},{6,4},{7,5},{8,10},{9,11},{10,... | collective-permute-start | bytes 36872 | tf_op jit(solution)/shard_map/ppermute | solution.py:1164
  371.2 22.4 %copy-start.3 = (f32[512,1024]{1,0:T(8,128)S(1)}, f32[512,1024]{1,0:T(8,128)}, u32[]{:S(2)}) copy-start(f32[512,1024]{1,0:T(8,128)} %get-tuple-element.49.refs_0_) | copy-start | bytes 6291460
  377.5 47.4 %collective-permute-start.17 = (bf16[4,2112,128]{2,1,0:T(8,128)(2,1)}, bf16[4,2112,128]{2,1,0:T(8,128)(2,1)}, u32[]{:S(2)}, u32[]{:S(2)}) collective-permute-start(bf16[4,2112,128]{2,1,0:T(8,128)(2,1)} %get-tuple-element.116), channel_id=1, source_target_pairs={{0,4},{1,5},{2,6},{3,7},{4,0},{5,1},{6,2},{7,3},{8,12},{9,13},{10,... | collective-permute-start | bytes 6488072 | tf_op jit(solution)/shard_map/ppermute | solution.py:1164
  392.6 34.9 %collective-permute-start.20 = (bf16[4,2112,128]{2,1,0:T(8,128)(2,1)}, bf16[4,2112,128]{2,1,0:T(8,128)(2,1)S(1)}, u32[]{:S(2)}, u32[]{:S(2)}) collective-permute-start(bf16[4,2112,128]{2,1,0:T(8,128)(2,1)} %get-tuple-element.119), channel_id=1, source_target_pairs={{0,4},{1,5},{2,6},{3,7},{4,0},{5,1},{6,2},{7,3},{8,12},{9,13},{10,... | collective-permute-start | bytes 6488072 | tf_op jit(solution)/shard_map/ppermute | solution.py:1164
  393.1 34.9 %collective-permute-start.23 = (bf16[4,2112,128]{2,1,0:T(8,128)(2,1)}, bf16[4,2112,128]{2,1,0:T(8,128)(2,1)S(1)}, u32[]{:S(2)}, u32[]{:S(2)}) collective-permute-start(bf16[4,2112,128]{2,1,0:T(8,128)(2,1)} %get-tuple-element.118), channel_id=1, source_target_pairs={{0,4},{1,5},{2,6},{3,7},{4,0},{5,1},{6,2},{7,3},{8,12},{9,13},{10,... | collective-permute-start | bytes 6488072 | tf_op jit(solution)/shard_map/ppermute | solution.py:1164
  393.2 36.3 %collective-permute-start.26 = (bf16[4,2112,128]{2,1,0:T(8,128)(2,1)}, bf16[4,2112,128]{2,1,0:T(8,128)(2,1)S(1)}, u32[]{:S(2)}, u32[]{:S(2)}) collective-permute-start(bf16[4,2112,128]{2,1,0:T(8,128)(2,1)} %get-tuple-element.117), channel_id=1, source_target_pairs={{0,4},{1,5},{2,6},{3,7},{4,0},{5,1},{6,2},{7,3},{8,12},{9,13},{10,... | collective-permute-start | bytes 6488072 | tf_op jit(solution)/shard_map/ppermute | solution.py:1164
  398.1 11.2 %collective-permute-start.15 = (bf16[2,768,128]{2,1,0:T(8,128)(2,1)S(1)}, bf16[2,768,128]{2,1,0:T(8,128)(2,1)S(1)}, u32[]{:S(2)}, u32[]{:S(2)}) collective-permute-start(bf16[2,768,128]{2,1,0:T(8,128)(2,1)S(1)} %get-tuple-element.127), channel_id=1, source_target_pairs={{0,16},{1,17},{2,18},{3,19},{4,20},{5,21},{6,22},{7,23},{8,24},{9,... | collective-permute-start | bytes 1179656 | tf_op jit(solution)/shard_map/ppermute | solution.py:1164
  400.2 23.9 %copy-start.9 = (bf16[2,1024,128]{2,1,0:T(8,128)(2,1)}, bf16[2,1024,128]{2,1,0:T(8,128)(2,1)S(1)}, u32[]{:S(2)}) copy-start(bf16[2,1024,128]{2,1,0:T(8,128)(2,1)S(1)} %get-tuple-element.124) | copy-start | bytes 1572868
  409.3 13.2 %collective-permute-start.30 = (bf16[2,1024,128]{2,1,0:T(8,128)(2,1)S(1)}, bf16[2,1024,128]{2,1,0:T(8,128)(2,1)S(1)}, u32[]{:S(2)}, u32[]{:S(2)}) collective-permute-start(bf16[2,1024,128]{2,1,0:T(8,128)(2,1)S(1)} %get-tuple-element.125), channel_id=1, source_target_pairs={{0,16},{1,17},{2,18},{3,19},{4,20},{5,21},{6,22},{7,23},{8,24},{9,... | collective-permute-start | bytes 1572872 | tf_op jit(solution)/shard_map/ppermute | solution.py:1164
  422.5 22.6 %collective-permute-start.6 = (bf16[512,1024]{1,0:T(8,128)(2,1)}, bf16[512,1024]{1,0:T(8,128)(2,1)}, u32[]{:S(2)}, u32[]{:S(2)}) collective-permute-start(bf16[512,1024]{1,0:T(8,128)(2,1)} %get-tuple-element.123), channel_id=1, source_target_pairs={{3,2},{7,6},{11,10},{15,14},{19,18},{23,22},{27,26},{31,30}} | collective-permute-start | bytes 3145736 | tf_op jit(solution)/shard_map/ppermute | solution.py:1164
  424.9 22.9 %collective-permute-start.4 = (bf16[512,1024]{1,0:T(8,128)(2,1)}, bf16[512,1024]{1,0:T(8,128)(2,1)}, u32[]{:S(2)}, u32[]{:S(2)}) collective-permute-start(bf16[512,1024]{1,0:T(8,128)(2,1)} %fusion.16), channel_id=1, source_target_pairs={{0,1},{1,2},{4,5},{5,6},{8,9},{9,10},{12,13},{13,14},{16,17},{17,1... | collective-permute-start | bytes 3145736 | tf_op jit(solution)/shard_map/ppermute | solution.py:1164
  427.5 10.5 %collective-permute-start.16 = (bf16[768,128]{1,0:T(8,128)(2,1)S(1)}, bf16[768,128]{1,0:T(8,128)(2,1)S(1)}, u32[]{:S(2)}, u32[]{:S(2)}) collective-permute-start(bf16[768,128]{1,0:T(8,128)(2,1)S(1)} %fusion.50), channel_id=1, source_target_pairs={{0,8},{1,9},{2,10},{3,11},{4,12},{5,13},{6,14},{7,15},{8,0},{9,1},... | collective-permute-start | bytes 589832 | tf_op jit(solution)/shard_map/ppermute | solution.py:1164
  428.0 13.7 %collective-permute-start.31 = (bf16[1024,128]{1,0:T(8,128)(2,1)}, bf16[1024,128]{1,0:T(8,128)(2,1)}, u32[]{:S(2)}, u32[]{:S(2)}) collective-permute-start(bf16[1024,128]{1,0:T(8,128)(2,1)} %fusion.48), channel_id=1, source_target_pairs={{0,8},{1,9},{2,10},{3,11},{4,12},{5,13},{6,14},{7,15},{8,0},{9,1},... | collective-permute-start | bytes 786440 | tf_op jit(solution)/shard_map/ppermute | solution.py:1164
  436.5 27.2 %collective-permute-start.18 = (bf16[2,2112,128]{2,1,0:T(8,128)(2,1)}, bf16[2,2112,128]{2,1,0:T(8,128)(2,1)}, u32[]{:S(2)}, u32[]{:S(2)}) collective-permute-start(bf16[2,2112,128]{2,1,0:T(8,128)(2,1)} %get-tuple-element.103), channel_id=1, source_target_pairs={{0,16},{1,17},{2,18},{3,19},{4,20},{5,21},{6,22},{7,23},{8,24},{9,... | collective-permute-start | bytes 3244040 | tf_op jit(solution)/shard_map/ppermute | solution.py:1164
  439.0 8.8 %copy-start.1 = (bf16[4,512,1024]{2,1,0:T(8,128)(2,1)S(1)}, bf16[4,512,1024]{2,1,0:T(8,128)(2,1)}, u32[]{:S(2)}) copy-start(bf16[4,512,1024]{2,1,0:T(8,128)(2,1)} %get-tuple-element.71) | copy-start | bytes 12582916
  442.9 43.8 %collective-permute-start.21 = (bf16[2,2112,128]{2,1,0:T(8,128)(2,1)}, bf16[2,2112,128]{2,1,0:T(8,128)(2,1)S(1)}, u32[]{:S(2)}, u32[]{:S(2)}) collective-permute-start(bf16[2,2112,128]{2,1,0:T(8,128)(2,1)} %get-tuple-element.114), channel_id=1, source_target_pairs={{0,16},{1,17},{2,18},{3,19},{4,20},{5,21},{6,22},{7,23},{8,24},{9,... | collective-permute-start | bytes 3244040 | tf_op jit(solution)/shard_map/ppermute | solution.py:1164
  443.6 66.3 %collective-permute-start.24 = (bf16[2,2112,128]{2,1,0:T(8,128)(2,1)}, bf16[2,2112,128]{2,1,0:T(8,128)(2,1)S(1)}, u32[]{:S(2)}, u32[]{:S(2)}) collective-permute-start(bf16[2,2112,128]{2,1,0:T(8,128)(2,1)} %get-tuple-element.112), channel_id=1, source_target_pairs={{0,16},{1,17},{2,18},{3,19},{4,20},{5,21},{6,22},{7,23},{8,24},{9,... | collective-permute-start | bytes 3244040 | tf_op jit(solution)/shard_map/ppermute | solution.py:1164
  445.1 23.7 %copy-start.6 = (bf16[2,2112,128]{2,1,0:T(8,128)(2,1)S(1)}, bf16[2,2112,128]{2,1,0:T(8,128)(2,1)}, u32[]{:S(2)}) copy-start(bf16[2,2112,128]{2,1,0:T(8,128)(2,1)} %get-tuple-element.102) | copy-start | bytes 3244036
  445.1 84.8 %collective-permute-start.27 = (bf16[2,2112,128]{2,1,0:T(8,128)(2,1)}, bf16[2,2112,128]{2,1,0:T(8,128)(2,1)S(1)}, u32[]{:S(2)}, u32[]{:S(2)}) collective-permute-start(bf16[2,2112,128]{2,1,0:T(8,128)(2,1)} %get-tuple-element.110), channel_id=1, source_target_pairs={{0,16},{1,17},{2,18},{3,19},{4,20},{5,21},{6,22},{7,23},{8,24},{9,... | collective-permute-start | bytes 3244040 | tf_op jit(solution)/shard_map/ppermute | solution.py:1164
  450.4 108.4 %collective-permute-start.7 = (bf16[512,1024]{1,0:T(8,128)(2,1)S(1)}, bf16[512,1024]{1,0:T(8,128)(2,1)S(1)}, u32[]{:S(2)}, u32[]{:S(2)}) collective-permute-start(bf16[512,1024]{1,0:T(8,128)(2,1)S(1)} %get-tuple-element.121), channel_id=1, source_target_pairs={{2,1},{3,2},{6,5},{7,6},{10,9},{11,10},{14,13},{15,14},{18,17},{19... | collective-permute-start | bytes 3145736 | tf_op jit(solution)/shard_map/ppermute | solution.py:1164
  463.7 109.8 %collective-permute-start.5 = (bf16[512,1024]{1,0:T(8,128)(2,1)S(1)}, bf16[512,1024]{1,0:T(8,128)(2,1)S(1)}, u32[]{:S(2)}, u32[]{:S(2)}) collective-permute-start(bf16[512,1024]{1,0:T(8,128)(2,1)S(1)} %get-tuple-element.120), channel_id=1, source_target_pairs={{0,1},{1,2},{2,3},{4,5},{5,6},{6,7},{8,9},{9,10},{10,11},{12,13},{... | collective-permute-start | bytes 3145736 | tf_op jit(solution)/shard_map/ppermute | solution.py:1164
  486.8 43.9 %collective-permute-start.19 = (bf16[2112,128]{1,0:T(8,128)(2,1)S(1)}, bf16[2112,128]{1,0:T(8,128)(2,1)S(1)}, u32[]{:S(2)}, u32[]{:S(2)}) collective-permute-start(bf16[2112,128]{1,0:T(8,128)(2,1)S(1)} %fusion.31), channel_id=1, source_target_pairs={{0,8},{1,9},{2,10},{3,11},{4,12},{5,13},{6,14},{7,15},{8,0},{9,1},... | collective-permute-start | bytes 1622024 | tf_op jit(solution)/shard_map/ppermute | solution.py:1164
  509.9 23.5 %collective-permute-start.22 = (bf16[2112,128]{1,0:T(8,128)(2,1)S(1)}, bf16[2112,128]{1,0:T(8,128)(2,1)S(1)}, u32[]{:S(2)}, u32[]{:S(2)}) collective-permute-start(bf16[2112,128]{1,0:T(8,128)(2,1)S(1)} %fusion.33), channel_id=1, source_target_pairs={{0,8},{1,9},{2,10},{3,11},{4,12},{5,13},{6,14},{7,15},{8,0},{9,1},... | collective-permute-start | bytes 1622024 | tf_op jit(solution)/shard_map/ppermute | solution.py:1164
  530.0 15.2 %collective-permute-start.25 = (bf16[2112,128]{1,0:T(8,128)(2,1)S(1)}, bf16[2112,128]{1,0:T(8,128)(2,1)S(1)}, u32[]{:S(2)}, u32[]{:S(2)}) collective-permute-start(bf16[2112,128]{1,0:T(8,128)(2,1)S(1)} %fusion.35), channel_id=1, source_target_pairs={{0,8},{1,9},{2,10},{3,11},{4,12},{5,13},{6,14},{7,15},{8,0},{9,1},... | collective-permute-start | bytes 1622024 | tf_op jit(solution)/shard_map/ppermute | solution.py:1164
  530.6 22.1 %collective-permute-start.28 = (bf16[2112,128]{1,0:T(8,128)(2,1)S(1)}, bf16[2112,128]{1,0:T(8,128)(2,1)S(1)}, u32[]{:S(2)}, u32[]{:S(2)}) collective-permute-start(bf16[2112,128]{1,0:T(8,128)(2,1)S(1)} %fusion.37), channel_id=1, source_target_pairs={{0,8},{1,9},{2,10},{3,11},{4,12},{5,13},{6,14},{7,15},{8,0},{9,1},... | collective-permute-start | bytes 1622024 | tf_op jit(solution)/shard_map/ppermute | solution.py:1164
  553.5 14.3 %collective-permute-start.32 = (bf16[2368,128]{1,0:T(8,128)(2,1)S(1)}, bf16[2368,128]{1,0:T(8,128)(2,1)S(1)}, u32[]{:S(2)}, u32[]{:S(2)}) collective-permute-start(bf16[2368,128]{1,0:T(8,128)(2,1)S(1)} %pad_maximum_fusion.3), channel_id=1, source_target_pairs={{0,1},{4,5},{8,9},{12,13},{16,17},{20,21},{24,25},{28,29}} | collective-permute-start | bytes 1818632 | tf_op jit(solution)/shard_map/ppermute | solution.py:1164
  559.1 22.7 %collective-permute-start.8 = (bf16[512,1024]{1,0:T(8,128)(2,1)S(1)}, bf16[512,1024]{1,0:T(8,128)(2,1)S(1)}, u32[]{:S(2)}, u32[]{:S(2)}) collective-permute-start(bf16[512,1024]{1,0:T(8,128)(2,1)S(1)} %fusion.15), channel_id=1, source_target_pairs={{1,0},{2,1},{3,2},{5,4},{6,5},{7,6},{9,8},{10,9},{11,10},{13,12},{... | collective-permute-start | bytes 3145736 | tf_op jit(solution)/shard_map/ppermute | solution.py:1164
  560.5 12.1 %collective-permute-start.35 = (bf16[2368,128]{1,0:T(8,128)(2,1)S(1)}, bf16[2368,128]{1,0:T(8,128)(2,1)S(1)}, u32[]{:S(2)}, u32[]{:S(2)}) collective-permute-start(bf16[2368,128]{1,0:T(8,128)(2,1)S(1)} %pad_maximum_fusion.4), channel_id=1, source_target_pairs={{3,2},{7,6},{11,10},{15,14},{19,18},{23,22},{27,26},{31,30}} | collective-permute-start | bytes 1818632 | tf_op jit(solution)/shard_map/ppermute | solution.py:1164
  568.0 13.9 %copy-start.2 = (bf16[1,512,1024]{2,1,0:T(8,128)(2,1)S(1)}, bf16[1,512,1024]{2,1,0:T(8,128)(2,1)}, u32[]{:S(2)}) copy-start(bf16[1,512,1024]{2,1,0:T(8,128)(2,1)} %param.20) | copy-start | bytes 3145732
  568.0 14.7 %collective-permute-start.33 = (bf16[2368,128]{1,0:T(8,128)(2,1)S(1)}, bf16[2368,128]{1,0:T(8,128)(2,1)S(1)}, u32[]{:S(2)}, u32[]{:S(2)}) collective-permute-start(bf16[2368,128]{1,0:T(8,128)(2,1)S(1)} %add_convert_fusion.4), channel_id=1, source_target_pairs={{0,1},{1,2},{4,5},{5,6},{8,9},{9,10},{12,13},{13,14},{16,17},{17,1... | collective-permute-start | bytes 1818632 | tf_op jit(solution)/shard_map/ppermute | solution.py:1164
  572.8 13.7 %collective-permute-start.36 = (bf16[2368,128]{1,0:T(8,128)(2,1)S(1)}, bf16[2368,128]{1,0:T(8,128)(2,1)S(1)}, u32[]{:S(2)}, u32[]{:S(2)}) collective-permute-start(bf16[2368,128]{1,0:T(8,128)(2,1)S(1)} %add_convert_fusion.2), channel_id=1, source_target_pairs={{2,1},{3,2},{6,5},{7,6},{10,9},{11,10},{14,13},{15,14},{18,17},{19... | collective-permute-start | bytes 1818632 | tf_op jit(solution)/shard_map/ppermute | solution.py:1164
  582.9 11.0 %collective-permute-start.34 = (bf16[2368,128]{1,0:T(8,128)(2,1)S(1)}, bf16[2368,128]{1,0:T(8,128)(2,1)S(1)}, u32[]{:S(2)}, u32[]{:S(2)}) collective-permute-start(bf16[2368,128]{1,0:T(8,128)(2,1)S(1)} %add_convert_fusion.3), channel_id=1, source_target_pairs={{0,1},{1,2},{2,3},{4,5},{5,6},{6,7},{8,9},{9,10},{10,11},{12,13},{... | collective-permute-start | bytes 1818632 | tf_op jit(solution)/shard_map/ppermute | solution.py:1164
  586.6 30.2 %collective-permute-start.37 = (bf16[2368,128]{1,0:T(8,128)(2,1)S(1)}, bf16[2368,128]{1,0:T(8,128)(2,1)S(1)}, u32[]{:S(2)}, u32[]{:S(2)}) collective-permute-start(bf16[2368,128]{1,0:T(8,128)(2,1)S(1)} %add_convert_fusion.1), channel_id=1, source_target_pairs={{1,0},{2,1},{3,2},{5,4},{6,5},{7,6},{9,8},{10,9},{11,10},{13,12},{... | collective-permute-start | bytes 1818632 | tf_op jit(solution)/shard_map/ppermute | solution.py:1164
  (21 other events, 49.0 us)

commit v2 on v1

--- a/solution.py
+++ b/solution.py
@@ -20,6 +20,8 @@
 ATTN_ROWS = 784
 VMEM_LIMIT = 56 << 20
 OPEN_COPIES = 66
+CLOSE_COPIES = 64
+CLOSE_VMEM = 60 << 20
 
 
 def arrivals(plane):
@@ -443,7 +445,7 @@
 
     def go(self, number, source, target, to, when=None):
         copy = self.copy(number, source, target, to)
-        self.started.append((copy, when))
+        self.started.append((number, source, target, to, when))
         if when is None:
             copy.start()
         else:
@@ -457,7 +459,8 @@
             pl.when(when)(copy.wait_recv)
 
     def drain(self):
-        for copy, when in self.started:
+        for *parts, when in self.started:
+            copy = self.copy(*parts)
             if when is None:
                 copy.wait_send()
             else:
@@ -814,10 +817,15 @@
     )(hidden, attn_piece, out_piece, feed_piece, cosine, sine_part, first_values, begin_column)
 
 
-def feed_kernel(normed_ref, grad_ref, pieces, feed_ref, back_ref, made_out, weight, made, act, gate, up, sem, out_sem):
-    slot = pl.program_id(0)
-    place = lax.axis_index("dp")
-    now = lax.rem(slot, 2)
+def feed_kernel(*refs):
+    normed_ref, grad_ref, middle_ref, pieces = refs[:4]
+    back_ref, out_ref, made_out = refs[4:7]
+    fed, weight, mine, theirs, made, halves, other_halves, send, recv, sem, out_sem = refs[7:]
+    links = Links(send, recv)
+    core = (flip(links.place, 1), links.depth)
+    mine_first, theirs_first = lax.rem(links.place, 2), 1 - lax.rem(links.place, 2)
+    count = weight.shape[1] // 3
+    rows = normed_ref.shape[0]
 
     def load(which, buffer):
         return [
@@ -832,218 +840,605 @@
     def flush(which, buffer):
         return [
             pltpu.make_async_copy(
-                made.at[buffer, :, piece_columns(place, index)],
-                made_out.at[which, index & 1, index >> 1],
-                out_sem.at[buffer, index],
+                made.at[buffer, :, pl.ds(piece * PIECE, PIECE)],
+                made_out.at[which, piece],
+                out_sem.at[buffer, piece],
             )
-            for index in range(8)
+            for piece in range(4)
         ]
 
-    @pl.when(slot == 0)
-    def _():
-        for copy in load(slot, now):
-            copy.start()
-        feed_ref[...] = jnp.zeros_like(feed_ref)
-        back_ref[...] = jnp.zeros_like(back_ref)
-
-    @pl.when(slot + 1 < PLANES)
-    def _():
-        for copy in load(slot + 1, 1 - now):
-            copy.start()
-
-    for copy in load(slot, now):
-        copy.wait()
-
-    @pl.when(slot >= 2)
-    def _():
-        for copy in flush(slot - 2, now):
-            copy.wait()
-
-    count = weight.shape[1] // 3
-    rows = normed_ref.shape[0]
+    for copy in load(0, 0):
+        copy.start()
+    barrier = pltpu.get_barrier_semaphore()
+    pl.semaphore_signal(barrier, inc=1, device_id=core, device_id_type=MESH)
+    pl.semaphore_wait(barrier, 1)
+    base = links.number(8)
+    for index, ref in enumerate((normed_ref, grad_ref)):
+        for piece in range(4):
+            links.go(
+                base + 4 * index + piece,
+                ref.at[:, columns_of(2 * piece + theirs_first)],
+                other_halves.at[index, :, pl.ds(piece * PIECE, PIECE)],
+                core,
+            )
+            halves[index, :, pl.ds(piece * PIECE, PIECE)] = ref[:, columns_of(2 * piece + mine_first)]
+    fed[...] = jnp.zeros_like(fed)
+    back_ref[...] = jnp.zeros_like(back_ref)
+    for index in range(2):
+        for piece in range(4):
+            links.got(
+                base + 4 * index + piece, other_halves.at[index, :, pl.ds(piece * PIECE, PIECE)]
+            )
+    given = links.number(PLANES)
+    hand = lambda slot: links.copy(given + slot, mine.at[lax.rem(slot, 2)], theirs.at[slot], core)
     spans = [pl.ds(index * count, count) for index in range(3)]
     half = rows // 2
-    for tile in range(2):
-        at = pl.ds(tile * half, half)
-        normed, grad = normed_ref[at, :], grad_ref[at, :]
-        gates = tokens_dot(weight[now, spans[0], :], normed, 1, 1)
-        ups = tokens_dot(weight[now, spans[1], :], normed, 1, 1)
-        backs = tokens_dot(weight[now, spans[2], :], grad, 1, 1)
-        sig = jax.nn.sigmoid(gates)
-        active = gates * sig
-        act[:, at] = (active * ups).astype(jnp.bfloat16)
-        gate[:, at] = (backs * ups * sig * (1.0 + gates * (1.0 - sig))).astype(jnp.bfloat16)
-        up[:, at] = (backs * active).astype(jnp.bfloat16)
-
-    def columns(tile, carried):
-        lanes = columns_of(tile, 256)
-        normed, grad = normed_ref[:, lanes], grad_ref[:, lanes]
-        made[now, spans[0], lanes] = tokens_dot(gate[...], normed, 1, 0).astype(jnp.bfloat16)
-        made[now, spans[1], lanes] = tokens_dot(up[...], normed, 1, 0).astype(jnp.bfloat16)
-        made[now, spans[2], lanes] = tokens_dot(act[...], grad, 1, 0).astype(jnp.bfloat16)
-        feed_ref[:, lanes] += tokens_dot(act[...], weight[now, spans[2], lanes], 0, 0)
-        back_ref[:, lanes] += tokens_dot(gate[...], weight[now, spans[0], lanes], 0, 0) + tokens_dot(
-            up[...], weight[now, spans[1], lanes], 0, 0
-        )
+
+    def forward(slot):
+        now = lax.rem(slot, 2)
+        for copy in load(slot, now):
+            copy.wait()
+
+        @pl.when(slot + 1 < PLANES)
+        def _():
+            for copy in load(slot + 1, 1 - now):
+                copy.start()
+
+        @pl.when(slot >= 2)
+        def _():
+            hand(slot - 2).wait_send()
+
+        for tile in range(2):
+            at = pl.ds(tile * half, half)
+            normed, grad = normed_ref[at, :], grad_ref[at, :]
+            gates = tokens_dot(weight[now, spans[0], :], normed, 1, 1)
+            ups = tokens_dot(weight[now, spans[1], :], normed, 1, 1)
+            backs = tokens_dot(weight[now, spans[2], :], grad, 1, 1)
+            sig = jax.nn.sigmoid(gates)
+            active = gates * sig
+            mine[now, 2, :, at] = (active * ups).astype(jnp.bfloat16)
+            mine[now, 0, :, at] = (backs * ups * sig * (1.0 + gates * (1.0 - sig))).astype(jnp.bfloat16)
+            mine[now, 1, :, at] = (backs * active).astype(jnp.bfloat16)
+        hand(slot).start()
+
+        def columns(tile, carried):
+            lanes = columns_of(tile, 256)
+            fed[:, lanes] += tokens_dot(mine[now, 2], weight[now, spans[2], lanes], 0, 0)
+            back_ref[:, lanes] += tokens_dot(
+                mine[now, 0], weight[now, spans[0], lanes], 0, 0
+            ) + tokens_dot(mine[now, 1], weight[now, spans[1], lanes], 0, 0)
+            return carried
+
+        lax.fori_loop(0, D // 256, columns, 0)
+
+    def backward(slot):
+        now = lax.rem(slot, 2)
+        hand(slot).wait_recv()
+
+        @pl.when(slot >= 2)
+        def _():
+            for copy in flush(slot - 2, now):
+                copy.wait()
+
+        def columns(tile, carried):
+            lanes = columns_of(tile, 256)
+            for index in range(3):
+                which = index // 2
+                made[now, spans[index], lanes] = (
+                    tokens_dot(mine[now, index], halves[which, :, lanes], 1, 0)
+                    + tokens_dot(theirs[slot, index], other_halves[which, :, lanes], 1, 0)
+                ).astype(jnp.bfloat16)
+            return carried
+
+        lax.fori_loop(0, 2, columns, 0)
+        for copy in flush(slot, now):
+            copy.start()
+
+    def one(step, carried):
+        pl.when(step < PLANES)(lambda: forward(step))
+        pl.when(step >= 1)(lambda: backward(step - 1))
         return carried
 
-    lax.fori_loop(0, D // 256, columns, 0)
-    for copy in flush(slot, now):
-        copy.start()
-
-    @pl.when(slot == PLANES - 1)
-    def _():
-        for copy in flush(slot - 1, 1 - now) + flush(slot, now):
+    lax.fori_loop(0, PLANES + 1, one, 0)
+    out_ref[...] = (middle_ref[...] + fed[...]).astype(jnp.bfloat16)
+    for slot in (PLANES - 2, PLANES - 1):
+        hand(slot).wait_send()
+        for copy in flush(slot, slot % 2):
             copy.wait()
-
-
-def feed(normed, grad, pieces):
+    links.drain()
+
+
+def feed(normed, grad, middle, pieces):
     rows = normed.shape[0]
     count = pieces.shape[2]
-    any_spec = pl.BlockSpec(memory_space=pl.ANY)
-    whole = pl.BlockSpec((rows, D), lambda i: (0, 0))
-    total = jax.ShapeDtypeStruct((rows, D), jnp.float32)
-    narrow = pltpu.VMEM((count // 3, rows), jnp.bfloat16)
+    any_spec, vmem = pl.BlockSpec(memory_space=pl.ANY), pl.BlockSpec(memory_space=pltpu.VMEM)
+    low = jnp.bfloat16
     return pl.pallas_call(
         feed_kernel,
-        grid=(PLANES,),
-        in_specs=[whole, whole, any_spec],
-        out_specs=[whole, whole, any_spec],
+        in_specs=[vmem, vmem, vmem, any_spec],
+        out_specs=[vmem, vmem, any_spec],
         out_shape=[
-            total,
-            total,
-            jax.ShapeDtypeStruct((PLANES, 2, 4, count, PIECE), jnp.bfloat16),
+            jax.ShapeDtypeStruct((rows, D), jnp.float32),
+            jax.ShapeDtypeStruct((rows, D), low),
+            jax.ShapeDtypeStruct((PLANES, 4, count, PIECE), low),
         ],
         scratch_shapes=[
-            pltpu.VMEM((2, count, D), jnp.bfloat16),
-            pltpu.VMEM((2, count, D), jnp.bfloat16),
-            narrow,
-            narrow,
-            narrow,
+            pltpu.VMEM((rows, D), jnp.float32),
+            pltpu.VMEM((2, count, D), low),
+            pltpu.VMEM((2, 3, count // 3, rows), low),
+            pltpu.VMEM((PLANES, 3, count // 3, rows), low),
+            pltpu.VMEM((2, count, 4 * PIECE), low),
+            pltpu.VMEM((2, rows, 4 * PIECE), low),
+            pltpu.VMEM((2, rows, 4 * PIECE), low),
+            pltpu.SemaphoreType.DMA((12,)),
+            pltpu.SemaphoreType.DMA((12,)),
             pltpu.SemaphoreType.DMA((2, 8)),
-            pltpu.SemaphoreType.DMA((2, 8)),
+            pltpu.SemaphoreType.DMA((2, 4)),
         ],
-        compiler_params=pltpu.CompilerParams(vmem_limit_bytes=VMEM_LIMIT),
-        cost_estimate=cost(24 * rows * D * count, 40 << 20),
+        compiler_params=pltpu.CompilerParams(
+            vmem_limit_bytes=VMEM_LIMIT, collective_id=2, has_side_effects=True
+        ),
         name="feed",
-    )(normed, grad, pieces)
-
-
-def flash_back_kernel(*refs):
-    low_ref, q_ref, k_ref, v_ref, o_ref = refs[:5]
-    incoming = refs[5:9]
-    log_ref, begin_ref, cos_ref, sin_ref = refs[9:13]
-    dq_ref, dk_ref, dv_ref, first_ref = refs[13:17]
-    grad, inner, total, queries, grads, sem = refs[17:]
-    pair, block = pl.program_id(0), pl.program_id(1)
-    depth = lax.axis_index("mp")
+    )(normed, grad, middle, pieces)
+
+
+def add_into(target, source):
+    rows = target.shape[0]
+    chunk = next(c for c in (352, 256, rows) if rows % c == 0)
+
+    def one(index, carried):
+        span = pl.ds(pl.multiple_of(index * chunk, chunk), chunk)
+        target[span, :] = (
+            target[span, :].astype(jnp.float32) + source[span, :].astype(jnp.float32)
+        ).astype(jnp.bfloat16)
+        return carried
+
+    lax.fori_loop(0, rows // chunk, one, 0)
+
+
+class Fold:
+    def __init__(self, links, whole, first, final, bits):
+        self.links, self.first, self.final = links, [first.at[m] for m in range(2)], final
+        self.base = links.number(3)
+        chip = lax.div(links.place, 2)
+        ones = lambda bit: lax.rem(lax.div(chip, bit), 2)
+        near, far = ones(bits[0]), ones(bits[1])
+        self.away = [whole((1 - near) * bits[0] + m * bits[1]) for m in range(2)]
+        self.stay = [whole(near * bits[0] + m * bits[1]) for m in range(2)]
+        self.near_to = (flip(links.place, 2 * bits[0]), links.depth)
+        self.far_to = (flip(links.place, 2 * bits[1]), links.depth)
+        self.passed, self.own = first.at[1 - far], first.at[far]
+
+    def one(self):
+        for m in range(2):
+            self.links.go(self.base + m, self.away[m], self.first[m], self.near_to)
+
+    def two(self, stay=None):
+        for m in range(2):
+            self.links.got(self.base + m, self.first[m])
+            add_into(self.first[m], self.stay[m] if stay is None else stay[m])
+        self.links.go(self.base + 2, self.passed, self.final, self.far_to)
+
+    def end(self):
+        self.links.got(self.base + 2, self.final)
+        add_into(self.final, self.own)
+
+
+class LineFold:
+    def __init__(self, links, block, held):
+        self.links = links
+        self.held = [[held.at[way, step] for step in range(PLANES - 1)] for way in range(2)]
+        self.base = links.number(2 * (PLANES - 1))
+        depth = links.depth
+        self.blocks, self.sends, self.sums, self.takes, self.to = [], [], [], [], []
+        for step in range(1, PLANES):
+            right = jnp.minimum(depth + PLANES - step, PLANES - 1)
+            left = jnp.maximum(depth - PLANES + step, 0)
+            self.blocks.append((block(left), block(right)))
+            self.sends.append((depth >= PLANES - step, depth < step))
+            self.takes.append(((depth >= PLANES - 1 - step) & (depth < PLANES - 1), (depth <= step) & (depth > 0)))
+        self.ends = (depth == PLANES - 1, depth == 0)
+        self.to = (
+            (links.place, jnp.maximum(depth - 1, 0)),
+            (links.place, jnp.minimum(depth + 1, PLANES - 1)),
+        )
+        self.inner = [
+            [self.sends[step][way] & jnp.logical_not(self.ends[way]) for way in range(2)]
+            for step in range(PLANES - 1)
+        ]
+        self.outer = [
+            [self.sends[step][way] & self.ends[way] for way in range(2)] for step in range(PLANES - 1)
+        ]
+
+    def launch(self, step):
+        for way in range(2):
+            self.links.go(
+                self.base + 2 * (step - 1) + way,
+                self.blocks[step - 1][way],
+                self.held[way][step - 1],
+                self.to[way],
+                self.outer[step - 1][way],
+            )
+
+    def take(self, step):
+        for way in range(2):
+            self.links.got(
+                self.base + 2 * (step - 1) + way, self.held[way][step - 1], self.takes[step - 1][way]
+            )
+
+    def forward(self, step):
+        for way in range(2):
+            before = self.held[way][step - 2]
+            block = self.blocks[step - 1][way]
+
+            @pl.when(self.inner[step - 1][way])
+            def _():
+                add_into(before, block)
+
+            self.links.go(
+                self.base + 2 * (step - 1) + way,
+                before,
+                self.held[way][step - 1],
+                self.to[way],
+                self.inner[step - 1][way],
+            )
+
+    def total(self, own, out):
+        depth = self.links.depth
+        rows = out.shape[0]
+        chunk = next(c for c in (352, 256, rows) if rows % c == 0)
+
+        def one(index, carried):
+            span = pl.ds(pl.multiple_of(index * chunk, chunk), chunk)
+            value = own[span, :].astype(jnp.float32)
+            sides = [self.held[way][PLANES - 2][span, :].astype(jnp.float32) for way in range(2)]
+            value = value + jnp.where(depth < PLANES - 1, sides[0], 0.0)
+            out[span, :] = value + jnp.where(depth > 0, sides[1], 0.0)
+            return carried
+
+        lax.fori_loop(0, rows // chunk, one, 0)
+
+
+def close_kernel(*refs):
+    (made, low_in, attended_in, q_in, k_in, v_in, o_in, n_in, weight_in, cos_in, sin_in) = refs[:11]
+    incoming = refs[11:15]
+    log_ref, begin_ref, gain_ref, small_in = refs[15:19]
+    first_ref, back_ref, feed_total, out_total, attn_total, small_ref = refs[19:25]
+    (
+        q_ref, k_ref, v_ref, o_ref, n_ref, weight_ref, cos_ref, sin_ref, grad, inner, total, made_ref,
+        stay, feed_first, feed_final, feed_held, out_made, out_core, out_first, out_final, out_held,
+        attn_core, attn_first, attn_final, partial, partial_held, small_got,
+        send, recv, local,
+    ) = refs[25:]
+    links = Links(send, recv)
+    place, depth = links.place, links.depth
     length = q_ref.shape[0]
-    rows = length // BLOCKS
     shard = length // PLANES
-    lane = lax.broadcasted_iota(jnp.int32, (rows, 128), 1)
-
-    @pl.when(block == 0)
-    def _():
+    parity, chip = lax.rem(place, 2), lax.div(place, 2)
+    core = (flip(place, 1), depth)
+    loads = []
+
+    def load(source, target):
+        copy = pltpu.make_async_copy(source, target, local.at[len(loads)])
+        copy.start()
+        loads.append(copy)
+        return copy
+
+    order = (3, 2, 1, 0)
+    folds = {
+        slot: Fold(
+            links,
+            lambda i, slot=slot: made.at[slot, i],
+            feed_first.at[slot],
+            feed_final.at[slot],
+            (1, 2) if slot % 2 else (2, 1),
+        )
+        for slot in order
+    }
+    out_fold = Fold(links, lambda i: out_core.at[i], out_first, out_final, (1, 2))
+    attn_fold = Fold(links, lambda i: attn_core.at[i], attn_first, attn_final, (1, 2))
+
+    def slot_holding(block):
+        found = 0
+        for plane in range(PLANES):
+            for slot, (_, _, held) in enumerate(SLOTS[plane]):
+                found = found + jnp.where((depth == plane) & (block == held), slot, 0)
+        return found
+
+    feed_line = LineFold(links, lambda j: feed_final.at[slot_holding(j)], feed_held)
+    out_line = LineFold(
+        links, lambda j: out_final.at[pl.ds(pl.multiple_of(j * 256, 256), 256), :], out_held
+    )
+    line = LineFold(links, lambda j: partial.at[j], partial_held)
+    out_swap, attn_swap = links.number(4), links.number(4)
+    sides = [columns_of(2 * i + parity) for i in range(4)]
+    others = [columns_of(2 * i + 1 - parity) for i in range(4)]
+    across = links.number(PLANES)
+    tiny = links.number(6)
+    stays = [[stay.at[index, m] for m in range(2)] for index in range(2)]
+    tiny_to = [core, (flip(place, 2), depth), (flip(place, 4), depth)]
+    plane_to = [(place, lax.rem(depth + step, PLANES)) for step in range(1, PLANES)]
+    plane_rows = [lax.rem(depth - step + PLANES, PLANES) for step in range(PLANES)]
+
+    attended_ref, low_ref = partial.at[0], partial.at[1]
+    first_loads = [load(attended_in, attended_ref), load(low_in, low_ref)]
+    for slot in order[:2]:
+        for m in range(2):
+            load(folds[slot].stay[m], stays[slot % 2][m])
+    q_loads = [load(source, target) for source, target in ((q_in, q_ref), (k_in, k_ref), (v_in, v_ref), (o_in, o_ref), (cos_in, cos_ref), (sin_in, sin_ref))]
+    own_rows = pl.ds(pl.multiple_of(depth * shard, shard), shard)
+    q_loads.append(load(incoming[0], grad.at[own_rows, :]))
+    late = [load(n_in, n_ref), load(weight_in, weight_ref)]
+
+    links.greet()
+    for step in range(1, PLANES):
+        links.go(across + step, incoming[step], grad.at[own_rows, :], plane_to[step - 1])
+    for slot in order[:2]:
+        folds[slot].one()
+
+    for copy in first_loads:
+        copy.wait()
+    for index in range(4):
+        rows = pl.ds(index * 256, 256)
+        out_made[rows, :] = tokens_dot(attended_ref[:, rows], low_ref[...], 0, 0).astype(jnp.bfloat16)
+    out_swaps = [links.copy(out_swap + i, out_made.at[:, others[i]], out_core.at[i], core) for i in range(4)]
+    for copy in out_swaps:
+        copy.start()
+    for i in range(4):
+        links.got(out_swap + i, out_core.at[i])
+        add_into(out_core.at[i], out_made.at[:, sides[i]])
+    out_fold.one()
+
+    def restay(slot):
         copies = [
-            pltpu.make_async_copy(
-                piece.at[:, pl.ds(pl.multiple_of(pair * 128, 128), 128)],
-                grad.at[pl.ds(pl.multiple_of(lax.rem(depth - index + PLANES, PLANES) * shard, shard), shard)],
-                sem.at[index],
-            )
-            for index, piece in enumerate(incoming)
+            pltpu.make_async_copy(folds[slot].stay[m], stays[slot % 2][m], local.at[16 + 2 * (slot % 2) + m])
+            for m in range(2)
         ]
-        for copy in copies:
+        return copies
+
+    for copy in loads[2:6]:
+        copy.wait()
+    for copy in q_loads:
+        copy.wait()
+    for slot in order[:2]:
+        folds[slot].two(stays[slot % 2])
+    for slot in order[2:]:
+        folds[slot].one()
+        for copy in restay(slot):
             copy.start()
-        for copy in copies:
-            copy.wait()
-        total[...] = jnp.zeros_like(total)
-        for index in range(BLOCKS):
-            span = pl.ds(index * rows, rows)
-            product = grad[span, :].astype(jnp.float32) * o_ref[span, :].astype(jnp.float32)
-            turned = jnp.transpose(product)
+    for step in range(1, PLANES):
+        links.got(across + step, grad.at[pl.ds(pl.multiple_of(plane_rows[step] * shard, shard), shard), :])
+
+    lane = lax.broadcasted_iota(jnp.int32, (shard, 128), 1)
+    keeps = [lane < HD, lane >= HD]
+    down = lax.broadcasted_iota(jnp.int32, (shard, shard), 0)
+    along = lax.broadcasted_iota(jnp.int32, (1, shard), 1)
+
+    def masked(values, head):
+        return jnp.where(keeps[head], values, jnp.zeros_like(values))
+
+    def after_a():
+        for slot in order[:2]:
+            folds[slot].end()
+        feed_line.launch(1)
+        feed_line.launch(2)
+        out_fold.two()
+
+    def after_b():
+        feed_line.take(1)
+        feed_line.forward(2)
+        out_fold.end()
+
+    def after_c():
+        for slot in order[2:]:
+            for copy in restay(slot):
+                copy.wait()
+            folds[slot].two(stays[slot % 2])
+
+    def after_d():
+        for slot in order[2:]:
+            folds[slot].end()
+        feed_line.launch(3)
+        feed_line.take(2)
+        feed_line.forward(3)
+        out_line.launch(1)
+        out_line.launch(2)
+        out_line.launch(3)
+
+    def back_step(step, carried):
+        pair, block = lax.div(step, PLANES), lax.rem(step, PLANES)
+        lanes = columns_of(pair)
+        start = pl.multiple_of(block * shard, shard)
+        own = pl.ds(start, shard)
+
+        @pl.when(block == 0)
+        def _():
+            total[...] = jnp.zeros_like(total)
+            for index in range(PLANES):
+                span = pl.ds(index * shard, shard)
+                turned = jnp.transpose(
+                    grad[span, lanes].astype(jnp.float32) * o_ref[span, lanes].astype(jnp.float32)
+                )
+                for head in range(2):
+                    inner[head : head + 1, span] = jnp.sum(
+                        turned[head * HD : head * HD + HD], axis=0, keepdims=True
+                    )
+
+        keys, values = k_ref[own, lanes], v_ref[own, lanes]
+        own_keys = [masked(keys, head) for head in range(2)]
+
+        def tile(index, sums, visible):
+            key_sum, value_sum = sums
+            span = pl.ds(pl.multiple_of(index * shard, shard), shard)
+            query_block, grad_block = q_ref[span, lanes], grad[span, lanes]
+            query_sum = total[span, :]
             for head in range(2):
-                inner[head : head + 1, span] = jnp.sum(
-                    turned[head * HD : head * HD + HD], axis=0, keepdims=True
+                query, out_grad = masked(query_block, head), masked(grad_block, head)
+                scores = tokens_dot(keys, query, 1, 1)
+                shares = jnp.where(
+                    visible, jnp.exp2(scores - log_ref[pair, head : head + 1, span]), 0.0
                 )
-                keep = (lane < HD) == (head == 0)
-                none = jnp.zeros((rows, 128), jnp.bfloat16)
-                queries[head, span, :] = jnp.where(keep, q_ref[span, :], none)
-                grads[head, span, :] = jnp.where(keep, grad[span, :], none)
-
-    start = pl.multiple_of(block * rows, rows)
-    keys, values = k_ref[pl.ds(start, rows), :], v_ref[pl.ds(start, rows), :]
-    keeps = [lane < HD, lane >= HD]
-    own_keys = [jnp.where(keep, keys, jnp.zeros_like(keys)) for keep in keeps]
-    seen = start + lax.broadcasted_iota(jnp.int32, (rows, rows), 0)
-    across = lax.broadcasted_iota(jnp.int32, (1, rows), 1)
-
-    def one(index, carried):
-        key_sum, value_sum = carried
-        at = pl.multiple_of(index * rows, rows)
-        span = pl.ds(at, rows)
-        visible = (seen >= begin_ref[0:1, span]) & (seen <= across + at)
-        query_sum = total[span, :]
-        for head in range(2):
-            query, out_grad = queries[head, span, :], grads[head, span, :]
-            scores = tokens_dot(keys, query, 1, 1)
-            shares = jnp.where(visible, jnp.exp2(scores - log_ref[0, head : head + 1, span]), 0.0)
-            share_grad = tokens_dot(values, out_grad, 1, 1)
-            score_grad = (shares * (share_grad - inner[head : head + 1, span])).astype(jnp.bfloat16)
-            value_sum = value_sum + tokens_dot(shares.astype(jnp.bfloat16), out_grad, 1, 0)
-            key_sum = key_sum + tokens_dot(score_grad, query, 1, 0)
-            query_sum = query_sum + tokens_dot(score_grad, own_keys[head], 0, 0)
-        total[span, :] = query_sum
-        return (key_sum, value_sum)
-
-    last = block + 1
-    for index in range(1, BLOCKS):
-        reaches = (index > block) & (low_ref[index] < start + rows)
-        last = last + jnp.where(reaches, 1, 0)
-    empty = jnp.zeros((rows, 128), jnp.float32)
-    key_sum, value_sum = lax.fori_loop(block, last, one, (empty, empty))
-    span = pl.ds(start, rows)
-    dk_ref[span, :] = turn(key_sum * (1 / LOG2E), cos_ref[span, :], sin_ref[span, :], False).astype(jnp.bfloat16)
-    dv_ref[span, :] = (0.5 * value_sum).astype(jnp.bfloat16)
-    first_ref[span, :] = 0.5 * value_sum
-    query_sum = total[span, :] * HD**-0.5
-    dq_ref[span, :] = turn(query_sum, cos_ref[span, :], sin_ref[span, :], False).astype(jnp.bfloat16)
-
-
-def flash_back(queries, keys, values, attended, incoming, logs, begin_row, cosine, sine_part, lows):
-    length, width = queries.shape
-    pairs = width // 128
-    column = pl.BlockSpec((length, 128), lambda p, j, low: (0, p))
-    table = pl.BlockSpec((length, 128), lambda p, j, low: (0, 0))
-    any_spec = pl.BlockSpec(memory_space=pl.ANY)
+                share_grad = tokens_dot(values, out_grad, 1, 1)
+                score_grad = (shares * (share_grad - inner[head : head + 1, span])).astype(jnp.bfloat16)
+                value_sum = value_sum + tokens_dot(shares.astype(jnp.bfloat16), out_grad, 1, 0)
+                key_sum = key_sum + tokens_dot(score_grad, query, 1, 0)
+                query_sum = query_sum + tokens_dot(score_grad, own_keys[head], 0, 0)
+            total[span, :] = query_sum
+            return (key_sum, value_sum)
+
+        empty = jnp.zeros((shard, 128), jnp.float32)
+        sums = tile(
+            block, (empty, empty), (down >= begin_ref[0:1, own] - start) & (down <= along)
+        )
+        key_sum, value_sum = lax.fori_loop(
+            block + 1,
+            PLANES,
+            lambda i, held: tile(
+                i,
+                held,
+                down >= begin_ref[0:1, pl.ds(pl.multiple_of(i * shard, shard), shard)] - start,
+            ),
+            sums,
+        )
+        cosine, sine_part = cos_ref[own, :], sin_ref[own, :]
+        made_ref[own, columns_of(pair)] = turn(
+            total[own, :] * HD**-0.5, cosine, sine_part, False
+        ).astype(jnp.bfloat16)
+        made_ref[own, columns_of(2 + pair)] = turn(
+            key_sum * (1 / LOG2E), cosine, sine_part, False
+        ).astype(jnp.bfloat16)
+        half_sum = 0.5 * value_sum
+        made_ref[own, columns_of(4 + pair)] = half_sum.astype(jnp.bfloat16)
+        first_ref[own, lanes] = half_sum
+        for when, pump in ((0, after_a), (3, after_b), (4, after_c), (6, after_d)):
+            pl.when(step == when)(pump)
+        return carried
+
+    lax.fori_loop(0, 2 * PLANES, back_step, 0)
+    for copy in late:
+        copy.wait()
+    small_ref[...] = small_in[...]
+
+    def input_back(index, carried):
+        block = jnp.where(depth < PLANES // 2, PLANES - 1 - index, index)
+        rows = pl.ds(pl.multiple_of(block * shard, shard), shard)
+        value = tokens_dot(made_ref[rows, :], weight_ref[pl.ds(0, 768), :], 1, 0)
+        partial[block] = value.astype(jnp.bfloat16)
+        gain = (
+            jnp.sum(value * n_ref[rows, :].astype(jnp.float32), axis=0, keepdims=True)
+            / gain_ref[0:1, :]
+        )
+        for piece in range(8):
+            small_ref[0, piece : piece + 1, :] += gain[:, piece * PIECE : piece * PIECE + PIECE]
+        return carried
+
+    input_back(0, 0)
+    line.launch(1)
+    lax.fori_loop(1, PLANES, input_back, 0)
+    line.launch(2)
+    line.launch(3)
+    out_line.take(1)
+    out_line.forward(2)
+
+    links.go(tiny, small_ref.at[0], small_got.at[0], tiny_to[0])
+    for copy in out_swaps:
+        copy.wait_send()
+    attn_made = out_made.at[pl.ds(0, 768), :]
+    for index in range(3):
+        rows = pl.ds(index * 256, 256)
+        attn_made[rows, :] = tokens_dot(made_ref[:, rows], n_ref[...], 0, 0).astype(jnp.bfloat16)
+    for i in range(4):
+        links.go(attn_swap + i, attn_made.at[:, others[i]], attn_core.at[i], core)
+    links.got(tiny, small_got.at[0])
+    small_ref[1] = small_ref[0] + small_got[0]
+    links.go(tiny + 1, small_ref.at[1], small_got.at[1], tiny_to[1])
+    for i in range(4):
+        links.got(attn_swap + i, attn_core.at[i])
+        add_into(attn_core.at[i], attn_made.at[:, sides[i]])
+    attn_fold.one()
+    line.take(1)
+    line.forward(2)
+    links.got(tiny + 1, small_got.at[1])
+    small_ref[2] = small_ref[1] + small_got[1]
+    links.go(tiny + 2, small_ref.at[2], small_got.at[2], tiny_to[2])
+    feed_line.take(3)
+    feed_line.total(feed_final.at[0], feed_total)
+    out_line.take(2)
+    out_line.forward(3)
+    attn_fold.two()
+    links.got(tiny + 2, small_got.at[2])
+    small_ref[3] = small_ref[2] + small_got[2]
+    small_place = small_got.at[3 + depth]
+    for step in range(1, PLANES):
+        links.go(tiny + 2 + step, small_ref.at[3], small_place, plane_to[step - 1])
+    small_got[3 + depth] = small_ref[3]
+    out_line.take(3)
+    out_line.total(out_final.at[pl.ds(pl.multiple_of(depth * 256, 256), 256), :], out_total)
+    line.take(2)
+    line.forward(3)
+    attn_fold.end()
+    attn_total[...] = attn_final[...].astype(jnp.float32)
+    for step in range(1, PLANES):
+        links.got(tiny + 2 + step, small_got.at[3 + plane_rows[step]])
+    small_ref[4] = small_got[3] + small_got[4] + small_got[5] + small_got[6]
+    line.take(3)
+    line.total(partial.at[depth], back_ref)
+    links.drain()
+
+
+def closing(made, low_ref, attended_own, heads, normed, weight, tables, incoming, logs, begin_row, gains, small):
+    length, width = heads[0].shape
+    rows = low_ref.shape[0]
+    count = made.shape[2]
+    low, full = jnp.bfloat16, jnp.float32
+    any_spec, vmem = pl.BlockSpec(memory_space=pl.ANY), pl.BlockSpec(memory_space=pltpu.VMEM)
+    shape = jax.ShapeDtypeStruct
     return pl.pallas_call(
-        flash_back_kernel,
-        grid_spec=pltpu.PrefetchScalarGridSpec(
-            num_scalar_prefetch=1,
-            grid=(pairs, BLOCKS),
-            in_specs=[column] * 4
-            + [any_spec] * 4
-            + [
-                pl.BlockSpec((1, 8, length), lambda p, j, low: (p, 0, 0)),
-                pl.BlockSpec((8, length), lambda p, j, low: (0, 0)),
-                table,
-                table,
-            ],
-            out_specs=[column] * 4,
-            scratch_shapes=[
-                pltpu.VMEM((length, 128), jnp.bfloat16),
-                pltpu.VMEM((8, length), jnp.float32),
-                pltpu.VMEM((length, 128), jnp.float32),
-                pltpu.VMEM((2, length, 128), jnp.bfloat16),
-                pltpu.VMEM((2, length, 128), jnp.bfloat16),
-                pltpu.SemaphoreType.DMA((PLANES,)),
-            ],
+        close_kernel,
+        in_specs=[any_spec] * 15 + [vmem] * 4,
+        out_specs=[vmem] * 6,
+        out_shape=[
+            shape((length, width), full),
+            shape((rows, D), full),
+            shape((count, PIECE), full),
+            shape((256, PIECE), full),
+            shape((768, PIECE), full),
+            shape((5, 24, PIECE), full),
+        ],
+        scratch_shapes=[pltpu.VMEM((length, width), low)] * 4
+        + [
+            pltpu.VMEM((length, D), low),
+            pltpu.VMEM((ATTN_ROWS, D), low),
+            pltpu.VMEM((length, 128), full),
+            pltpu.VMEM((length, 128), full),
+            pltpu.VMEM((length, width), low),
+            pltpu.VMEM((8, length), full),
+            pltpu.VMEM((length, 128), full),
+            pltpu.VMEM((length, 768), low),
+            pltpu.VMEM((2, 2, count, PIECE), low),
+            pltpu.VMEM((PLANES, 2, count, PIECE), low),
+            pltpu.VMEM((PLANES, count, PIECE), low),
+            pltpu.VMEM((2, PLANES - 1, count, PIECE), low),
+            pltpu.VMEM((D, D), low),
+            pltpu.VMEM((4, D, PIECE), low),
+            pltpu.VMEM((2, D, PIECE), low),
+            pltpu.VMEM((D, PIECE), low),
+            pltpu.VMEM((2, PLANES - 1, 256, PIECE), low),
+            pltpu.VMEM((4, 768, PIECE), low),
+            pltpu.VMEM((2, 768, PIECE), low),
+            pltpu.VMEM((768, PIECE), low),
+            pltpu.VMEM((PLANES, rows, D), low),
+            pltpu.VMEM((2, PLANES - 1, rows, D), low),
+            pltpu.VMEM((7, 24, PIECE), full),
+            pltpu.SemaphoreType.DMA((CLOSE_COPIES,)),
+            pltpu.SemaphoreType.DMA((CLOSE_COPIES,)),
+            pltpu.SemaphoreType.DMA((20,)),
+        ],
+        compiler_params=pltpu.CompilerParams(
+            vmem_limit_bytes=CLOSE_VMEM, collective_id=3, has_side_effects=True
         ),
-        out_shape=[jax.ShapeDtypeStruct((length, width), jnp.bfloat16)] * 3
-        + [jax.ShapeDtypeStruct((length, width), jnp.float32)],
-        compiler_params=pltpu.CompilerParams(vmem_limit_bytes=VMEM_LIMIT),
-        cost_estimate=cost(24 * length * length * width, 12 << 20),
-        name="flash_back",
-    )(lows, queries, keys, values, attended, *incoming, logs, begin_row, cosine, sine_part)
+        name="closing",
+    )(made, low_ref, attended_own, *heads, normed, weight, *tables, *incoming, logs, begin_row, gains, small)
 
 
 def middle_back_kernel(*refs):
@@ -1084,138 +1479,6 @@
         cost_estimate=cost(2 * rows * D * D, 12 << 20),
         name="middle_back",
     )(middle, grad, back, weight, gains)
-
-
-def grad_kernel(*refs):
-    wide, other_ref, out_ref, acc, sem = refs[:-4], refs[-4], refs[-3], refs[-2], refs[-1]
-    place = lax.axis_index("dp")
-    step = pl.program_id(0)
-    row = 0
-    for one in wide:
-        count = one.shape[1]
-        acc[pl.ds(row, count), :] = tokens_dot(one[...], other_ref[...], 0, 0).astype(jnp.bfloat16)
-        row += count
-    copies = []
-    for part in range(2):
-        at = jnp.bitwise_xor(place, 2 * step + part)
-        to = out_ref.at[lax.rem(at, 2), lax.div(at, 2)]
-        copies.append(pltpu.make_async_copy(acc.at[:, pl.ds(part * PIECE, PIECE)], to, sem.at[part]))
-    for copy in copies:
-        copy.start()
-    for copy in copies:
-        copy.wait()
-
-
-def weight_grad(wide, other, name):
-    rows = other.shape[0]
-    count = sum(one.shape[1] for one in wide)
-    return pl.pallas_call(
-        grad_kernel,
-        grid=(D // 256,),
-        in_specs=[pl.BlockSpec(one.shape, lambda i: (0, 0)) for one in wide]
-        + [pl.BlockSpec((rows, 256), lambda i: (0, i))],
-        out_specs=pl.BlockSpec(memory_space=pl.ANY),
-        out_shape=jax.ShapeDtypeStruct((2, 4, count, PIECE), jnp.bfloat16),
-        scratch_shapes=[pltpu.VMEM((count, 256), jnp.bfloat16), pltpu.SemaphoreType.DMA((2,))],
-        compiler_params=pltpu.CompilerParams(vmem_limit_bytes=VMEM_LIMIT),
-        cost_estimate=cost(2 * rows * D * count, 8 << 20),
-        name=name,
-    )(*wide, other)
-
-
-def input_back_kernel(dq_ref, dk_ref, dv_ref, weight_ref, n_ref, gain_ref, out_ref, gain_grad_ref):
-    @pl.when(pl.program_id(0) == 0)
-    def _():
-        gain_grad_ref[...] = jnp.zeros_like(gain_grad_ref)
-
-    incoming = (
-        tokens_dot(dq_ref[...], weight_ref[pl.ds(0, 256), :], 1, 0)
-        + tokens_dot(dk_ref[...], weight_ref[pl.ds(256, 256), :], 1, 0)
-        + tokens_dot(dv_ref[...], weight_ref[pl.ds(512, 256), :], 1, 0)
-    )
-    out_ref[0] = incoming.astype(jnp.bfloat16)
-    gain_grad_ref[0:1, :] += (
-        jnp.sum(incoming * n_ref[...].astype(jnp.float32), axis=0, keepdims=True) / gain_ref[0:1, :]
-    )
-
-
-def input_back(grads, weight, normed, gains):
-    length = normed.shape[0]
-    rows = length // PLANES
-    tile = pl.BlockSpec((rows, 256), lambda i: (i, 0))
-    whole = lambda *shape: pl.BlockSpec(shape, lambda i: (0,) * len(shape))
-    return pl.pallas_call(
-        input_back_kernel,
-        grid=(PLANES,),
-        in_specs=[tile] * 3
-        + [whole(ATTN_ROWS, D), pl.BlockSpec((rows, D), lambda i: (i, 0)), whole(16, D)],
-        out_specs=[pl.BlockSpec((1, rows, D), lambda i: (i, 0, 0)), whole(8, D)],
-        out_shape=[
-            jax.ShapeDtypeStruct((PLANES, rows, D), jnp.bfloat16),
-            jax.ShapeDtypeStruct((8, D), jnp.float32),
-        ],
-        compiler_params=pltpu.CompilerParams(vmem_limit_bytes=VMEM_LIMIT),
-        cost_estimate=cost(2 * length * D * 768, 12 << 20),
-        name="input_back",
-    )(*grads, weight, normed, gains)
-
-
-def permute(values, pairs):
-    return lax.ppermute(values, ("dp", "mp"), pairs)
-
-
-def swap(values, bit):
-    return permute(
-        values,
-        [
-            (place * PLANES + depth, (place ^ bit) * PLANES + depth)
-            for place in range(8)
-            for depth in range(PLANES)
-        ],
-    )
-
-
-def along(values, moves):
-    return permute(
-        values,
-        [(place * PLANES + a, place * PLANES + b) for place in range(8) for a, b in moves],
-    )
-
-
-def added(a, b):
-    return (a.astype(jnp.float32) + b.astype(jnp.float32)).astype(jnp.bfloat16)
-
-
-def fold(keep, send, bits):
-    got = swap(send, 1)
-    mine, theirs = added(keep[:2], got[:2]), added(keep[2:], got[2:])
-    got = swap(theirs, bits[0])
-    mine, theirs = added(mine[0], got[0]), added(mine[1], got[1])
-    return added(mine, swap(theirs, bits[1]))
-
-
-def fold_line(block, depth):
-    right = left = None
-    for step in range(1, PLANES):
-        there = block(jnp.minimum(depth + PLANES - step, PLANES - 1))
-        right = along(
-            there if right is None else added(there, right), [(a, a + 1) for a in range(step)]
-        )
-        there = block(jnp.maximum(depth - PLANES + step, 0))
-        left = along(
-            there if left is None else added(there, left),
-            [(a, a - 1) for a in range(PLANES - step, PLANES)],
-        )
-    return (
-        block(depth).astype(jnp.float32) + right.astype(jnp.float32) + left.astype(jnp.float32)
-    )
-
-
-def exchange(parts):
-    return [parts[0]] + [
-        along(parts[step], [(a, (a + step) % PLANES) for a in range(PLANES)])
-        for step in range(1, PLANES)
-    ]
 
 
 def fast_shards(
@@ -1298,59 +1561,34 @@
         first_values[0],
         begins[:, None],
     )
-    feed_out, normed_two_grad, feed_parts = feed(normed_two, out_cotangent, feed_all)
-    made = [fold(feed_parts[slot, 0], feed_parts[slot, 1], (4, 2)) for slot in range(PLANES)]
-    layer_output = (middle + feed_out).astype(low)[None]
+    normed_two_grad, layer_output, made = feed(normed_two, out_cotangent, middle, feed_all)
+    layer_output = layer_output[None]
     branch_low, middle_grad, gain_two, *out_grads = middle_back(
         middle, out_cotangent, normed_two_grad, out_weight, gains
     )
-    incoming = exchange(out_grads)
-    out_made = weight_grad([attended_own], branch_low, "output_grad")
-    out_made = fold(out_made[0], out_made[1], (4, 2))
-    feed_made = jnp.stack(made)
-
-    dq, dk, dv, values_grad = flash_back(
-        queries,
-        keys,
-        values,
-        attended,
-        incoming,
-        logs,
-        jnp.broadcast_to(begins[None], (8, length)),
-        cosine,
-        sine_part,
-        lows,
-    )
-    slot_table = jnp.array(
-        [[[s[2] for s in SLOTS[plane]].index(j) for j in range(PLANES)] for plane in range(PLANES)],
-        jnp.int32,
-    )[depth]
-    weight_total = fold_line(
-        lambda j: jnp.concatenate(
-            [
-                lax.dynamic_index_in_dim(feed_made, slot_table[j], 0, False),
-                lax.dynamic_slice_in_dim(out_made, j * 256, 256, 0),
-            ]
-        ),
-        depth,
-    )
-    input_partial, gain_one = input_back((dq, dk, dv), attn_weight, normed, gains)
-    attn_made = weight_grad([dq, dk, dv], normed, "input_grad")
-    normed_grad = fold_line(lambda j: lax.dynamic_index_in_dim(input_partial, j, 0, False), depth)
-    attn_total = fold(attn_made[0], attn_made[1], (4, 2)).astype(jnp.float32)
-
     small = jnp.concatenate(
         [
-            gain_one[0].reshape(8, PIECE),
+            jnp.zeros((8, PIECE), jnp.float32),
             gain_two[0].reshape(8, PIECE),
             jnp.broadcast_to(jnp.sum(squares[:2], axis=1)[:, None], (2, PIECE)),
             jnp.zeros((6, PIECE), jnp.float32),
         ]
     )
-    for bit in (1, 2, 4):
-        small = small + swap(small, bit)
-    for bit in (1, 2):
-        small = small + along(small, [(a, a ^ bit) for a in range(PLANES)])
+    values_grad, normed_grad, feed_total, out_total, attn_total, small = closing(
+        made,
+        branch_low,
+        attended_own,
+        (queries, keys, values, attended),
+        normed,
+        attn_weight,
+        (cosine, sine_part),
+        out_grads,
+        logs,
+        jnp.broadcast_to(begins[None], (8, length)),
+        gains,
+        jnp.broadcast_to(small[None], (5, 24, PIECE)),
+    )
+    small = small[4]
     value_norms = jnp.sqrt(small[16:18, 0] / (8 * length * D))
     gain_total = lax.dynamic_index_in_dim(small[:16].reshape(2, 8, PIECE), place, 1, False)
 
@@ -1359,9 +1597,8 @@
     input_part, _ = norm_back(hidden32, factor_one, gains[0], normed_grad)
     input_grad = (middle_grad + input_part)[None]
 
-    expand_total = weight_total[: 2 * ffs].reshape(2, ffs, PIECE).transpose(0, 2, 1)
-    reduce_total = weight_total[2 * ffs : 3 * ffs]
-    out_total = weight_total[3 * ffs :]
+    expand_total = feed_total[: 2 * ffs].reshape(2, ffs, PIECE).transpose(0, 2, 1)
+    reduce_total = feed_total[2 * ffs :]
     attn_total = attn_total.reshape(3, 256, PIECE).transpose(0, 2, 1)
     new_input = adamw(input_proj, attn_total, old_moment_input, old_square_input, D ** (-0.5), 0.1)
     new_output = adamw(

time: 630 us -> 475 us (0.75)
  waiting for transfers between devices: 161 us -> 0 us
  Pallas kernels: 315 us -> 427 us
  starting transfers between devices: 55.3 us -> 0 us
  other arithmetic: 55.9 us -> 29.9 us
  between operations: 15.4 us -> 1.4 us
  local copies, waits for them, and re-layouts: 20.2 us -> 10.1 us
    ppermute x38 -> x0, waiting for transfers between devices: 161 us -> none  [permute(): return lax.ppermute(values, ('dp', 'mp'), pairs)]
    pallas_call x5 -> x2, Pallas kernels: 111 us -> 223 us  [the longest x1 180 us: closing(): pl.pallas_call(close_kernel, in_specs=[any_spec] * 15 + [vmem] * 4, out_s...]
    ppermute x38 -> x0, starting transfers between devices: 55.3 us -> none  [permute(): return lax.ppermute(values, ('dp', 'mp'), pairs)]
    convert_element_type x18 -> x0, other arithmetic: 19 us -> none  [added(): return (a.astype(jnp.float32) + b.astype(jnp.float32)).astype(jnp.bfloat16)]
    squeeze x5 -> x1, local copies, waits for them, and re-layouts: 11.2 us -> 0.71 us  [fast_shards(): small = small[4]]
  transfers between devices with their start and end apart: 38 -> 0, of which waited for: 15 -> 0; matrix products, arithmetic and copies ran while one was open for 8% -> 0% of each run, Pallas kernels for 3% -> 0%
where the time goes in v2:
time: 475 us; the launch traced here: 468 us
  Pallas kernels  427 us (90%)
  other arithmetic  29.9 us (6%)
  local copies, waits for them, and re-layouts  10.1 us (2%)
    pallas_call x1, Pallas kernels, opening(): pl.pallas_call(open_kernel, in_specs=[any_spec] * 4 + [vmem] * 4, out_spe...  198 us
    pallas_call x1, Pallas kernels, closing(): pl.pallas_call(close_kernel, in_specs=[any_spec] * 15 + [vmem] * 4, out_s...  180 us
    pallas_call x1, Pallas kernels, feed(): pl.pallas_call(feed_kernel, in_specs=[vmem, vmem, vmem, any_spec], out_sp...  42.8 us

profile of v2, /device:TPU:0, one launch (start us, length us, event | category | flops | bytes accessed | tf_op | source)
XLA Modules:
  0.0 468.4 jit_solution(8874085663981096405)
XLA Ops:
  0.7 1.5 fusion.14
  2.1 4.6 compare_select_fusion.5
  6.7 3.7 fusion.9
  10.5 0.0 copy-start.17
  10.5 0.0 copy-start.2
  10.5 3.0 pad_maximum_fusion
  13.5 4.0 fusion.25
  17.5 1.3 copy.45.refs_7_
  18.8 0.0 copy-done.2
  18.9 0.8 pad_maximum_fusion.2.refs_3_
  19.8 0.0 copy-done.5
  19.8 0.2 copy.43
  20.0 0.1 pad.16.clone
  20.1 0.0 copy-done.18
  20.1 0.9 maximum_maximum_fusion.refs_1_
  20.9 0.6 convert_element_type.51.refs_2_
  21.6 197.5 %opening.1 = (bf16[2048,256]{1,0:T(8,128)(2,1)}, bf16[2048,256]{1,0:T(8,128)(2,1)}, bf16[2048,256]{1,0:T(8,128)(2,1)}, bf16[2048,256]{1,0:T(8,128)(2,1)}, bf16[2...) custom-call(bf16[512,1024]{1,0:T(8,128)(2,1)} %bitcast.35, ...), custom_call_target="tpu_custom_call" | custom-call | tf_op jit(solution)/shard_map/opening/pallas_call | solution.py:780
  219.1 42.8 %feed.1 = (f32[512,1024]{1,0:T(8,128)}, bf16[512,1024]{1,0:T(8,128)(2,1)}, bf16[4,4,2112,128]{3,2,1,0:T(8,128)(2,1)}) custom-call(bf16[512,1024]{1,0:T(8,128)(2,1)} %get-tuple-element.49.refs_0_, bf16[512,1024]{1,0:T(8,128)(2,1)} %bitcast.36, f32[512,1024]{1,0:T(8,128)} %get-tuple-element.50.refs_2_.refs_0_, bf16[4,8,2112,128]{3,2,1,0:T(8,128)(2,1)} %get-tuple-element.51.refs_3_), custom_call_target="tpu_custom_call" | custom-call | tf_op jit(solution)/shard_map/feed/pallas_call | solution.py:956
  261.9 6.5 %middle_back.1 = (bf16[512,1024]{1,0:T(8,128)(2,1)}, f32[512,1024]{1,0:T(8,128)}, f32[8,1024]{1,0:T(8,128)}, bf16[512,256]{1,0:T(8,128)(2,1)}, bf16[512,256]{1,0...) custom-call(f32[512,1024]{1,0:T(8,128)} %get-tuple-element.50.refs_2_.refs_0_, ...), custom_call_target="tpu_custom_call" | custom-call | flops 1073741824 | bytes 12582912 | tf_op jit(solution)/shard_map/middle_back/pallas_call | solution.py:1470
  268.4 0.8 slice.26
  269.1 0.8 slice_reduce_fusion
  270.0 0.1 pad.2.clone
  270.0 0.1 pad.3.clone
  270.1 0.1 maximum_maximum_fusion.1
  270.2 0.6 broadcast_in_dim.97.refs_18_
  270.8 0.6 broadcast_in_dim.93.refs_16_
  271.5 180.2 %closing.1 = (f32[2048,256]{1,0:T(8,128)}, f32[512,1024]{1,0:T(8,128)}, f32[2112,128]{1,0:T(8,128)}, f32[256,128]{1,0:T(8,128)}, f32[768,128]{1,0:T(8,128)}, /*index=5*/f32[5,24,128]{2,1,0:T(8,128)}) custom-call(bf16[4,4,2112,128]{3,2,1,0:T(8,128)(2,1)} %get-tuple-element.57.refs_0_, bf16[512,1024]{1,0:T(8,128)(2,1)} %get-tuple-element.58.refs_1_, ...), custom_call_target="tpu_custom_call" | custom-call | tf_op jit(solution)/shard_map/closing/pallas_call | solution.py:1396
  451.7 1.2 slice.31
  452.9 0.0 copy-start
  452.9 1.7 multiply_subtract_fusion
  454.6 0.9 slice.28
  455.5 0.0 copy-done
  455.5 0.1 copy-done.1
  455.6 0.6 fusion
  456.2 0.2 copy-done.3
  456.4 1.9 fusion.4
  458.3 0.2 copy.46
  458.5 0.0 copy-start.14
  458.5 0.0 copy-start.15
  458.5 1.2 multiply_subtract_fusion.1
  459.7 2.4 multiply_subtract_fusion.2
  462.2 0.8 multiply_subtract_fusion.3
  463.0 0.7 slice_bitcast_fusion.1
  463.7 0.6 multiply_subtract_fusion.4
  464.3 0.7 slice_bitcast_fusion
  465.0 0.6 fusion.19
  465.6 1.0 copy.49
  466.6 1.3 copy.50
  (44 shorter events, 0.2 us)
Async XLA Ops:
  10.5 3.0 copy-start.17
  10.5 8.4 %copy-start.2 = (f32[2,128,704]{1,2,0:T(8,128)S(1)}, f32[2,128,704]{1,2,0:T(8,128)}, u32[]{:S(2)}) copy-start(f32[2,128,704]{1,2,0:T(8,128)} %param.25) | copy-start | bytes 2162692
  13.5 5.4 %copy-start.6 = (f32[704,128]{1,0:T(8,128)S(1)}, f32[704,128]{1,0:T(8,128)}, u32[]{:S(2)}) copy-start(f32[704,128]{1,0:T(8,128)} %param.26) | copy-start | bytes 1081348
  13.5 6.3 %copy-start.5 = (f32[3,128,256]{2,1,0:T(8,128)S(1)}, f32[3,128,256]{2,1,0:T(8,128)}, u32[]{:S(2)}) copy-start(f32[3,128,256]{2,1,0:T(8,128)} %param.23) | copy-start | bytes 1179652
  18.9 1.2 copy-start.18
  18.9 2.1 copy-start.10
  271.5 181.4 %copy-start.8 = (f32[2,128,704]{1,2,0:T(8,128)S(1)}, f32[2,128,704]{1,2,0:T(8,128)}, u32[]{:S(2)}) copy-start(f32[2,128,704]{1,2,0:T(8,128)} %param.30) | copy-start | bytes 2162692
  271.5 181.4 %copy-start.9 = (f32[2,128,704]{1,2,0:T(8,128)S(1)}, f32[2,128,704]{1,2,0:T(8,128)}, u32[]{:S(2)}) copy-start(f32[2,128,704]{1,2,0:T(8,128)} %param.35) | copy-start | bytes 2162692
  452.9 2.6 copy-start
  452.9 2.7 copy-start.1
  454.6 1.8 copy-start.3
  456.4 1.9 copy-start.11
  456.4 2.1 copy-start.12
  456.4 2.1 copy-start.13
  458.5 3.7 copy-start.14
  458.5 3.7 copy-start.15
  458.5 3.7 copy-start.16
  459.7 4.0 copy-start.19
  459.7 4.0 copy-start.20
  459.7 5.9 %copy-start.7 = (bf16[512,1024]{1,0:T(8,128)(2,1)S(1)}, bf16[512,1024]{1,0:T(8,128)(2,1)}, u32[]{:S(2)}) copy-start(bf16[512,1024]{1,0:T(8,128)(2,1)} %get-tuple-element.52) | copy-start | bytes 3145732
  462.2 4.4 copy-start.4

commit v3 on v2

--- a/solution.py
+++ b/solution.py
@@ -19,8 +19,8 @@
 BLOCKS = 4
 ATTN_ROWS = 784
 VMEM_LIMIT = 56 << 20
-OPEN_COPIES = 66
-CLOSE_COPIES = 64
+OPEN_COPIES = 80
+CLOSE_COPIES = 80
 CLOSE_VMEM = 60 << 20
 
 
@@ -426,7 +426,7 @@
 
 class Links:
     def __init__(self, send, recv):
-        self.send, self.recv, self.count, self.started = send, recv, 0, []
+        self.send, self.recv, self.count, self.started, self.waited = send, recv, 0, [], []
         self.place, self.depth = lax.axis_index("dp"), lax.axis_index("mp")
 
     def number(self, count=1):
@@ -461,15 +461,18 @@
     def drain(self):
         for *parts, when in self.started:
             copy = self.copy(*parts)
+            for plane in [plane for number, plane in self.waited if number == parts[0]]:
+                when = when & (self.depth != plane)
             if when is None:
                 copy.wait_send()
             else:
                 pl.when(when)(copy.wait_send)
 
-    def greet(self):
+    def greet(self, planes=True):
         barrier = pltpu.get_barrier_semaphore()
         others = [(flip(self.place, bit), self.depth) for bit in (1, 2, 4)]
-        others += [(self.place, lax.rem(self.depth + step, PLANES)) for step in range(1, PLANES)]
+        if planes:
+            others += [(self.place, lax.rem(self.depth + step, PLANES)) for step in range(1, PLANES)]
         for other in others:
             pl.semaphore_signal(barrier, inc=1, device_id=other, device_id_type=MESH)
         pl.semaphore_wait(barrier, len(others))
@@ -477,48 +480,89 @@
 
 class Spread:
     def __init__(self, links, own, spot, bits):
-        self.links, self.own, self.spot, self.bits = links, own, spot, bits
+        self.links, self.own = links, own
         self.base = links.number(7)
         place = links.place
-        self.first, self.second = flip(place, bits[0]), flip(place, bits[1])
-        self.both = flip(self.first, bits[1])
-
-    def to(self, bit):
-        return (flip(self.links.place, bit), self.links.depth)
+        first, second = flip(place, bits[0]), flip(place, bits[1])
+        self.spots = [spot(piece) for piece in (place, first, second, flip(first, bits[1]))]
+        self.lands = [
+            spot(flip(piece, 1)) for piece in (place, first, second, flip(first, bits[1]))
+        ]
+        self.near, self.far, self.core = [
+            (flip(place, bit), links.depth) for bit in (bits[0], bits[1], 1)
+        ]
 
     def one(self):
-        links = self.links
-        links.go(self.base, self.own, self.spot(links.place), self.to(self.bits[0]))
+        self.links.go(self.base, self.own, self.spots[0], self.near)
 
     def two(self):
-        links = self.links
-        to = self.to(self.bits[1])
-        links.go(self.base + 1, self.own, self.spot(links.place), to)
-        links.got(self.base, self.spot(self.first))
-        links.go(self.base + 2, self.spot(self.first), self.spot(self.first), to)
+        links, spots = self.links, self.spots
+        links.go(self.base + 1, self.own, spots[0], self.far)
+        links.got(self.base, spots[1])
+        links.go(self.base + 2, spots[1], spots[1], self.far)
 
     def three(self):
-        links = self.links
-        to = self.to(1)
-        links.go(self.base + 3, self.own, self.spot(links.place), to)
-        links.go(self.base + 4, self.spot(self.first), self.spot(self.first), to)
-        links.got(self.base + 1, self.spot(self.second))
-        links.go(self.base + 5, self.spot(self.second), self.spot(self.second), to)
-        links.got(self.base + 2, self.spot(self.both))
-        links.go(self.base + 6, self.spot(self.both), self.spot(self.both), to)
+        links, spots = self.links, self.spots
+        links.go(self.base + 3, self.own, spots[0], self.core)
+        links.go(self.base + 4, spots[1], spots[1], self.core)
+        links.got(self.base + 1, spots[2])
+        links.go(self.base + 5, spots[2], spots[2], self.core)
+        links.got(self.base + 2, spots[3])
+        links.go(self.base + 6, spots[3], spots[3], self.core)
 
     def end(self):
-        links = self.links
-        for index, piece in enumerate((links.place, self.first, self.second, self.both)):
-            links.got(self.base + 3 + index, self.spot(flip(piece, 1)))
+        for index, land in enumerate(self.lands):
+            self.links.got(self.base + 3 + index, land)
+
+
+class Halves:
+    def __init__(self, parts):
+        self.parts = parts
+
+    def one(self):
+        for part in self.parts:
+            part.one()
+
+    def two(self, *given):
+        for index, part in enumerate(self.parts):
+            part.two(*[one[index] for one in given])
+
+    def three(self):
+        for part in self.parts:
+            part.three()
+
+    def end(self):
+        for part in self.parts:
+            part.end()
+
+
+def half_of(ref, half):
+    rows = ref.shape[-2] // 2
+    lead = (slice(None),) * (len(ref.shape) - 2)
+    return ref.at[(*lead, pl.ds(half * rows, rows), slice(None))]
+
+
+def halved_spread(links, own, spot):
+    return Halves(
+        [
+            Spread(
+                links,
+                half_of(own, half),
+                lambda piece, half=half: half_of(spot(piece), half),
+                ((2, 4), (4, 2))[half],
+            )
+            for half in range(2)
+        ]
+    )
 
 
 class Relay:
     def __init__(self, links, own, put):
         self.links, self.own, self.put = links, own, put
         self.base = links.number(2 * (PLANES - 1))
-
-    def send(self, hop):
+        self.waited = links.waited
+
+    def send(self, hop, only=None):
         links, depth = self.links, self.links.depth
         for way in range(2):
             to = depth + (1 if way else -1)
@@ -527,6 +571,8 @@
                 if way
                 else (depth <= PLANES - hop) & (depth > 0)
             )
+            if only is not None:
+                when = when & (depth == only[way])
             source = self.own if hop == 1 else self.put(depth, way, hop - 1)
             links.go(
                 self.base + 2 * (hop - 1) + way,
@@ -536,11 +582,22 @@
                 when,
             )
 
-    def take(self, hop):
+    def take(self, hop, only=None):
         links, depth = self.links, self.links.depth
         for way in range(2):
             when = depth >= hop if way else depth + hop < PLANES
+            if only is not None:
+                when = when & (depth == only[way])
             links.got(self.base + 2 * (hop - 1) + way, self.put(depth, way, hop), when)
+
+    def left(self, hop, only):
+        links, depth = self.links, self.links.depth
+        for way in range(2):
+            source = self.own if hop == 1 else self.put(depth, way, hop - 1)
+            to = (links.place, jnp.clip(depth + (1 if way else -1), 0, PLANES - 1))
+            copy = links.copy(self.base + 2 * (hop - 1) + way, source, source, to)
+            pl.when(depth == only[way])(copy.wait_send)
+            self.waited.append((self.base + 2 * (hop - 1) + way, only[way]))
 
 
 def open_kernel(*refs):
@@ -575,13 +632,12 @@
         links, out_ref.at[:, columns_of(place)], lambda piece: out_ref.at[:, columns_of(piece)], (2, 4)
     )
     slots = [
-        Spread(
+        halved_spread(
             links,
             feed_piece if slot == 0 else feed_all.at[slot, place],
             lambda piece, slot=slot: feed_all.at[slot, piece],
-            (2, 4) if slot % 2 == 0 else (4, 2),
-        )
-        for slot in range(PLANES)
+        )
+        for slot in range(PLANES - 1)
     ]
     across = links.number(PLANES)
 
@@ -632,22 +688,31 @@
 
         lax.fori_loop(0, 2, one, 0)
 
+    ends, inner = (PLANES - 1, 0), (PLANES - 2, 1)
     project(depth)
     wide.take(1)
     wide.send(2)
+    feeds.send(1, ends)
     thin.take(1)
     thin.send(2)
     slots[0].two()
     project_hop(1)
     wide.take(2)
     wide.send(3)
+    feeds.take(1, inner)
+    feeds.send(1, inner)
+    feeds.send(2, inner)
     thin.take(2)
     thin.send(3)
     project_hop(2)
     slots[0].three()
     wide.take(3)
+    wide.left(3, (1, PLANES - 2))
+    feeds.take(1, (1, PLANES - 2))
+    feeds.take(2, (1, PLANES - 2))
+    for hop in range(1, PLANES):
+        feeds.send(hop, (1, PLANES - 2))
     thin.take(3)
-    feeds.send(1)
     outs.one()
     project_hop(3)
     store(n_ref, n_out)
@@ -706,43 +771,36 @@
         rows = pl.ds(pl.multiple_of(block * shard, shard), shard)
         return links.copy(across + step, o_ref.at[rows, :], own_columns, (place, block))
 
-    def flash(step):
-        block = lax.rem(depth + step, PLANES)
-
-        def one(pair, carried):
-            flash_pair(block, pair)
-            return carried
-
-        lax.fori_loop(0, 2, one, 0)
-
-    flash(3)
-    hand(3).start()
-    feeds.take(1)
-    feeds.send(2)
-    slots[1].one()
-    outs.two()
-    slots[0].end()
-
-    def middle_steps(index, carried):
-        step = 2 - index
-        flash(step)
-        hand(step).start()
+    near = (0, PLANES - 1)
+
+    def pump_a():
+        feeds.take(1, near)
+        slots[1].one()
+        outs.two()
+
+    def pump_b():
+        slots[1].two()
+        slots[0].end()
+
+    def pump_c():
+        feeds.take(2, near)
+        slots[2].one()
+        outs.three()
+
+    pumps = ((0, pump_a), (1, pump_b), (2, pump_c), (4, slots[1].three), (5, slots[2].two))
+
+    def flash(index, carried):
+        step, pair = PLANES - 1 - lax.div(index, 2), lax.rem(index, 2)
+        flash_pair(lax.rem(depth + step, PLANES), pair)
+        pl.when((pair == 1) & (step > 0))(lambda: hand(step).start())
+        for when, pump in pumps:
+            pl.when(index == when)(pump)
         return carried
 
-    lax.fori_loop(0, 2, middle_steps, 0)
-    feeds.take(2)
-    feeds.send(3)
-    slots[1].two()
-    slots[2].one()
-    outs.three()
-    flash(0)
+    lax.fori_loop(0, 2 * PLANES, flash, 0)
     own_rows = pl.ds(pl.multiple_of(depth * shard, shard), shard)
     attended_ref[:, columns_of(depth, 256)] = o_ref[own_rows, :]
     store(o_ref, o_out)
-    feeds.take(3)
-    slots[2].two()
-    slots[3].one()
-    slots[1].three()
     outs.end()
     store(out_ref, out_weight_out)
     for step in range(1, PLANES):
@@ -759,10 +817,8 @@
         normed_ref[rows, :] = (middle * factor * gain_ref[1:2, :]).astype(jnp.bfloat16)
     slots[2].three()
     slots[1].end()
-    slots[3].two()
+    feeds.take(3)
     slots[2].end()
-    slots[3].three()
-    slots[3].end()
     for step in range(1, PLANES):
         hand(step).wait_send()
     links.drain()
@@ -820,8 +876,9 @@
 def feed_kernel(*refs):
     normed_ref, grad_ref, middle_ref, pieces = refs[:4]
     back_ref, out_ref, made_out = refs[4:7]
-    fed, weight, mine, theirs, made, halves, other_halves, send, recv, sem, out_sem = refs[7:]
+    fed, weight, mine, theirs, made, halves, other_halves, send, recv, sem, out_sem, last_sem = refs[7:]
     links = Links(send, recv)
+    place = links.place
     core = (flip(links.place, 1), links.depth)
     mine_first, theirs_first = lax.rem(links.place, 2), 1 - lax.rem(links.place, 2)
     count = weight.shape[1] // 3
@@ -849,9 +906,12 @@
 
     for copy in load(0, 0):
         copy.start()
-    barrier = pltpu.get_barrier_semaphore()
-    pl.semaphore_signal(barrier, inc=1, device_id=core, device_id_type=MESH)
-    pl.semaphore_wait(barrier, 1)
+    far = pieces.at[PLANES - 1, place]
+    last = halved_spread(links, far, lambda piece: weight.at[2, :, columns_of(piece)])
+    last_own = pltpu.make_async_copy(far, weight.at[2, :, columns_of(place)], last_sem)
+    last_own.start()
+    links.greet(planes=False)
+    last.one()
     base = links.number(8)
     for index, ref in enumerate((normed_ref, grad_ref)):
         for piece in range(4):
@@ -876,14 +936,23 @@
 
     def forward(slot):
         now = lax.rem(slot, 2)
-        for copy in load(slot, now):
-            copy.wait()
-
-        @pl.when(slot + 1 < PLANES)
+        held = jnp.where(slot == PLANES - 1, 2, now)
+
+        @pl.when(slot < PLANES - 1)
+        def _():
+            for copy in load(slot, now):
+                copy.wait()
+
+        @pl.when(slot + 2 < PLANES)
         def _():
             for copy in load(slot + 1, 1 - now):
                 copy.start()
 
+        @pl.when(slot == PLANES - 1)
+        def _():
+            last_own.wait()
+            last.end()
+
         @pl.when(slot >= 2)
         def _():
             hand(slot - 2).wait_send()
@@ -891,9 +960,9 @@
         for tile in range(2):
             at = pl.ds(tile * half, half)
             normed, grad = normed_ref[at, :], grad_ref[at, :]
-            gates = tokens_dot(weight[now, spans[0], :], normed, 1, 1)
-            ups = tokens_dot(weight[now, spans[1], :], normed, 1, 1)
-            backs = tokens_dot(weight[now, spans[2], :], grad, 1, 1)
+            gates = tokens_dot(weight[held, spans[0], :], normed, 1, 1)
+            ups = tokens_dot(weight[held, spans[1], :], normed, 1, 1)
+            backs = tokens_dot(weight[held, spans[2], :], grad, 1, 1)
             sig = jax.nn.sigmoid(gates)
             active = gates * sig
             mine[now, 2, :, at] = (active * ups).astype(jnp.bfloat16)
@@ -903,10 +972,10 @@
 
         def columns(tile, carried):
             lanes = columns_of(tile, 256)
-            fed[:, lanes] += tokens_dot(mine[now, 2], weight[now, spans[2], lanes], 0, 0)
+            fed[:, lanes] += tokens_dot(mine[now, 2], weight[held, spans[2], lanes], 0, 0)
             back_ref[:, lanes] += tokens_dot(
-                mine[now, 0], weight[now, spans[0], lanes], 0, 0
-            ) + tokens_dot(mine[now, 1], weight[now, spans[1], lanes], 0, 0)
+                mine[now, 0], weight[held, spans[0], lanes], 0, 0
+            ) + tokens_dot(mine[now, 1], weight[held, spans[1], lanes], 0, 0)
             return carried
 
         lax.fori_loop(0, D // 256, columns, 0)
@@ -936,6 +1005,8 @@
 
     def one(step, carried):
         pl.when(step < PLANES)(lambda: forward(step))
+        pl.when(step == 0)(last.two)
+        pl.when(step == 2)(last.three)
         pl.when(step >= 1)(lambda: backward(step - 1))
         return carried
 
@@ -964,16 +1035,17 @@
         ],
         scratch_shapes=[
             pltpu.VMEM((rows, D), jnp.float32),
-            pltpu.VMEM((2, count, D), low),
+            pltpu.VMEM((3, count, D), low),
             pltpu.VMEM((2, 3, count // 3, rows), low),
             pltpu.VMEM((PLANES, 3, count // 3, rows), low),
             pltpu.VMEM((2, count, 4 * PIECE), low),
             pltpu.VMEM((2, rows, 4 * PIECE), low),
             pltpu.VMEM((2, rows, 4 * PIECE), low),
-            pltpu.SemaphoreType.DMA((12,)),
-            pltpu.SemaphoreType.DMA((12,)),
+            pltpu.SemaphoreType.DMA((26,)),
+            pltpu.SemaphoreType.DMA((26,)),
             pltpu.SemaphoreType.DMA((2, 8)),
             pltpu.SemaphoreType.DMA((2, 4)),
+            pltpu.SemaphoreType.DMA,
         ],
         compiler_params=pltpu.CompilerParams(
             vmem_limit_bytes=VMEM_LIMIT, collective_id=2, has_side_effects=True
@@ -984,7 +1056,7 @@
 
 def add_into(target, source):
     rows = target.shape[0]
-    chunk = next(c for c in (352, 256, rows) if rows % c == 0)
+    chunk = next(c for c in (352, 256, rows) if rows % c == 0 and c <= rows)
 
     def one(index, carried):
         span = pl.ds(pl.multiple_of(index * chunk, chunk), chunk)
@@ -1125,18 +1197,29 @@
         return copy
 
     order = (3, 2, 1, 0)
+
+    def halved_fold(whole, first, final):
+        return Halves(
+            [
+                Fold(
+                    links,
+                    lambda i, half=half: half_of(whole(i), half),
+                    half_of(first, half),
+                    half_of(final, half),
+                    ((1, 2), (2, 1))[half],
+                )
+                for half in range(2)
+            ]
+        )
+
     folds = {
-        slot: Fold(
-            links,
-            lambda i, slot=slot: made.at[slot, i],
-            feed_first.at[slot],
-            feed_final.at[slot],
-            (1, 2) if slot % 2 else (2, 1),
+        slot: halved_fold(
+            lambda i, slot=slot: made.at[slot, i], feed_first.at[slot], feed_final.at[slot]
         )
         for slot in order
     }
-    out_fold = Fold(links, lambda i: out_core.at[i], out_first, out_final, (1, 2))
-    attn_fold = Fold(links, lambda i: attn_core.at[i], attn_first, attn_final, (1, 2))
+    out_fold = halved_fold(lambda i: out_core.at[i], out_first, out_final)
+    attn_fold = halved_fold(lambda i: attn_core.at[i], attn_first, attn_final)
 
     def slot_holding(block):
         found = 0
@@ -1153,9 +1236,24 @@
     out_swap, attn_swap = links.number(4), links.number(4)
     sides = [columns_of(2 * i + parity) for i in range(4)]
     others = [columns_of(2 * i + 1 - parity) for i in range(4)]
-    across = links.number(PLANES)
+    across = links.number(2 * PLANES)
     tiny = links.number(6)
-    stays = [[stay.at[index, m] for m in range(2)] for index in range(2)]
+    stays = [
+        [[half_of(stay.at[index, m], half) for m in range(2)] for half in range(2)] for index in range(2)
+    ]
+    stay_sems = [[[16 + 4 * index + 2 * half + m for m in range(2)] for half in range(2)] for index in range(2)]
+
+    def restay(slot):
+        return [
+            pltpu.make_async_copy(
+                folds[slot].parts[half].stay[m],
+                stays[slot % 2][half][m],
+                local.at[stay_sems[slot % 2][half][m]],
+            )
+            for half in range(2)
+            for m in range(2)
+        ]
+
     tiny_to = [core, (flip(place, 2), depth), (flip(place, 4), depth)]
     plane_to = [(place, lax.rem(depth + step, PLANES)) for step in range(1, PLANES)]
     plane_rows = [lax.rem(depth - step + PLANES, PLANES) for step in range(PLANES)]
@@ -1163,18 +1261,24 @@
     attended_ref, low_ref = partial.at[0], partial.at[1]
     first_loads = [load(attended_in, attended_ref), load(low_in, low_ref)]
     for slot in order[:2]:
-        for m in range(2):
-            load(folds[slot].stay[m], stays[slot % 2][m])
+        for copy in restay(slot):
+            copy.start()
     q_loads = [load(source, target) for source, target in ((q_in, q_ref), (k_in, k_ref), (v_in, v_ref), (o_in, o_ref), (cos_in, cos_ref), (sin_in, sin_ref))]
     own_rows = pl.ds(pl.multiple_of(depth * shard, shard), shard)
     q_loads.append(load(incoming[0], grad.at[own_rows, :]))
     late = [load(n_in, n_ref), load(weight_in, weight_ref)]
 
     links.greet()
-    for step in range(1, PLANES):
-        links.go(across + step, incoming[step], grad.at[own_rows, :], plane_to[step - 1])
-    for slot in order[:2]:
-        folds[slot].one()
+    for pair in range(2):
+        lanes = pl.ds(pair * 128, 128)
+        for step in range(1, PLANES):
+            links.go(
+                across + 4 * pair + step,
+                incoming[step].at[:, lanes],
+                grad.at[own_rows, lanes],
+                plane_to[step - 1],
+            )
+    folds[3].one()
 
     for copy in first_loads:
         copy.wait()
@@ -1187,27 +1291,29 @@
     for i in range(4):
         links.got(out_swap + i, out_core.at[i])
         add_into(out_core.at[i], out_made.at[:, sides[i]])
-    out_fold.one()
-
-    def restay(slot):
-        copies = [
-            pltpu.make_async_copy(folds[slot].stay[m], stays[slot % 2][m], local.at[16 + 2 * (slot % 2) + m])
-            for m in range(2)
-        ]
-        return copies
-
-    for copy in loads[2:6]:
-        copy.wait()
     for copy in q_loads:
         copy.wait()
-    for slot in order[:2]:
+
+    def fold_two(slot):
+        for copy in restay(slot):
+            copy.wait()
         folds[slot].two(stays[slot % 2])
-    for slot in order[2:]:
-        folds[slot].one()
-        for copy in restay(slot):
-            copy.start()
-    for step in range(1, PLANES):
-        links.got(across + step, grad.at[pl.ds(pl.multiple_of(plane_rows[step] * shard, shard), shard), :])
+
+    fold_two(3)
+    folds[2].one()
+    grad_rows = [
+        [
+            grad.at[pl.ds(pl.multiple_of(plane_rows[step] * shard, shard), shard), pl.ds(pair * 128, 128)]
+            for step in range(PLANES)
+        ]
+        for pair in range(2)
+    ]
+
+    def take_grads(pair):
+        for step in range(1, PLANES):
+            links.got(across + 4 * pair + step, grad_rows[pair][step])
+
+    take_grads(0)
 
     lane = lax.broadcasted_iota(jnp.int32, (shard, 128), 1)
     keeps = [lane < HD, lane >= HD]
@@ -1218,32 +1324,38 @@
         return jnp.where(keeps[head], values, jnp.zeros_like(values))
 
     def after_a():
-        for slot in order[:2]:
-            folds[slot].end()
+        folds[3].end()
         feed_line.launch(1)
+        out_fold.one()
+
+    def after_b():
+        fold_two(2)
+        folds[1].one()
+        for copy in restay(1):
+            copy.start()
+
+    def after_c():
+        folds[2].end()
         feed_line.launch(2)
-        out_fold.two()
-
-    def after_b():
         feed_line.take(1)
         feed_line.forward(2)
+        out_fold.two()
+        take_grads(1)
+
+    def after_d():
+        fold_two(1)
+        folds[0].one()
+        for copy in restay(0):
+            copy.start()
         out_fold.end()
 
-    def after_c():
-        for slot in order[2:]:
-            for copy in restay(slot):
-                copy.wait()
-            folds[slot].two(stays[slot % 2])
-
-    def after_d():
-        for slot in order[2:]:
-            folds[slot].end()
+    def after_e():
+        folds[1].end()
         feed_line.launch(3)
         feed_line.take(2)
         feed_line.forward(3)
-        out_line.launch(1)
-        out_line.launch(2)
-        out_line.launch(3)
+        for step in range(1, PLANES):
+            out_line.launch(step)
 
     def back_step(step, carried):
         pair, block = lax.div(step, PLANES), lax.rem(step, PLANES)
@@ -1310,7 +1422,7 @@
         half_sum = 0.5 * value_sum
         made_ref[own, columns_of(4 + pair)] = half_sum.astype(jnp.bfloat16)
         first_ref[own, lanes] = half_sum
-        for when, pump in ((0, after_a), (3, after_b), (4, after_c), (6, after_d)):
+        for when, pump in ((0, after_a), (1, after_b), (3, after_c), (5, after_d), (7, after_e)):
             pl.when(step == when)(pump)
         return carried
 
@@ -1337,6 +1449,7 @@
     lax.fori_loop(1, PLANES, input_back, 0)
     line.launch(2)
     line.launch(3)
+    fold_two(0)
     out_line.take(1)
     out_line.forward(2)
 
@@ -1361,6 +1474,7 @@
     links.got(tiny + 1, small_got.at[1])
     small_ref[2] = small_ref[1] + small_got[1]
     links.go(tiny + 2, small_ref.at[2], small_got.at[2], tiny_to[2])
+    folds[0].end()
     feed_line.take(3)
     feed_line.total(feed_final.at[0], feed_total)
     out_line.take(2)
@@ -1432,7 +1546,7 @@
             pltpu.VMEM((7, 24, PIECE), full),
             pltpu.SemaphoreType.DMA((CLOSE_COPIES,)),
             pltpu.SemaphoreType.DMA((CLOSE_COPIES,)),
-            pltpu.SemaphoreType.DMA((20,)),
+            pltpu.SemaphoreType.DMA((24,)),
         ],
         compiler_params=pltpu.CompilerParams(
             vmem_limit_bytes=CLOSE_VMEM, collective_id=3, has_side_effects=True

time: 475 us -> 412 us (0.87)
  Pallas kernels: 427 us -> 364 us
    pallas_call x1, Pallas kernels: 198 us -> 147 us  [opening(): pl.pallas_call(open_kernel, in_specs=[any_spec] * 4 + [vmem] * 4, out_spe...]
    pallas_call x1, Pallas kernels: 180 us -> 165 us  [closing(): pl.pallas_call(close_kernel, in_specs=[any_spec] * 15 + [vmem] * 4, out_s...]
where the time goes in v3:
time: 412 us; the launch traced here: 405 us
  Pallas kernels  364 us (88%)
  other arithmetic  29.9 us (7%)
  local copies, waits for them, and re-layouts  10.1 us (2%)
    pallas_call x1, Pallas kernels, closing(): pl.pallas_call(close_kernel, in_specs=[any_spec] * 15 + [vmem] * 4, out_s...  165 us
    pallas_call x1, Pallas kernels, opening(): pl.pallas_call(open_kernel, in_specs=[any_spec] * 4 + [vmem] * 4, out_spe...  147 us
    pallas_call x1, Pallas kernels, feed(): pl.pallas_call(feed_kernel, in_specs=[vmem, vmem, vmem, any_spec], out_sp...  46 us
    select_n x2, other arithmetic, fast_shards(): begins = jnp.where(seg_row == number, start, begins)  8.58 us

profile of v3, /device:TPU:0, one launch (start us, length us, event | category | flops | bytes accessed | tf_op | source)
XLA Modules:
  0.0 405.1 jit_solution(17733860986655435085)
XLA Ops:
  0.7 1.5 fusion.14
  2.1 4.6 %compare_select_fusion.5 = s32[1,2048]{1,0:T(1,128)S(1)} fusion(s32[1,2048]{1,0:T(1,128)} %param.20, s32[]{:T(128)} %get-tuple-element.84, s32[]{:T(128)} %get-tuple-element.82, s32[]{:T(128)} %get-tuple-element.86, s32[]{:T(128)} %get-tuple-element.85, s32[]{:T(128)} %get-tuple-element.83, s32[]{:T(128)} %get-tuple-element.81), kind=kLoop, calls=%fused_computation.44 | loop fusion | flops 24576 | bytes 16408 | tf_op jit(solution)/shard_map/jit(_where)/select_n | solution.py:1644
  6.7 3.7 fusion.9
  10.5 0.0 copy-start.17
  10.5 0.0 copy-start.2
  10.5 3.0 pad_maximum_fusion
  13.5 4.0 fusion.25
  17.5 1.3 copy.45.refs_7_
  18.8 0.0 copy-done.2
  18.9 0.8 pad_maximum_fusion.2.refs_3_
  19.8 0.2 copy.43
  20.0 0.1 pad.16.clone
  20.1 0.0 copy-done.18
  20.1 0.9 maximum_maximum_fusion.refs_1_
  20.9 0.6 convert_element_type.51.refs_2_
  21.6 146.6 %opening.1 = (bf16[2048,256]{1,0:T(8,128)(2,1)}, bf16[2048,256]{1,0:T(8,128)(2,1)}, bf16[2048,256]{1,0:T(8,128)(2,1)}, bf16[2048,256]{1,0:T(8,128)(2,1)}, bf16[2...) custom-call(bf16[512,1024]{1,0:T(8,128)(2,1)} %bitcast.35, ...), custom_call_target="tpu_custom_call" | custom-call | tf_op jit(solution)/shard_map/opening/pallas_call | solution.py:836
  168.2 46.0 %feed.1 = (f32[512,1024]{1,0:T(8,128)}, bf16[512,1024]{1,0:T(8,128)(2,1)}, bf16[4,4,2112,128]{3,2,1,0:T(8,128)(2,1)}) custom-call(bf16[512,1024]{1,0:T(8,128)(2,1)} %get-tuple-element.49.refs_0_, bf16[512,1024]{1,0:T(8,128)(2,1)} %bitcast.36, f32[512,1024]{1,0:T(8,128)} %get-tuple-element.50.refs_2_.refs_0_, bf16[4,8,2112,128]{3,2,1,0:T(8,128)(2,1)} %get-tuple-element.51.refs_3_), custom_call_target="tpu_custom_call" | custom-call | tf_op jit(solution)/shard_map/feed/pallas_call | solution.py:1027
  214.2 6.5 %middle_back.1 = (bf16[512,1024]{1,0:T(8,128)(2,1)}, f32[512,1024]{1,0:T(8,128)}, f32[8,1024]{1,0:T(8,128)}, bf16[512,256]{1,0:T(8,128)(2,1)}, bf16[512,256]{1,0...) custom-call(f32[512,1024]{1,0:T(8,128)} %get-tuple-element.50.refs_2_.refs_0_, ...), custom_call_target="tpu_custom_call" | custom-call | flops 1073741824 | bytes 12582912 | tf_op jit(solution)/shard_map/middle_back/pallas_call | solution.py:1584
  220.7 0.8 slice.26
  221.5 0.8 slice_reduce_fusion
  222.3 0.1 pad.2.clone
  222.4 0.1 pad.3.clone
  222.5 0.1 maximum_maximum_fusion.1
  222.5 0.6 broadcast_in_dim.97.refs_18_
  223.2 0.6 broadcast_in_dim.93.refs_16_
  223.8 164.8 %closing.1 = (f32[2048,256]{1,0:T(8,128)}, f32[512,1024]{1,0:T(8,128)}, f32[2112,128]{1,0:T(8,128)}, f32[256,128]{1,0:T(8,128)}, f32[768,128]{1,0:T(8,128)}, /*index=5*/f32[5,24,128]{2,1,0:T(8,128)}) custom-call(bf16[4,4,2112,128]{3,2,1,0:T(8,128)(2,1)} %get-tuple-element.57.refs_0_, bf16[512,1024]{1,0:T(8,128)(2,1)} %get-tuple-element.58.refs_1_, ...), custom_call_target="tpu_custom_call" | custom-call | tf_op jit(solution)/shard_map/closing/pallas_call | solution.py:1510
  388.7 1.2 slice.31
  389.8 0.0 copy-start
  389.9 1.7 multiply_subtract_fusion
  391.6 0.9 slice.28
  392.5 0.1 copy-done.1
  392.5 0.6 fusion
  393.1 0.2 copy-done.3
  393.3 1.9 fusion.4
  395.2 0.0 copy-done.11
  395.2 0.2 copy.46
  395.4 0.0 copy-start.14
  395.4 0.0 copy-start.15
  395.5 1.2 multiply_subtract_fusion.1
  396.7 2.4 multiply_subtract_fusion.2
  399.1 0.0 copy-done.15
  399.1 0.8 multiply_subtract_fusion.3
  399.9 0.7 slice_bitcast_fusion.1
  400.6 0.6 multiply_subtract_fusion.4
  401.2 0.7 slice_bitcast_fusion
  401.9 0.6 fusion.19
  402.6 1.0 copy.49
  403.6 1.3 copy.50
  (44 shorter events, 0.2 us)
Async XLA Ops:
  10.5 3.0 copy-start.17
  10.5 8.4 %copy-start.2 = (f32[2,128,704]{1,2,0:T(8,128)S(1)}, f32[2,128,704]{1,2,0:T(8,128)}, u32[]{:S(2)}) copy-start(f32[2,128,704]{1,2,0:T(8,128)} %param.25) | copy-start | bytes 2162692
  13.5 5.4 %copy-start.6 = (f32[704,128]{1,0:T(8,128)S(1)}, f32[704,128]{1,0:T(8,128)}, u32[]{:S(2)}) copy-start(f32[704,128]{1,0:T(8,128)} %param.26) | copy-start | bytes 1081348
  13.5 6.3 %copy-start.5 = (f32[3,128,256]{2,1,0:T(8,128)S(1)}, f32[3,128,256]{2,1,0:T(8,128)}, u32[]{:S(2)}) copy-start(f32[3,128,256]{2,1,0:T(8,128)} %param.23) | copy-start | bytes 1179652
  18.9 1.2 copy-start.18
  18.9 2.1 copy-start.10
  223.8 166.0 %copy-start.8 = (f32[2,128,704]{1,2,0:T(8,128)S(1)}, f32[2,128,704]{1,2,0:T(8,128)}, u32[]{:S(2)}) copy-start(f32[2,128,704]{1,2,0:T(8,128)} %param.30) | copy-start | bytes 2162692
  223.8 166.0 %copy-start.9 = (f32[2,128,704]{1,2,0:T(8,128)S(1)}, f32[2,128,704]{1,2,0:T(8,128)}, u32[]{:S(2)}) copy-start(f32[2,128,704]{1,2,0:T(8,128)} %param.35) | copy-start | bytes 2162692
  389.8 2.6 copy-start
  389.9 2.7 copy-start.1
  391.6 1.8 copy-start.3
  393.3 1.9 copy-start.11
  393.3 2.1 copy-start.12
  393.3 2.1 copy-start.13
  395.4 3.7 copy-start.14
  395.4 3.7 copy-start.15
  395.5 3.7 copy-start.16
  396.7 4.0 copy-start.19
  396.7 4.0 copy-start.20
  396.7 5.9 %copy-start.7 = (bf16[512,1024]{1,0:T(8,128)(2,1)S(1)}, bf16[512,1024]{1,0:T(8,128)(2,1)}, u32[]{:S(2)}) copy-start(bf16[512,1024]{1,0:T(8,128)(2,1)} %get-tuple-element.52) | copy-start | bytes 3145732
  399.1 4.4 %copy-start.4 = (f32[2048,256]{1,0:T(8,128)S(1)}, f32[2048,256]{1,0:T(8,128)}, u32[]{:S(2)}) copy-start(f32[2048,256]{1,0:T(8,128)} %get-tuple-element.74) | copy-start | bytes 6291460

commit v4 on v3

--- a/solution.py
+++ b/solution.py
@@ -3,6 +3,7 @@
 
 import jax
 import jax.numpy as jnp
+import numpy as np
 from jax import lax
 from jax.experimental import pallas as pl
 from jax.experimental.pallas import tpu as pltpu
@@ -600,11 +601,57 @@
             self.waited.append((self.base + 2 * (hop - 1) + way, only[way]))
 
 
+def position_tables(length):
+    rates = 10000.0 ** (-2.0 * np.arange(HD // 2) / HD)
+    angles = np.arange(length)[:, None] * rates[None, :]
+    cosine, sine = np.cos(angles), np.sin(angles)
+    return (
+        jnp.asarray(np.concatenate([cosine] * 4, axis=1), jnp.float32),
+        jnp.asarray(np.concatenate([-sine, sine, -sine, sine], axis=1), jnp.float32),
+    )
+
+
+def rope_tables_from(seg_ref, cos_at, sin_at, cos_ref, sin_ref, begin_ref, marks):
+    length = cos_at.shape[0]
+    segs = seg_ref[0:1, :].astype(jnp.float32)
+    spots = lax.broadcasted_iota(jnp.int32, (1, length), 1).astype(jnp.float32)
+    begins = jnp.zeros((1, length), jnp.float32)
+    marks[...] = jnp.zeros_like(marks)
+    for number in range(7):
+        start = jnp.sum(jnp.where(segs < number, 1.0, 0.0), axis=1, keepdims=True)
+        begins = jnp.where(segs == number, start, begins)
+        marks[number : number + 1, :] = jnp.where(spots == start, 1.0, 0.0)
+    begin_ref[...] = jnp.broadcast_to(begins.astype(jnp.int32), begin_ref.shape)
+    pick = lambda table: lax.dot_general(
+        marks[...],
+        table[...],
+        (((1,), (0,)), ((), ())),
+        precision=lax.Precision.HIGHEST,
+        preferred_element_type=jnp.float32,
+    )
+    first_cos, first_sin = pick(cos_at), pick(sin_at)
+    rows = length // PLANES
+    for block in range(PLANES):
+        span = pl.ds(block * rows, rows)
+        documents = jnp.transpose(
+            jnp.broadcast_to(segs[:, block * rows : block * rows + rows], (128, rows))
+        )
+        cosine = jnp.zeros((rows, 128), jnp.float32)
+        sine = jnp.zeros((rows, 128), jnp.float32)
+        for number in range(7):
+            here = documents == number
+            cosine = jnp.where(here, first_cos[number : number + 1], cosine)
+            sine = jnp.where(here, first_sin[number : number + 1], sine)
+        cos_ref[span, :] = cos_at[span, :] * cosine + sin_at[span, :] * sine
+        sin_ref[span, :] = sin_at[span, :] * cosine - cos_at[span, :] * sine
+
+
 def open_kernel(*refs):
-    hidden, attn_piece, out_piece, feed_piece, cos_ref, sin_ref, first_ref, begin_ref = refs[:8]
-    q_out, k_out, v_out, o_out, n_out, weight_out, out_weight_out, feed_all = refs[8:16]
-    gain_ref, square_ref, log_ref, middle_ref, normed_ref, attended_ref = refs[16:22]
-    held, q_ref, k_ref, v_ref, o_ref, n_ref, weight_ref, out_ref, send, recv, local = refs[22:]
+    hidden, attn_piece, out_piece, feed_piece, cos_at, sin_at, first_ref, seg_ref = refs[:8]
+    q_out, k_out, v_out, o_out, n_out, weight_out, out_weight_out, feed_all, cos_out, sin_out = refs[8:18]
+    gain_ref, square_ref, log_ref, middle_ref, normed_ref, attended_ref, begin_ref = refs[18:25]
+    held, q_ref, k_ref, v_ref, o_ref, n_ref, weight_ref, out_ref, cos_ref, sin_ref, turned_v, marks = refs[25:37]
+    send, recv, local = refs[37:]
     links = Links(send, recv)
     place, depth = links.place, links.depth
     shard = hidden.shape[0]
@@ -653,10 +700,13 @@
     attn.two()
     attn.three()
     slots[0].one()
+    rope_tables_from(seg_ref, cos_at, sin_at, cos_ref, sin_ref, begin_ref, marks)
     attn.end()
     for copy in (own_hidden, own_attn, own_out, own_feed):
         copy.wait()
     store(weight_ref, weight_out)
+    store(cos_ref, cos_out)
+    store(sin_ref, sin_out)
     gain_ref[...] = weight_ref[pl.ds(768, 16), :].astype(jnp.float32)
 
     def project(block):
@@ -677,6 +727,10 @@
         first = first_ref[rows, :].astype(jnp.float32)
         blended = 0.5 * value + 0.5 * first
         v_ref[rows, :] = blended.astype(jnp.bfloat16)
+        for half in range(2):
+            turned_v[half, :, rows] = jnp.transpose(
+                blended[:, half * 128 : half * 128 + 128]
+            ).astype(jnp.bfloat16)
         square_ref[0:1, :] += jnp.sum(first * first, axis=0, keepdims=True)
         square_ref[1:2, :] += jnp.sum(blended * blended, axis=0, keepdims=True)
 
@@ -710,8 +764,8 @@
     wide.left(3, (1, PLANES - 2))
     feeds.take(1, (1, PLANES - 2))
     feeds.take(2, (1, PLANES - 2))
-    for hop in range(1, PLANES):
-        feeds.send(hop, (1, PLANES - 2))
+    feeds.send(1, (1, PLANES - 2))
+    feeds.send(2, (1, PLANES - 2))
     thin.take(3)
     outs.one()
     project_hop(3)
@@ -721,48 +775,52 @@
     store(v_ref, v_out)
 
     lane = lax.broadcasted_iota(jnp.int32, (shard, 128), 1)
-    inside = lax.broadcasted_iota(jnp.int32, (shard, shard), 1)
-    down = lax.broadcasted_iota(jnp.int32, (shard, 1), 0)
-
-    def flash_pair(block, pair):
+    down = lax.broadcasted_iota(jnp.int32, (shard, shard), 0)
+    along = lax.broadcasted_iota(jnp.int32, (1, shard), 1)
+
+    def flash_block(block):
         rows = pl.ds(pl.multiple_of(block * shard, shard), shard)
-        lanes = columns_of(pair)
-        query = q_ref[rows, lanes]
-        begin = begin_ref[rows, :]
+        begin = begin_ref[0:1, rows]
+        pairs = [q_ref[rows, pl.ds(pair * 128, 128)] for pair in range(2)]
         parts = [
-            jnp.where((lane < HD) == (head == 0), query, jnp.zeros_like(query)) for head in range(2)
+            jnp.where((lane < HD) == (head % 2 == 0), pairs[head // 2], jnp.zeros_like(pairs[0]))
+            for head in range(4)
         ]
 
         def tile(index, carried, visible):
             span = pl.ds(pl.multiple_of(index * shard, shard), shard)
-            keys, values = k_ref[span, lanes], v_ref[span, lanes]
+            raw = [
+                tokens_dot(k_ref[span, pl.ds(head // 2 * 128, 128)], parts[head], 1, 1)
+                for head in range(4)
+            ]
             after = []
-            for head in range(2):
+            for head in range(4):
                 top, total, summed = carried[3 * head : 3 * head + 3]
-                scores = jnp.where(visible, tokens_dot(parts[head], keys, 1, 1), -1e30)
-                raised_top = jnp.maximum(top, jnp.max(scores, axis=1, keepdims=True))
+                scores = jnp.where(visible, raw[head], -1e30)
+                raised_top = jnp.maximum(top, jnp.max(scores, axis=0, keepdims=True))
                 shrink = jnp.exp2(top - raised_top)
                 shares = jnp.exp2(scores - raised_top)
-                total = total * shrink + jnp.sum(shares, axis=1, keepdims=True)
-                summed = summed * shrink + tokens_dot(shares.astype(jnp.bfloat16), values, 1, 0)
+                total = total * shrink + jnp.sum(shares, axis=0, keepdims=True)
+                values = turned_v[head // 2, pl.ds(head % 2 * HD, HD), span]
+                summed = summed * shrink + tokens_dot(values, shares.astype(jnp.bfloat16), 1, 0)
                 after += [raised_top, total, summed]
             return tuple(after)
 
         fresh = (
-            jnp.full((shard, 1), -1e30, jnp.float32),
-            jnp.zeros((shard, 1), jnp.float32),
-            jnp.zeros((shard, 128), jnp.float32),
-        )
-        carried = tile(block, fresh + fresh, (inside >= begin - block * shard) & (inside <= down))
-        top0, total0, sum0, top1, total1, sum1 = lax.fori_loop(
-            0, block, lambda j, held: tile(j, held, inside >= begin - j * shard), carried
-        )
-        o_ref[rows, lanes] = jnp.where(lane < HD, sum0 / total0, sum1 / total1).astype(jnp.bfloat16)
-        turned = jnp.transpose(
-            jnp.where(lane < HD, top0 + jnp.log2(total0), top1 + jnp.log2(total1))
-        )
-        log_ref[pair, 0:1, rows] = turned[0:1]
-        log_ref[pair, 1:2, rows] = turned[HD : HD + 1]
+            jnp.full((1, shard), -1e30, jnp.float32),
+            jnp.zeros((1, shard), jnp.float32),
+            jnp.zeros((HD, shard), jnp.float32),
+        )
+        carried = tile(block, fresh * 4, (down >= begin - block * shard) & (down <= along))
+        carried = lax.fori_loop(
+            0, block, lambda j, held: tile(j, held, down >= begin - j * shard), carried
+        )
+        for pair in range(2):
+            ends = [carried[3 * (2 * pair + head) : 3 * (2 * pair + head) + 3] for head in range(2)]
+            both = jnp.concatenate([summed / total for _, total, summed in ends], axis=0)
+            o_ref[rows, pl.ds(pair * 128, 128)] = jnp.transpose(both).astype(jnp.bfloat16)
+            for head, (top, total, _) in enumerate(ends):
+                log_ref[pair, head : head + 1, rows] = top + jnp.log2(total)
 
     own_columns = attended_ref.at[:, columns_of(depth, 256)]
 
@@ -787,22 +845,25 @@
         slots[2].one()
         outs.three()
 
-    pumps = ((0, pump_a), (1, pump_b), (2, pump_c), (4, slots[1].three), (5, slots[2].two))
+    pumps = ((0, pump_a), (1, pump_b), (2, pump_c))
 
     def flash(index, carried):
-        step, pair = PLANES - 1 - lax.div(index, 2), lax.rem(index, 2)
-        flash_pair(lax.rem(depth + step, PLANES), pair)
-        pl.when((pair == 1) & (step > 0))(lambda: hand(step).start())
+        step = PLANES - 1 - index
+        flash_block(lax.rem(depth + step, PLANES))
+        pl.when(step > 0)(lambda: hand(step).start())
         for when, pump in pumps:
             pl.when(index == when)(pump)
         return carried
 
-    lax.fori_loop(0, 2 * PLANES, flash, 0)
+    lax.fori_loop(0, PLANES, flash, 0)
+    feeds.send(3, (1, PLANES - 2))
     own_rows = pl.ds(pl.multiple_of(depth * shard, shard), shard)
     attended_ref[:, columns_of(depth, 256)] = o_ref[own_rows, :]
     store(o_ref, o_out)
     outs.end()
     store(out_ref, out_weight_out)
+    slots[1].three()
+    slots[2].two()
     for step in range(1, PLANES):
         source = lax.rem(depth - step + PLANES, PLANES)
         links.got(across + step, attended_ref.at[:, columns_of(source, 256)])
@@ -826,17 +887,18 @@
         copy.wait()
 
 
-def opening(hidden, attn_piece, out_piece, feed_piece, cosine, sine_part, first_values, begin_column):
+def opening(hidden, attn_piece, out_piece, feed_piece, first_values, seg_row):
     length, width = first_values.shape
     rows = hidden.shape[0]
     count = feed_piece.shape[0]
     low, full = jnp.bfloat16, jnp.float32
     any_spec, vmem = pl.BlockSpec(memory_space=pl.ANY), pl.BlockSpec(memory_space=pltpu.VMEM)
     shape = jax.ShapeDtypeStruct
+    cos_at, sin_at = position_tables(length)
     return pl.pallas_call(
         open_kernel,
         in_specs=[any_spec] * 4 + [vmem] * 4,
-        out_specs=[any_spec] * 8 + [vmem] * 6,
+        out_specs=[any_spec] * 10 + [vmem] * 7,
         out_shape=[
             shape((length, width), low),
             shape((length, width), low),
@@ -846,12 +908,15 @@
             shape((ATTN_ROWS, D), low),
             shape((D, D), low),
             shape((PLANES, 8, count, PIECE), low),
+            shape((length, 128), full),
+            shape((length, 128), full),
             shape((16, D), full),
             shape((8, width), full),
             shape((width // 128, 8, length), full),
             shape((rows, D), full),
             shape((rows, D), low),
             shape((rows, D), low),
+            shape((8, length), jnp.int32),
         ],
         scratch_shapes=[
             pltpu.VMEM((PLANES, rows, D), low),
@@ -862,15 +927,19 @@
             pltpu.VMEM((length, D), low),
             pltpu.VMEM((ATTN_ROWS, D), low),
             pltpu.VMEM((D, D), low),
+            pltpu.VMEM((length, 128), full),
+            pltpu.VMEM((length, 128), full),
+            pltpu.VMEM((width // 128, 128, length), low),
+            pltpu.VMEM((8, length), full),
             pltpu.SemaphoreType.DMA((OPEN_COPIES,)),
             pltpu.SemaphoreType.DMA((OPEN_COPIES,)),
-            pltpu.SemaphoreType.DMA((12,)),
+            pltpu.SemaphoreType.DMA((14,)),
         ],
         compiler_params=pltpu.CompilerParams(
             vmem_limit_bytes=VMEM_LIMIT, collective_id=1, has_side_effects=True
         ),
         name="opening",
-    )(hidden, attn_piece, out_piece, feed_piece, cosine, sine_part, first_values, begin_column)
+    )(hidden, attn_piece, out_piece, feed_piece, cos_at, sin_at, first_values, seg_row)
 
 
 def feed_kernel(*refs):
@@ -970,15 +1039,10 @@
             mine[now, 1, :, at] = (backs * active).astype(jnp.bfloat16)
         hand(slot).start()
 
-        def columns(tile, carried):
-            lanes = columns_of(tile, 256)
-            fed[:, lanes] += tokens_dot(mine[now, 2], weight[held, spans[2], lanes], 0, 0)
-            back_ref[:, lanes] += tokens_dot(
-                mine[now, 0], weight[held, spans[0], lanes], 0, 0
-            ) + tokens_dot(mine[now, 1], weight[held, spans[1], lanes], 0, 0)
-            return carried
-
-        lax.fori_loop(0, D // 256, columns, 0)
+        fed[...] += tokens_dot(mine[now, 2], weight[held, spans[2], :], 0, 0)
+        back_ref[...] += tokens_dot(mine[now, 0], weight[held, spans[0], :], 0, 0) + tokens_dot(
+            mine[now, 1], weight[held, spans[1], :], 0, 0
+        )
 
     def backward(slot):
         now = lax.rem(slot, 2)
@@ -1177,7 +1241,7 @@
     log_ref, begin_ref, gain_ref, small_in = refs[15:19]
     first_ref, back_ref, feed_total, out_total, attn_total, small_ref = refs[19:25]
     (
-        q_ref, k_ref, v_ref, o_ref, n_ref, weight_ref, cos_ref, sin_ref, grad, inner, total, made_ref,
+        q_ref, k_ref, v_ref, o_ref, weight_ref, cos_ref, sin_ref, grad, inner, total, made_ref,
         stay, feed_first, feed_final, feed_held, out_made, out_core, out_first, out_final, out_held,
         attn_core, attn_first, attn_final, partial, partial_held, small_got,
         send, recv, local,
@@ -1266,7 +1330,7 @@
     q_loads = [load(source, target) for source, target in ((q_in, q_ref), (k_in, k_ref), (v_in, v_ref), (o_in, o_ref), (cos_in, cos_ref), (sin_in, sin_ref))]
     own_rows = pl.ds(pl.multiple_of(depth * shard, shard), shard)
     q_loads.append(load(incoming[0], grad.at[own_rows, :]))
-    late = [load(n_in, n_ref), load(weight_in, weight_ref)]
+    weight_load = load(weight_in, weight_ref)
 
     links.greet()
     for pair in range(2):
@@ -1383,19 +1447,24 @@
             key_sum, value_sum = sums
             span = pl.ds(pl.multiple_of(index * shard, shard), shard)
             query_block, grad_block = q_ref[span, lanes], grad[span, lanes]
-            query_sum = total[span, :]
+            queries = [masked(query_block, head) for head in range(2)]
+            out_grads = [masked(grad_block, head) for head in range(2)]
+            scores = [tokens_dot(keys, queries[head], 1, 1) for head in range(2)]
+            share_grads = [tokens_dot(values, out_grads[head], 1, 1) for head in range(2)]
+            score_grads = []
             for head in range(2):
-                query, out_grad = masked(query_block, head), masked(grad_block, head)
-                scores = tokens_dot(keys, query, 1, 1)
                 shares = jnp.where(
-                    visible, jnp.exp2(scores - log_ref[pair, head : head + 1, span]), 0.0
+                    visible, jnp.exp2(scores[head] - log_ref[pair, head : head + 1, span]), 0.0
                 )
-                share_grad = tokens_dot(values, out_grad, 1, 1)
-                score_grad = (shares * (share_grad - inner[head : head + 1, span])).astype(jnp.bfloat16)
-                value_sum = value_sum + tokens_dot(shares.astype(jnp.bfloat16), out_grad, 1, 0)
-                key_sum = key_sum + tokens_dot(score_grad, query, 1, 0)
-                query_sum = query_sum + tokens_dot(score_grad, own_keys[head], 0, 0)
-            total[span, :] = query_sum
+                score_grads.append(
+                    (shares * (share_grads[head] - inner[head : head + 1, span])).astype(jnp.bfloat16)
+                )
+                value_sum = value_sum + tokens_dot(shares.astype(jnp.bfloat16), out_grads[head], 1, 0)
+            for head in range(2):
+                key_sum = key_sum + tokens_dot(score_grads[head], queries[head], 1, 0)
+            total[span, :] += tokens_dot(score_grads[0], own_keys[0], 0, 0) + tokens_dot(
+                score_grads[1], own_keys[1], 0, 0
+            )
             return (key_sum, value_sum)
 
         empty = jnp.zeros((shard, 128), jnp.float32)
@@ -1427,21 +1496,19 @@
         return carried
 
     lax.fori_loop(0, 2 * PLANES, back_step, 0)
-    for copy in late:
-        copy.wait()
+    quarters = [q_ref, k_ref, v_ref, o_ref]
+    quarter_loads = [
+        load(n_in.at[:, pl.ds(index * 256, 256)], quarter) for index, quarter in enumerate(quarters)
+    ]
+    weight_load.wait()
     small_ref[...] = small_in[...]
 
     def input_back(index, carried):
         block = jnp.where(depth < PLANES // 2, PLANES - 1 - index, index)
         rows = pl.ds(pl.multiple_of(block * shard, shard), shard)
-        value = tokens_dot(made_ref[rows, :], weight_ref[pl.ds(0, 768), :], 1, 0)
-        partial[block] = value.astype(jnp.bfloat16)
-        gain = (
-            jnp.sum(value * n_ref[rows, :].astype(jnp.float32), axis=0, keepdims=True)
-            / gain_ref[0:1, :]
-        )
-        for piece in range(8):
-            small_ref[0, piece : piece + 1, :] += gain[:, piece * PIECE : piece * PIECE + PIECE]
+        partial[block] = tokens_dot(made_ref[rows, :], weight_ref[pl.ds(0, 768), :], 1, 0).astype(
+            jnp.bfloat16
+        )
         return carried
 
     input_back(0, 0)
@@ -1449,6 +1516,24 @@
     lax.fori_loop(1, PLANES, input_back, 0)
     line.launch(2)
     line.launch(3)
+    for copy in quarter_loads:
+        copy.wait()
+
+    def gain_back(block, carried):
+        rows = pl.ds(pl.multiple_of(block * shard, shard), shard)
+        for index, quarter in enumerate(quarters):
+            value = partial[block, :, pl.ds(index * 256, 256)].astype(jnp.float32)
+            lanes = pl.ds(index * 256, 256)
+            gain = (
+                jnp.sum(value * quarter[rows, :].astype(jnp.float32), axis=0, keepdims=True)
+                / gain_ref[0:1, lanes]
+            )
+            for half in range(2):
+                piece = 2 * index + half
+                small_ref[0, piece : piece + 1, :] += gain[:, half * PIECE : half * PIECE + PIECE]
+        return carried
+
+    lax.fori_loop(0, PLANES, gain_back, 0)
     fold_two(0)
     out_line.take(1)
     out_line.forward(2)
@@ -1459,7 +1544,10 @@
     attn_made = out_made.at[pl.ds(0, 768), :]
     for index in range(3):
         rows = pl.ds(index * 256, 256)
-        attn_made[rows, :] = tokens_dot(made_ref[:, rows], n_ref[...], 0, 0).astype(jnp.bfloat16)
+        for quarter in range(4):
+            attn_made[rows, pl.ds(quarter * 256, 256)] = tokens_dot(
+                made_ref[:, rows], quarters[quarter][...], 0, 0
+            ).astype(jnp.bfloat16)
     for i in range(4):
         links.go(attn_swap + i, attn_made.at[:, others[i]], attn_core.at[i], core)
     links.got(tiny, small_got.at[0])
@@ -1521,7 +1609,6 @@
         ],
         scratch_shapes=[pltpu.VMEM((length, width), low)] * 4
         + [
-            pltpu.VMEM((length, D), low),
             pltpu.VMEM((ATTN_ROWS, D), low),
             pltpu.VMEM((length, 128), full),
             pltpu.VMEM((length, 128), full),
@@ -1595,6 +1682,65 @@
     )(middle, grad, back, weight, gains)
 
 
+def stepped(master, gradient, moment, square, step_rate, decay, outs, at):
+    new = adamw(master[at], gradient, moment[at], square[at], step_rate, decay)
+    for out, value in zip(outs, new):
+        out[at] = value
+
+
+def update_kernel(*refs):
+    hidden_ref, dm_ref, back_ref, gain_ref, attn_ref, out_ref, feed_ref, small_ref = refs[:8]
+    masters, moments, squares = refs[8:13], refs[13:18], refs[18:23]
+    grad_ref, norm_ref = refs[23:25]
+    outs = [refs[25 + index : 40 : 5] for index in range(5)]
+    place = lax.axis_index("dp")
+    hidden = hidden_ref[...].astype(jnp.float32)
+    factor = rms_factor(hidden)
+    grad_ref[...] = dm_ref[...] + norm_back(hidden, factor, gain_ref[0:1, :], back_ref[...])[0]
+    tokens = 8.0 * hidden_ref.shape[0] * PLANES
+    norm_ref[...] = jnp.sqrt(small_ref[16:24, :] / (tokens * D))
+    every = slice(None)
+    rates = (D**-0.5, max(1, 8 * HEADS * HD // LEN) ** -0.5, D**-0.5, (FF // 3) ** -0.5)
+
+    def weight(index, gradient, at):
+        stepped(
+            masters[index], gradient, moments[index], squares[index], rates[index], 0.1, outs[index], at
+        )
+
+    for which in range(3):
+        weight(0, jnp.transpose(attn_ref[pl.ds(which * 256, 256), :]), which)
+    weight(1, out_ref[...], (every, every))
+    count = masters[3].shape[0]
+    for which in range(2):
+        weight(2, feed_ref[pl.ds(which * count, count), :], which)
+    weight(3, feed_ref[pl.ds(2 * count, count), :], (every, every))
+    for which in range(2):
+        at = pl.ds(which, 1)
+        stepped(
+            masters[4],
+            small_ref[pl.ds(8 * which + place, 1), :],
+            moments[4],
+            squares[4],
+            0.2,
+            0.0,
+            outs[4],
+            (at, every),
+        )
+
+
+def update(hidden, dm, back, gains, totals, small, masters, moments, squares):
+    full = jnp.float32
+    shape = jax.ShapeDtypeStruct
+    return pl.pallas_call(
+        update_kernel,
+        out_shape=[shape(dm.shape, full), shape((8, PIECE), full)]
+        + [shape(one.shape, full) for one in masters] * 3,
+        compiler_params=pltpu.CompilerParams(vmem_limit_bytes=VMEM_LIMIT),
+        cost_estimate=cost(0, 16 << 20),
+        name="update",
+    )(hidden, dm, back, gains, *totals, small, *masters, *moments, *squares)
+
+
 def fast_shards(
     hidden_in,
     segment_ids,
@@ -1619,9 +1765,6 @@
     place, depth = lax.axis_index("dp"), lax.axis_index("mp")
     low = jnp.bfloat16
     hidden, out_cotangent = hidden_in[0], grad_out[0]
-    seg_row = segment_ids[0]
-    length = seg_row.shape[0]
-    shard = hidden.shape[0]
     ffs = reduce_proj.shape[0]
 
     attn_piece = jnp.concatenate(
@@ -1637,18 +1780,6 @@
             reduce_proj.astype(low),
         ]
     )
-
-    begins = jnp.zeros_like(seg_row)
-    for number in range(1, 7):
-        start = jnp.sum((seg_row < number).astype(jnp.int32))
-        begins = jnp.where(seg_row == number, start, begins)
-    lows = begins[:: length // BLOCKS]
-    offset = (jnp.arange(length, dtype=jnp.int32) - begins).astype(jnp.float32)
-    inverse_rates = 10000.0 ** (-2.0 * jnp.arange(HD // 2, dtype=jnp.float32) / HD)
-    angles = offset[:, None] * inverse_rates[None, :]
-    cosine, sine = jnp.cos(angles), jnp.sin(angles)
-    cosine = jnp.concatenate([cosine] * 4, axis=1)
-    sine_part = jnp.concatenate([-sine, sine, -sine, sine], axis=1)
 
     (
         queries,
@@ -1659,22 +1790,16 @@
         attn_weight,
         out_weight,
         feed_all,
+        cosine,
+        sine_part,
         gains,
         squares,
         logs,
         middle,
         normed_two,
         attended_own,
-    ) = opening(
-        hidden,
-        attn_piece,
-        output_proj.astype(low),
-        feed_piece,
-        cosine,
-        sine_part,
-        first_values[0],
-        begins[:, None],
-    )
+        begin_row,
+    ) = opening(hidden, attn_piece, output_proj.astype(low), feed_piece, first_values[0], segment_ids)
     normed_two_grad, layer_output, made = feed(normed_two, out_cotangent, middle, feed_all)
     layer_output = layer_output[None]
     branch_low, middle_grad, gain_two, *out_grads = middle_back(
@@ -1698,59 +1823,42 @@
         (cosine, sine_part),
         out_grads,
         logs,
-        jnp.broadcast_to(begins[None], (8, length)),
+        begin_row,
         gains,
         jnp.broadcast_to(small[None], (5, 24, PIECE)),
     )
     small = small[4]
-    value_norms = jnp.sqrt(small[16:18, 0] / (8 * length * D))
-    gain_total = lax.dynamic_index_in_dim(small[:16].reshape(2, 8, PIECE), place, 1, False)
-
-    hidden32 = hidden.astype(jnp.float32)
-    factor_one = rms_factor(hidden32)
-    input_part, _ = norm_back(hidden32, factor_one, gains[0], normed_grad)
-    input_grad = (middle_grad + input_part)[None]
-
-    expand_total = feed_total[: 2 * ffs].reshape(2, ffs, PIECE).transpose(0, 2, 1)
-    reduce_total = feed_total[2 * ffs :]
-    attn_total = attn_total.reshape(3, 256, PIECE).transpose(0, 2, 1)
-    new_input = adamw(input_proj, attn_total, old_moment_input, old_square_input, D ** (-0.5), 0.1)
-    new_output = adamw(
-        output_proj,
-        out_total,
+    masters = [input_proj, output_proj, expand_proj, reduce_proj, norm_gains]
+    moments = [
+        old_moment_input,
         old_moment_output,
+        old_moment_expand,
+        old_moment_reduce,
+        old_moment_gains,
+    ]
+    squares = [
+        old_square_input,
         old_square_output,
-        max(1, 8 * HEADS * HD // LEN) ** (-0.5),
-        0.1,
-    )
-    new_expand = adamw(
-        expand_proj, expand_total, old_moment_expand, old_square_expand, D ** (-0.5), 0.1
-    )
-    new_reduce = adamw(
-        reduce_proj, reduce_total, old_moment_reduce, old_square_reduce, (FF // 3) ** (-0.5), 0.1
-    )
-    new_gains = adamw(norm_gains, gain_total, old_moment_gains, old_square_gains, 0.2, 0.0)
-    return (
-        layer_output,
-        input_grad,
-        values_grad[None],
-        value_norms,
-        new_input[0],
-        new_output[0],
-        new_expand[0],
-        new_reduce[0],
-        new_gains[0],
-        new_input[1],
-        new_output[1],
-        new_expand[1],
-        new_reduce[1],
-        new_gains[1],
-        new_input[2],
-        new_output[2],
-        new_expand[2],
-        new_reduce[2],
-        new_gains[2],
-    )
+        old_square_expand,
+        old_square_reduce,
+        old_square_gains,
+    ]
+    for group in (masters, moments, squares):
+        group[2] = group[2].transpose(0, 2, 1)
+    input_grad, norms, *updated = update(
+        hidden,
+        middle_grad,
+        normed_grad,
+        gains,
+        (attn_total, out_total, feed_total),
+        small,
+        masters,
+        moments,
+        squares,
+    )
+    for index in (2, 7, 12):
+        updated[index] = updated[index].transpose(0, 2, 1)
+    return (layer_output, input_grad[None], values_grad[None], norms[:2, 0], *updated)
 
 
 def solution(mesh):

time: 412 us -> 386 us (0.937)
  other arithmetic: 29.9 us -> 5.45 us
  Pallas kernels: 364 us -> 369 us
    select_n x2 -> x0, other arithmetic: 8.58 us -> none  [fast_shards(): begins = jnp.where(seg_row == number, start, begins)]
    pallas_call x0 -> x1, Pallas kernels: none -> 8.37 us  [update(): pl.pallas_call(update_kernel, out_shape=[shape(dm.shape, full), shape((8,...]
    sub x5 -> x0, other arithmetic: 6.74 us -> none  [adamw(): master - step_rate * (update + decay * master)]
    pallas_call x1, Pallas kernels: 165 us -> 158 us  [closing(): pl.pallas_call(close_kernel, in_specs=[any_spec] * 15 + [vmem] * 4, out_s...]
    pallas_call x1, Pallas kernels: 147 us -> 152 us  [opening(): pl.pallas_call(open_kernel, in_specs=[any_spec] * 4 + [vmem] * 4, out_spe...]
where the time goes in v4:
time: 386 us; the launch traced here: 382 us
  Pallas kernels  369 us (96%)
  local copies, waits for them, and re-layouts  6.88 us (2%)
  other arithmetic  5.45 us (1%)
    pallas_call x1, Pallas kernels, closing(): pl.pallas_call(close_kernel, in_specs=[any_spec] * 15 + [vmem] * 4, out_s...  158 us
    pallas_call x1, Pallas kernels, opening(): pl.pallas_call(open_kernel, in_specs=[any_spec] * 4 + [vmem] * 4, out_spe...  152 us
    pallas_call x1, Pallas kernels, feed(): pl.pallas_call(feed_kernel, in_specs=[vmem, vmem, vmem, any_spec], out_sp...  43.5 us
    pallas_call x1, Pallas kernels, update(): pl.pallas_call(update_kernel, out_shape=[shape(dm.shape, full), shape((8,...  8.37 us

profile of v4, /device:TPU:0, one launch (start us, length us, event | category | flops | bytes accessed | tf_op | source)
XLA Modules:
  0.0 382.2 jit_solution(14717994610523998876)
XLA Ops:
  0.7 0.0 copy-start.1
  0.7 0.0 copy-start.4
  0.7 0.0 copy-start.3
  0.7 1.2 convert_element_type.18
  1.9 1.0 convert_element_type.19
  2.9 0.8 pad_maximum_fusion.refs_3_
  3.8 0.0 copy-done.1
  3.8 0.2 copy.41
  4.0 0.1 pad.8.clone
  4.0 0.0 copy-done.4
  4.0 0.9 maximum_maximum_fusion.refs_1_
  4.9 0.0 copy-done.3
  4.9 0.6 convert_element_type.17.refs_2_
  5.5 152.1 %opening.1 = (bf16[2048,256]{1,0:T(8,128)(2,1)}, bf16[2048,256]{1,0:T(8,128)(2,1)}, bf16[2048,256]{1,0:T(8,128)(2,1)}, bf16[2048,256]{1,0:T(8,128)(2,1)}, bf16[2...) custom-call(bf16[512,1024]{1,0:T(8,128)(2,1)} %bitcast.21, ...), custom_call_target="tpu_custom_call" | custom-call | tf_op jit(solution)/shard_map/opening/pallas_call | solution.py:898
  157.6 43.5 %feed.1 = (f32[512,1024]{1,0:T(8,128)}, bf16[512,1024]{1,0:T(8,128)(2,1)}, bf16[4,4,2112,128]{3,2,1,0:T(8,128)(2,1)}) custom-call(bf16[512,1024]{1,0:T(8,128)(2,1)} %get-tuple-element.69.refs_0_, bf16[512,1024]{1,0:T(8,128)(2,1)} %bitcast.23, f32[512,1024]{1,0:T(8,128)} %get-tuple-element.70.refs_2_.refs_0_, bf16[4,8,2112,128]{3,2,1,0:T(8,128)(2,1)} %get-tuple-element.71.refs_3_), custom_call_target="tpu_custom_call" | custom-call | tf_op jit(solution)/shard_map/feed/pallas_call | solution.py:1091
  201.1 6.5 %middle_back.1 = (bf16[512,1024]{1,0:T(8,128)(2,1)}, f32[512,1024]{1,0:T(8,128)}, f32[8,1024]{1,0:T(8,128)}, bf16[512,256]{1,0:T(8,128)(2,1)}, bf16[512,256]{1,0...) custom-call(f32[512,1024]{1,0:T(8,128)} %get-tuple-element.70.refs_2_.refs_0_, ...), custom_call_target="tpu_custom_call" | custom-call | flops 1073741824 | bytes 12582912 | tf_op jit(solution)/shard_map/middle_back/pallas_call | solution.py:1671
  207.6 0.8 slice.12
  208.3 0.8 slice_reduce_fusion
  209.2 0.1 pad.2.clone
  209.2 0.1 pad.3.clone
  209.3 0.1 maximum_maximum_fusion.1
  209.4 0.6 broadcast_in_dim.35.refs_18_
  210.0 158.4 %closing.1 = (f32[2048,256]{1,0:T(8,128)}, f32[512,1024]{1,0:T(8,128)}, f32[2112,128]{1,0:T(8,128)}, f32[256,128]{1,0:T(8,128)}, f32[768,128]{1,0:T(8,128)}, /*index=5*/f32[5,24,128]{2,1,0:T(8,128)}) custom-call(bf16[4,4,2112,128]{3,2,1,0:T(8,128)(2,1)} %get-tuple-element.77.refs_0_, bf16[512,1024]{1,0:T(8,128)(2,1)} %get-tuple-element.78.refs_1_, ...), custom_call_target="tpu_custom_call" | custom-call | tf_op jit(solution)/shard_map/closing/pallas_call | solution.py:1598
  368.5 1.3 slice_bitcast_fusion.refs_7_
  369.8 0.0 copy-start.2
  369.8 8.4 %update.1 = (f32[512,1024]{1,0:T(8,128)}, f32[8,128]{1,0:T(8,128)}, f32[3,128,256]{2,1,0:T(8,128)}, f32[256,128]{1,0:T(8,128)}, f32[2,704,128]{2,1,0:T(8,128)}, ...) custom-call(bf16[512,1024]{1,0:T(8,128)(2,1)} %bitcast.22, ...), custom_call_target="tpu_custom_call" | custom-call | bytes 16777216 | tf_op jit(solution)/shard_map/update/pallas_call | solution.py:1734
  378.2 0.0 copy-start
  378.2 1.5 slice_reduce_fusion.1
  379.6 0.0 copy-done.2
  379.6 1.0 copy.44
  380.6 0.0 copy-done
  380.6 1.3 copy.45
  (6 shorter events, 0.0 us)
Async XLA Ops:
  0.7 3.1 copy-start.1
  0.7 3.4 copy-start.4
  0.7 4.2 %copy-start.3 = (f32[256,128]{1,0:T(8,128)S(1)}, f32[256,128]{1,0:T(8,128)}, u32[]{:S(2)}) copy-start(f32[256,128]{1,0:T(8,128)} %refs_9_.1) | copy-start | bytes 393220
  369.8 9.8 %copy-start.2 = (bf16[512,1024]{1,0:T(8,128)(2,1)S(1)}, bf16[512,1024]{1,0:T(8,128)(2,1)}, u32[]{:S(2)}) copy-start(bf16[512,1024]{1,0:T(8,128)(2,1)} %get-tuple-element.72) | copy-start | bytes 3145732
  378.2 2.4 copy-start

commit v5 on v4

--- a/solution.py
+++ b/solution.py
@@ -502,6 +502,10 @@
         links.got(self.base, spots[1])
         links.go(self.base + 2, spots[1], spots[1], self.far)
 
+    def landed(self):
+        self.links.got(self.base + 1, self.spots[2])
+        self.links.got(self.base + 2, self.spots[3])
+
     def three(self):
         links, spots = self.links, self.spots
         links.go(self.base + 3, self.own, spots[0], self.core)
@@ -527,6 +531,10 @@
     def two(self, *given):
         for index, part in enumerate(self.parts):
             part.two(*[one[index] for one in given])
+
+    def landed(self):
+        for part in self.parts:
+            part.landed()
 
     def three(self):
         for part in self.parts:
@@ -563,8 +571,9 @@
         self.base = links.number(2 * (PLANES - 1))
         self.waited = links.waited
 
-    def send(self, hop, only=None):
+    def plan(self, hop, only=None):
         links, depth = self.links, self.links.depth
+        planned = []
         for way in range(2):
             to = depth + (1 if way else -1)
             when = (
@@ -575,13 +584,20 @@
             if only is not None:
                 when = when & (depth == only[way])
             source = self.own if hop == 1 else self.put(depth, way, hop - 1)
-            links.go(
-                self.base + 2 * (hop - 1) + way,
-                source,
-                self.put(to, way, hop),
-                (links.place, jnp.clip(to, 0, PLANES - 1)),
-                when,
+            planned.append(
+                (
+                    self.base + 2 * (hop - 1) + way,
+                    source,
+                    self.put(to, way, hop),
+                    (links.place, jnp.clip(to, 0, PLANES - 1)),
+                    when,
+                )
             )
+        return planned
+
+    def send(self, hop, only=None):
+        for parts in self.plan(hop, only):
+            self.links.go(*parts)
 
     def take(self, hop, only=None):
         links, depth = self.links, self.links.depth
@@ -765,7 +781,7 @@
     feeds.take(1, (1, PLANES - 2))
     feeds.take(2, (1, PLANES - 2))
     feeds.send(1, (1, PLANES - 2))
-    feeds.send(2, (1, PLANES - 2))
+    second = feeds.plan(2, (1, PLANES - 2))
     thin.take(3)
     outs.one()
     project_hop(3)
@@ -839,6 +855,9 @@
     def pump_b():
         slots[1].two()
         slots[0].end()
+        feeds.left(1, (1, PLANES - 2))
+        for parts in second:
+            links.go(*parts)
 
     def pump_c():
         feeds.take(2, near)
@@ -862,7 +881,6 @@
     store(o_ref, o_out)
     outs.end()
     store(out_ref, out_weight_out)
-    slots[1].three()
     slots[2].two()
     for step in range(1, PLANES):
         source = lax.rem(depth - step + PLANES, PLANES)
@@ -876,10 +894,9 @@
         middle_ref[rows, :] = middle
         factor = lax.rsqrt(jnp.mean(middle * middle, axis=-1, keepdims=True) + 1e-06)
         normed_ref[rows, :] = (middle * factor * gain_ref[1:2, :]).astype(jnp.bfloat16)
-    slots[2].three()
-    slots[1].end()
+    slots[1].landed()
+    slots[2].landed()
     feeds.take(3)
-    slots[2].end()
     for step in range(1, PLANES):
         hand(step).wait_send()
     links.drain()
@@ -953,14 +970,13 @@
     count = weight.shape[1] // 3
     rows = normed_ref.shape[0]
 
-    def load(which, buffer):
+    def load(slot):
+        own = range(8) if slot == 0 else [2 * piece + mine_first for piece in range(4)]
         return [
             pltpu.make_async_copy(
-                pieces.at[which, piece],
-                weight.at[buffer, :, pl.ds(piece * PIECE, PIECE)],
-                sem.at[buffer, piece],
+                pieces.at[slot, piece], weight.at[slot, :, columns_of(piece)], sem.at[slot, index]
             )
-            for piece in range(8)
+            for index, piece in enumerate(own)
         ]
 
     def flush(which, buffer):
@@ -973,11 +989,20 @@
             for piece in range(4)
         ]
 
-    for copy in load(0, 0):
-        copy.start()
+    loads = [load(slot) for slot in range(PLANES - 1)]
+    for copies in loads:
+        for copy in copies:
+            copy.start()
     far = pieces.at[PLANES - 1, place]
-    last = halved_spread(links, far, lambda piece: weight.at[2, :, columns_of(piece)])
-    last_own = pltpu.make_async_copy(far, weight.at[2, :, columns_of(place)], last_sem)
+    last = halved_spread(links, far, lambda piece: weight.at[PLANES - 1, :, columns_of(piece)])
+    last_own = pltpu.make_async_copy(far, weight.at[PLANES - 1, :, columns_of(place)], last_sem)
+    crossed = {slot: links.number(4) for slot in range(1, PLANES - 1)}
+    landings = {
+        slot: [
+            weight.at[slot, :, columns_of(2 * piece + theirs_first)] for piece in range(4)
+        ]
+        for slot in crossed
+    }
     last_own.start()
     links.greet(planes=False)
     last.one()
@@ -991,6 +1016,12 @@
                 core,
             )
             halves[index, :, pl.ds(piece * PIECE, PIECE)] = ref[:, columns_of(2 * piece + mine_first)]
+    for slot, number in crossed.items():
+        for piece in range(4):
+            own = 2 * piece + mine_first
+            links.go(
+                number + piece, pieces.at[slot, own], weight.at[slot, :, columns_of(own)], core
+            )
     fed[...] = jnp.zeros_like(fed)
     back_ref[...] = jnp.zeros_like(back_ref)
     for index in range(2):
@@ -1005,17 +1036,17 @@
 
     def forward(slot):
         now = lax.rem(slot, 2)
-        held = jnp.where(slot == PLANES - 1, 2, now)
-
-        @pl.when(slot < PLANES - 1)
-        def _():
-            for copy in load(slot, now):
+        held = slot
+
+        def ready(which):
+            for copy in loads[which]:
                 copy.wait()
-
-        @pl.when(slot + 2 < PLANES)
-        def _():
-            for copy in load(slot + 1, 1 - now):
-                copy.start()
+            if which:
+                for piece in range(4):
+                    links.got(crossed[which] + piece, landings[which][piece])
+
+        for which in range(PLANES - 1):
+            pl.when(slot == which)(functools.partial(ready, which))
 
         @pl.when(slot == PLANES - 1)
         def _():
@@ -1099,20 +1130,20 @@
         ],
         scratch_shapes=[
             pltpu.VMEM((rows, D), jnp.float32),
-            pltpu.VMEM((3, count, D), low),
+            pltpu.VMEM((PLANES, count, D), low),
             pltpu.VMEM((2, 3, count // 3, rows), low),
             pltpu.VMEM((PLANES, 3, count // 3, rows), low),
             pltpu.VMEM((2, count, 4 * PIECE), low),
             pltpu.VMEM((2, rows, 4 * PIECE), low),
             pltpu.VMEM((2, rows, 4 * PIECE), low),
-            pltpu.SemaphoreType.DMA((26,)),
-            pltpu.SemaphoreType.DMA((26,)),
-            pltpu.SemaphoreType.DMA((2, 8)),
+            pltpu.SemaphoreType.DMA((34,)),
+            pltpu.SemaphoreType.DMA((34,)),
+            pltpu.SemaphoreType.DMA((3, 8)),
             pltpu.SemaphoreType.DMA((2, 4)),
             pltpu.SemaphoreType.DMA,
         ],
         compiler_params=pltpu.CompilerParams(
-            vmem_limit_bytes=VMEM_LIMIT, collective_id=2, has_side_effects=True
+            vmem_limit_bytes=CLOSE_VMEM, collective_id=2, has_side_effects=True
         ),
         name="feed",
     )(normed, grad, middle, pieces)
@@ -1195,6 +1226,14 @@
                 self.to[way],
                 self.outer[step - 1][way],
             )
+
+    def left(self, step):
+        for way in range(2):
+            number = self.base + 2 * (step - 1) + way
+            block = self.blocks[step - 1][way]
+            copy = self.links.copy(number, block, block, self.to[way])
+            pl.when(self.outer[step - 1][way])(copy.wait_send)
+            self.links.waited.append((number, 0 if way else PLANES - 1))
 
     def take(self, step):
         for way in range(2):
@@ -1514,8 +1553,6 @@
     input_back(0, 0)
     line.launch(1)
     lax.fori_loop(1, PLANES, input_back, 0)
-    line.launch(2)
-    line.launch(3)
     for copy in quarter_loads:
         copy.wait()
 
@@ -1557,6 +1594,8 @@
         links.got(attn_swap + i, attn_core.at[i])
         add_into(attn_core.at[i], attn_made.at[:, sides[i]])
     attn_fold.one()
+    line.left(1)
+    line.launch(2)
     line.take(1)
     line.forward(2)
     links.got(tiny + 1, small_got.at[1])
@@ -1576,6 +1615,8 @@
     small_got[3 + depth] = small_ref[3]
     out_line.take(3)
     out_line.total(out_final.at[pl.ds(pl.multiple_of(depth * 256, 256), 256), :], out_total)
+    line.left(2)
+    line.launch(3)
     line.take(2)
     line.forward(3)
     attn_fold.end()

time: 386 us -> 380 us (0.984)
  Pallas kernels: 369 us -> 362 us
    pallas_call x1, Pallas kernels: 158 us -> 153 us  [closing(): pl.pallas_call(close_kernel, in_specs=[any_spec] * 15 + [vmem] * 4, out_s...]
where the time goes in v5:
time: 380 us; the launch traced here: 376 us
  Pallas kernels  362 us (95%)
  local copies, waits for them, and re-layouts  6.88 us (2%)
  other arithmetic  5.45 us (1%)
    pallas_call x1, Pallas kernels, closing(): pl.pallas_call(close_kernel, in_specs=[any_spec] * 15 + [vmem] * 4, out_s...  153 us
    pallas_call x1, Pallas kernels, opening(): pl.pallas_call(open_kernel, in_specs=[any_spec] * 4 + [vmem] * 4, out_spe...  149 us
    pallas_call x1, Pallas kernels, feed(): pl.pallas_call(feed_kernel, in_specs=[vmem, vmem, vmem, any_spec], out_sp...  44.8 us
    pallas_call x1, Pallas kernels, update(): pl.pallas_call(update_kernel, out_shape=[shape(dm.shape, full), shape((8,...  8.37 us

profile of v5, /device:TPU:0, one launch (start us, length us, event | category | flops | bytes accessed | tf_op | source)
XLA Modules:
  0.0 375.6 jit_solution(14861126436777179077)
XLA Ops:
  0.7 0.0 copy-start.1
  0.7 0.0 copy-start.4
  0.7 0.0 copy-start.3
  0.7 1.2 convert_element_type.18
  1.9 1.0 convert_element_type.19
  2.9 0.8 pad_maximum_fusion.refs_3_
  3.8 0.0 copy-done.1
  3.8 0.2 copy.41
  4.0 0.1 pad.8.clone
  4.0 0.0 copy-done.4
  4.0 0.9 maximum_maximum_fusion.refs_1_
  4.9 0.0 copy-done.3
  4.9 0.6 convert_element_type.17.refs_2_
  5.5 149.1 %opening.1 = (bf16[2048,256]{1,0:T(8,128)(2,1)}, bf16[2048,256]{1,0:T(8,128)(2,1)}, bf16[2048,256]{1,0:T(8,128)(2,1)}, bf16[2048,256]{1,0:T(8,128)(2,1)}, bf16[2...) custom-call(bf16[512,1024]{1,0:T(8,128)(2,1)} %bitcast.21, ...), custom_call_target="tpu_custom_call" | custom-call | tf_op jit(solution)/shard_map/opening/pallas_call | solution.py:915
  154.7 44.8 %feed.1 = (f32[512,1024]{1,0:T(8,128)}, bf16[512,1024]{1,0:T(8,128)(2,1)}, bf16[4,4,2112,128]{3,2,1,0:T(8,128)(2,1)}) custom-call(bf16[512,1024]{1,0:T(8,128)(2,1)} %get-tuple-element.69.refs_0_, bf16[512,1024]{1,0:T(8,128)(2,1)} %bitcast.23, f32[512,1024]{1,0:T(8,128)} %get-tuple-element.70.refs_2_.refs_0_, bf16[4,8,2112,128]{3,2,1,0:T(8,128)(2,1)} %get-tuple-element.71.refs_3_), custom_call_target="tpu_custom_call" | custom-call | tf_op jit(solution)/shard_map/feed/pallas_call | solution.py:1122
  199.5 6.5 %middle_back.1 = (bf16[512,1024]{1,0:T(8,128)(2,1)}, f32[512,1024]{1,0:T(8,128)}, f32[8,1024]{1,0:T(8,128)}, bf16[512,256]{1,0:T(8,128)(2,1)}, bf16[512,256]{1,0...) custom-call(f32[512,1024]{1,0:T(8,128)} %get-tuple-element.70.refs_2_.refs_0_, ...), custom_call_target="tpu_custom_call" | custom-call | flops 1073741824 | bytes 12582912 | tf_op jit(solution)/shard_map/middle_back/pallas_call | solution.py:1712
  206.0 0.8 slice.12
  206.7 0.8 slice_reduce_fusion
  207.5 0.1 pad.2.clone
  207.6 0.1 pad.3.clone
  207.7 0.1 maximum_maximum_fusion.1
  207.8 0.6 broadcast_in_dim.35.refs_18_
  208.4 153.4 %closing.1 = (f32[2048,256]{1,0:T(8,128)}, f32[512,1024]{1,0:T(8,128)}, f32[2112,128]{1,0:T(8,128)}, f32[256,128]{1,0:T(8,128)}, f32[768,128]{1,0:T(8,128)}, /*index=5*/f32[5,24,128]{2,1,0:T(8,128)}) custom-call(bf16[4,4,2112,128]{3,2,1,0:T(8,128)(2,1)} %get-tuple-element.77.refs_0_, bf16[512,1024]{1,0:T(8,128)(2,1)} %get-tuple-element.78.refs_1_, ...), custom_call_target="tpu_custom_call" | custom-call | tf_op jit(solution)/shard_map/closing/pallas_call | solution.py:1639
  361.8 1.3 slice_bitcast_fusion.refs_7_
  363.2 0.0 copy-start.2
  363.2 8.4 %update.1 = (f32[512,1024]{1,0:T(8,128)}, f32[8,128]{1,0:T(8,128)}, f32[3,128,256]{2,1,0:T(8,128)}, f32[256,128]{1,0:T(8,128)}, f32[2,704,128]{2,1,0:T(8,128)}, ...) custom-call(bf16[512,1024]{1,0:T(8,128)(2,1)} %bitcast.22, ...), custom_call_target="tpu_custom_call" | custom-call | bytes 16777216 | tf_op jit(solution)/shard_map/update/pallas_call | solution.py:1775
  371.5 0.0 copy-start
  371.5 1.5 slice_reduce_fusion.1
  373.0 0.0 copy-done.2
  373.0 1.0 copy.44
  374.0 0.0 copy-done
  374.0 1.3 copy.45
  (6 shorter events, 0.0 us)
Async XLA Ops:
  0.7 3.1 copy-start.1
  0.7 3.4 copy-start.4
  0.7 4.2 %copy-start.3 = (f32[256,128]{1,0:T(8,128)S(1)}, f32[256,128]{1,0:T(8,128)}, u32[]{:S(2)}) copy-start(f32[256,128]{1,0:T(8,128)} %refs_9_.1) | copy-start | bytes 393220
  363.2 9.8 %copy-start.2 = (bf16[512,1024]{1,0:T(8,128)(2,1)S(1)}, bf16[512,1024]{1,0:T(8,128)(2,1)}, u32[]{:S(2)}) copy-start(bf16[512,1024]{1,0:T(8,128)(2,1)} %get-tuple-element.72) | copy-start | bytes 3145732
  371.5 2.4 copy-start

commit v6 on v5

--- a/solution.py
+++ b/solution.py
@@ -1227,13 +1227,21 @@
                 self.outer[step - 1][way],
             )
 
-    def left(self, step):
-        for way in range(2):
-            number = self.base + 2 * (step - 1) + way
-            block = self.blocks[step - 1][way]
-            copy = self.links.copy(number, block, block, self.to[way])
-            pl.when(self.outer[step - 1][way])(copy.wait_send)
-            self.links.waited.append((number, 0 if way else PLANES - 1))
+    def outer_plan(self, step):
+        return [
+            (
+                self.base + 2 * (step - 1) + way,
+                self.blocks[step - 1][way],
+                self.held[way][step - 1],
+                self.to[way],
+                self.outer[step - 1][way],
+            )
+            for way in range(2)
+        ]
+
+    def go_all(self, planned):
+        for parts in planned:
+            self.links.go(*parts)
 
     def take(self, step):
         for way in range(2):
@@ -1280,7 +1288,7 @@
     log_ref, begin_ref, gain_ref, small_in = refs[15:19]
     first_ref, back_ref, feed_total, out_total, attn_total, small_ref = refs[19:25]
     (
-        q_ref, k_ref, v_ref, o_ref, weight_ref, cos_ref, sin_ref, grad, inner, total, made_ref,
+        q_ref, k_ref, v_ref, o_ref, weight_ref, cos_ref, sin_ref, grad, inner, query_acc, key_acc, made_ref,
         stay, feed_first, feed_final, feed_held, out_made, out_core, out_first, out_final, out_held,
         attn_core, attn_first, attn_final, partial, partial_held, small_got,
         send, recv, local,
@@ -1443,7 +1451,6 @@
         feed_line.take(1)
         feed_line.forward(2)
         out_fold.two()
-        take_grads(1)
 
     def after_d():
         fold_two(1)
@@ -1451,87 +1458,99 @@
         for copy in restay(0):
             copy.start()
         out_fold.end()
+        for step in range(1, PLANES):
+            out_line.launch(step)
 
     def after_e():
         folds[1].end()
         feed_line.launch(3)
-        feed_line.take(2)
-        feed_line.forward(3)
-        for step in range(1, PLANES):
-            out_line.launch(step)
-
-    def back_step(step, carried):
-        pair, block = lax.div(step, PLANES), lax.rem(step, PLANES)
+
+    weight_load.wait()
+    lower = depth < PLANES // 2
+    query_acc[...] = jnp.zeros_like(query_acc)
+    key_acc[...] = jnp.zeros_like(key_acc)
+    first_ref[...] = jnp.zeros_like(first_ref)
+    launches = [line.outer_plan(step) for step in range(1, PLANES)]
+
+    def rows_of(block):
+        return pl.ds(pl.multiple_of(block * shard, shard), shard)
+
+    def back_step(index, carried):
+        stage, pair = lax.div(index, 2), lax.rem(index, 2)
+        block = jnp.where(lower, PLANES - 1 - stage, stage)
         lanes = columns_of(pair)
-        start = pl.multiple_of(block * shard, shard)
-        own = pl.ds(start, shard)
-
-        @pl.when(block == 0)
+        own = rows_of(block)
+
+        @pl.when(stage == 0)
         def _():
-            total[...] = jnp.zeros_like(total)
-            for index in range(PLANES):
-                span = pl.ds(index * shard, shard)
+            for other in range(PLANES):
+                span = pl.ds(other * shard, shard)
                 turned = jnp.transpose(
                     grad[span, lanes].astype(jnp.float32) * o_ref[span, lanes].astype(jnp.float32)
                 )
                 for head in range(2):
-                    inner[head : head + 1, span] = jnp.sum(
+                    inner[pair, head : head + 1, span] = jnp.sum(
                         turned[head * HD : head * HD + HD], axis=0, keepdims=True
                     )
 
-        keys, values = k_ref[own, lanes], v_ref[own, lanes]
-        own_keys = [masked(keys, head) for head in range(2)]
-
-        def tile(index, sums, visible):
-            key_sum, value_sum = sums
-            span = pl.ds(pl.multiple_of(index * shard, shard), shard)
-            query_block, grad_block = q_ref[span, lanes], grad[span, lanes]
+        def tile(query_rows, key_rows, visible):
+            keys, values = k_ref[key_rows, lanes], v_ref[key_rows, lanes]
+            query_block, grad_block = q_ref[query_rows, lanes], grad[query_rows, lanes]
             queries = [masked(query_block, head) for head in range(2)]
             out_grads = [masked(grad_block, head) for head in range(2)]
             scores = [tokens_dot(keys, queries[head], 1, 1) for head in range(2)]
             share_grads = [tokens_dot(values, out_grads[head], 1, 1) for head in range(2)]
-            score_grads = []
+            score_grads, value_sum, key_sum = [], 0.0, 0.0
             for head in range(2):
                 shares = jnp.where(
-                    visible, jnp.exp2(scores[head] - log_ref[pair, head : head + 1, span]), 0.0
+                    visible,
+                    jnp.exp2(scores[head] - log_ref[pair, head : head + 1, query_rows]),
+                    0.0,
                 )
                 score_grads.append(
-                    (shares * (share_grads[head] - inner[head : head + 1, span])).astype(jnp.bfloat16)
+                    (shares * (share_grads[head] - inner[pair, head : head + 1, query_rows])).astype(
+                        jnp.bfloat16
+                    )
                 )
                 value_sum = value_sum + tokens_dot(shares.astype(jnp.bfloat16), out_grads[head], 1, 0)
             for head in range(2):
                 key_sum = key_sum + tokens_dot(score_grads[head], queries[head], 1, 0)
-            total[span, :] += tokens_dot(score_grads[0], own_keys[0], 0, 0) + tokens_dot(
-                score_grads[1], own_keys[1], 0, 0
-            )
-            return (key_sum, value_sum)
-
-        empty = jnp.zeros((shard, 128), jnp.float32)
-        sums = tile(
-            block, (empty, empty), (down >= begin_ref[0:1, own] - start) & (down <= along)
-        )
-        key_sum, value_sum = lax.fori_loop(
-            block + 1,
-            PLANES,
-            lambda i, held: tile(
-                i,
-                held,
-                down >= begin_ref[0:1, pl.ds(pl.multiple_of(i * shard, shard), shard)] - start,
-            ),
-            sums,
-        )
+            first_ref[key_rows, lanes] += value_sum
+            key_acc[key_rows, lanes] += key_sum
+            query_acc[query_rows, lanes] += tokens_dot(
+                score_grads[0], masked(keys, 0), 0, 0
+            ) + tokens_dot(score_grads[1], masked(keys, 1), 0, 0)
+
+        def off(other, held):
+            query = rows_of(jnp.where(lower, block, block + 1 + other))
+            key_block = jnp.where(lower, other, block)
+            tile(query, rows_of(key_block), down >= begin_ref[0:1, query] - key_block * shard)
+            return held
+
+        tile(own, own, (down >= begin_ref[0:1, own] - block * shard) & (down <= along))
+        lax.fori_loop(0, PLANES - 1 - stage, off, 0)
         cosine, sine_part = cos_ref[own, :], sin_ref[own, :]
         made_ref[own, columns_of(pair)] = turn(
-            total[own, :] * HD**-0.5, cosine, sine_part, False
+            query_acc[own, lanes] * HD**-0.5, cosine, sine_part, False
         ).astype(jnp.bfloat16)
         made_ref[own, columns_of(2 + pair)] = turn(
-            key_sum * (1 / LOG2E), cosine, sine_part, False
+            key_acc[own, lanes] * (1 / LOG2E), cosine, sine_part, False
         ).astype(jnp.bfloat16)
-        half_sum = 0.5 * value_sum
+        half_sum = 0.5 * first_ref[own, lanes]
         made_ref[own, columns_of(4 + pair)] = half_sum.astype(jnp.bfloat16)
         first_ref[own, lanes] = half_sum
-        for when, pump in ((0, after_a), (1, after_b), (3, after_c), (5, after_d), (7, after_e)):
-            pl.when(step == when)(pump)
+
+        @pl.when(pair == 1)
+        def _():
+            partial[block] = tokens_dot(
+                made_ref[own, :], weight_ref[pl.ds(0, 768), :], 1, 0
+            ).astype(jnp.bfloat16)
+            for number, parts in enumerate(launches):
+                pl.when(stage == number)(functools.partial(line.go_all, parts))
+
+        pl.when(index == 0)(lambda: take_grads(1))
+        for when, pump in ((0, after_a), (1, after_b), (2, after_c), (4, after_d), (7, after_e)):
+            pl.when(index == when)(pump)
         return carried
 
     lax.fori_loop(0, 2 * PLANES, back_step, 0)
@@ -1539,20 +1558,9 @@
     quarter_loads = [
         load(n_in.at[:, pl.ds(index * 256, 256)], quarter) for index, quarter in enumerate(quarters)
     ]
-    weight_load.wait()
     small_ref[...] = small_in[...]
-
-    def input_back(index, carried):
-        block = jnp.where(depth < PLANES // 2, PLANES - 1 - index, index)
-        rows = pl.ds(pl.multiple_of(block * shard, shard), shard)
-        partial[block] = tokens_dot(made_ref[rows, :], weight_ref[pl.ds(0, 768), :], 1, 0).astype(
-            jnp.bfloat16
-        )
-        return carried
-
-    input_back(0, 0)
-    line.launch(1)
-    lax.fori_loop(1, PLANES, input_back, 0)
+    line.take(1)
+    line.forward(2)
     for copy in quarter_loads:
         copy.wait()
 
@@ -1572,10 +1580,9 @@
 
     lax.fori_loop(0, PLANES, gain_back, 0)
     fold_two(0)
-    out_line.take(1)
-    out_line.forward(2)
-
     links.go(tiny, small_ref.at[0], small_got.at[0], tiny_to[0])
+    feed_line.take(2)
+    feed_line.forward(3)
     for copy in out_swaps:
         copy.wait_send()
     attn_made = out_made.at[pl.ds(0, 768), :]
@@ -1594,38 +1601,34 @@
         links.got(attn_swap + i, attn_core.at[i])
         add_into(attn_core.at[i], attn_made.at[:, sides[i]])
     attn_fold.one()
-    line.left(1)
-    line.launch(2)
-    line.take(1)
-    line.forward(2)
     links.got(tiny + 1, small_got.at[1])
     small_ref[2] = small_ref[1] + small_got[1]
     links.go(tiny + 2, small_ref.at[2], small_got.at[2], tiny_to[2])
-    folds[0].end()
-    feed_line.take(3)
-    feed_line.total(feed_final.at[0], feed_total)
-    out_line.take(2)
-    out_line.forward(3)
-    attn_fold.two()
+    line.take(2)
+    line.forward(3)
     links.got(tiny + 2, small_got.at[2])
     small_ref[3] = small_ref[2] + small_got[2]
     small_place = small_got.at[3 + depth]
     for step in range(1, PLANES):
         links.go(tiny + 2 + step, small_ref.at[3], small_place, plane_to[step - 1])
     small_got[3 + depth] = small_ref[3]
+    out_line.take(1)
+    out_line.forward(2)
+    attn_fold.two()
+    folds[0].end()
+    out_line.take(2)
+    out_line.forward(3)
+    attn_fold.end()
+    attn_total[...] = attn_final[...].astype(jnp.float32)
+    line.take(3)
+    line.total(partial.at[depth], back_ref)
+    feed_line.take(3)
+    feed_line.total(feed_final.at[0], feed_total)
     out_line.take(3)
     out_line.total(out_final.at[pl.ds(pl.multiple_of(depth * 256, 256), 256), :], out_total)
-    line.left(2)
-    line.launch(3)
-    line.take(2)
-    line.forward(3)
-    attn_fold.end()
-    attn_total[...] = attn_final[...].astype(jnp.float32)
     for step in range(1, PLANES):
         links.got(tiny + 2 + step, small_got.at[3 + plane_rows[step]])
     small_ref[4] = small_got[3] + small_got[4] + small_got[5] + small_got[6]
-    line.take(3)
-    line.total(partial.at[depth], back_ref)
     links.drain()
 
 
@@ -1654,8 +1657,9 @@
             pltpu.VMEM((length, 128), full),
             pltpu.VMEM((length, 128), full),
             pltpu.VMEM((length, width), low),
-            pltpu.VMEM((8, length), full),
-            pltpu.VMEM((length, 128), full),
+            pltpu.VMEM((2, 8, length), full),
+            pltpu.VMEM((length, width), full),
+            pltpu.VMEM((length, width), full),
             pltpu.VMEM((length, 768), low),
             pltpu.VMEM((2, 2, count, PIECE), low),
             pltpu.VMEM((PLANES, 2, count, PIECE), low),

time: 380 us -> 366 us (0.963)
  Pallas kernels: 362 us -> 348 us
    pallas_call x1, Pallas kernels: 153 us -> 140 us  [closing(): pl.pallas_call(close_kernel, in_specs=[any_spec] * 15 + [vmem] * 4, out_s...]
where the time goes in v6:
time: 366 us; the launch traced here: 362 us
  Pallas kernels  348 us (95%)
  local copies, waits for them, and re-layouts  6.88 us (2%)
  other arithmetic  5.45 us (1%)
    pallas_call x1, Pallas kernels, opening(): pl.pallas_call(open_kernel, in_specs=[any_spec] * 4 + [vmem] * 4, out_spe...  149 us
    pallas_call x1, Pallas kernels, closing(): pl.pallas_call(close_kernel, in_specs=[any_spec] * 15 + [vmem] * 4, out_s...  140 us
    pallas_call x1, Pallas kernels, feed(): pl.pallas_call(feed_kernel, in_specs=[vmem, vmem, vmem, any_spec], out_sp...  44.8 us
    pallas_call x1, Pallas kernels, update(): pl.pallas_call(update_kernel, out_shape=[shape(dm.shape, full), shape((8,...  8.37 us

profile of v6, /device:TPU:0, one launch (start us, length us, event | category | flops | bytes accessed | tf_op | source)
XLA Modules:
  0.0 361.8 jit_solution(4655527858703461972)
XLA Ops:
  0.7 0.0 copy-start.1
  0.7 0.0 copy-start.4
  0.7 0.0 copy-start.3
  0.7 1.2 convert_element_type.18
  1.9 1.0 convert_element_type.19
  2.9 0.8 pad_maximum_fusion.refs_3_
  3.8 0.0 copy-done.1
  3.8 0.2 copy.41
  4.0 0.1 pad.8.clone
  4.0 0.0 copy-done.4
  4.0 0.9 maximum_maximum_fusion.refs_1_
  4.9 0.0 copy-done.3
  4.9 0.6 convert_element_type.17.refs_2_
  5.5 149.1 %opening.1 = (bf16[2048,256]{1,0:T(8,128)(2,1)}, bf16[2048,256]{1,0:T(8,128)(2,1)}, bf16[2048,256]{1,0:T(8,128)(2,1)}, bf16[2048,256]{1,0:T(8,128)(2,1)}, bf16[2...) custom-call(bf16[512,1024]{1,0:T(8,128)(2,1)} %bitcast.21, ...), custom_call_target="tpu_custom_call" | custom-call | tf_op jit(solution)/shard_map/opening/pallas_call | solution.py:915
  154.7 44.8 %feed.1 = (f32[512,1024]{1,0:T(8,128)}, bf16[512,1024]{1,0:T(8,128)(2,1)}, bf16[4,4,2112,128]{3,2,1,0:T(8,128)(2,1)}) custom-call(bf16[512,1024]{1,0:T(8,128)(2,1)} %get-tuple-element.69.refs_0_, bf16[512,1024]{1,0:T(8,128)(2,1)} %bitcast.23, f32[512,1024]{1,0:T(8,128)} %get-tuple-element.70.refs_2_.refs_0_, bf16[4,8,2112,128]{3,2,1,0:T(8,128)(2,1)} %get-tuple-element.71.refs_3_), custom_call_target="tpu_custom_call" | custom-call | tf_op jit(solution)/shard_map/feed/pallas_call | solution.py:1122
  199.5 6.5 %middle_back.1 = (bf16[512,1024]{1,0:T(8,128)(2,1)}, f32[512,1024]{1,0:T(8,128)}, f32[8,1024]{1,0:T(8,128)}, bf16[512,256]{1,0:T(8,128)(2,1)}, bf16[512,256]{1,0...) custom-call(f32[512,1024]{1,0:T(8,128)} %get-tuple-element.70.refs_2_.refs_0_, ...), custom_call_target="tpu_custom_call" | custom-call | flops 1073741824 | bytes 12582912 | tf_op jit(solution)/shard_map/middle_back/pallas_call | solution.py:1716
  206.0 0.8 slice.12
  206.7 0.8 slice_reduce_fusion
  207.5 0.1 pad.2.clone
  207.6 0.1 pad.3.clone
  207.7 0.1 maximum_maximum_fusion.1
  207.8 0.6 broadcast_in_dim.35.refs_18_
  208.4 139.6 %closing.1 = (f32[2048,256]{1,0:T(8,128)}, f32[512,1024]{1,0:T(8,128)}, f32[2112,128]{1,0:T(8,128)}, f32[256,128]{1,0:T(8,128)}, f32[768,128]{1,0:T(8,128)}, /*index=5*/f32[5,24,128]{2,1,0:T(8,128)}) custom-call(bf16[4,4,2112,128]{3,2,1,0:T(8,128)(2,1)} %get-tuple-element.77.refs_0_, bf16[512,1024]{1,0:T(8,128)(2,1)} %get-tuple-element.78.refs_1_, ...), custom_call_target="tpu_custom_call" | custom-call | tf_op jit(solution)/shard_map/closing/pallas_call | solution.py:1642
  348.1 1.3 slice_bitcast_fusion.refs_7_
  349.4 0.0 copy-start.2
  349.4 8.4 %update.1 = (f32[512,1024]{1,0:T(8,128)}, f32[8,128]{1,0:T(8,128)}, f32[3,128,256]{2,1,0:T(8,128)}, f32[256,128]{1,0:T(8,128)}, f32[2,704,128]{2,1,0:T(8,128)}, ...) custom-call(bf16[512,1024]{1,0:T(8,128)(2,1)} %bitcast.22, ...), custom_call_target="tpu_custom_call" | custom-call | bytes 16777216 | tf_op jit(solution)/shard_map/update/pallas_call | solution.py:1779
  357.8 0.0 copy-start
  357.8 1.5 slice_reduce_fusion.1
  359.2 0.0 copy-done.2
  359.2 1.0 copy.44
  360.2 0.0 copy-done
  360.2 1.3 copy.45
  (6 shorter events, 0.0 us)
Async XLA Ops:
  0.7 3.1 copy-start.1
  0.7 3.4 copy-start.4
  0.7 4.2 %copy-start.3 = (f32[256,128]{1,0:T(8,128)S(1)}, f32[256,128]{1,0:T(8,128)}, u32[]{:S(2)}) copy-start(f32[256,128]{1,0:T(8,128)} %refs_9_.1) | copy-start | bytes 393220
  349.4 9.8 %copy-start.2 = (bf16[512,1024]{1,0:T(8,128)(2,1)S(1)}, bf16[512,1024]{1,0:T(8,128)(2,1)}, u32[]{:S(2)}) copy-start(bf16[512,1024]{1,0:T(8,128)(2,1)} %get-tuple-element.72) | copy-start | bytes 3145732
  357.8 2.4 copy-start

commit v7 on v6

--- a/solution.py
+++ b/solution.py
@@ -20,7 +20,7 @@
 BLOCKS = 4
 ATTN_ROWS = 784
 VMEM_LIMIT = 56 << 20
-OPEN_COPIES = 80
+OPEN_COPIES = 100
 CLOSE_COPIES = 80
 CLOSE_VMEM = 60 << 20
 
@@ -691,9 +691,18 @@
         lambda plane, way, hop: feed_all.at[slot_at(plane, way, hop), place],
     )
     attn = Spread(links, attn_piece, lambda piece: weight_ref.at[:, columns_of(piece)], (2, 4))
-    outs = Spread(
-        links, out_ref.at[:, columns_of(place)], lambda piece: out_ref.at[:, columns_of(piece)], (2, 4)
-    )
+    outs = []
+    for slot in range(PLANES):
+        block = at_plane(depth, [SLOTS[plane][slot][2] for plane in range(PLANES)])
+        rows = pl.ds(pl.multiple_of(block * 256, 256), 256)
+        outs.append(
+            Spread(
+                links,
+                out_piece if slot == 0 else out_ref.at[rows, columns_of(place)],
+                lambda piece, rows=rows: out_ref.at[rows, columns_of(piece)],
+                (2, 4) if slot % 2 else (4, 2),
+            )
+        )
     slots = [
         halved_spread(
             links,
@@ -715,9 +724,11 @@
     square_ref[...] = jnp.zeros_like(square_ref)
     attn.two()
     attn.three()
+    outs[0].one()
     slots[0].one()
     rope_tables_from(seg_ref, cos_at, sin_at, cos_ref, sin_ref, begin_ref, marks)
     attn.end()
+    outs[0].two()
     for copy in (own_hidden, own_attn, own_out, own_feed):
         copy.wait()
     store(weight_ref, weight_out)
@@ -765,8 +776,11 @@
     feeds.send(1, ends)
     thin.take(1)
     thin.send(2)
+    outs[1].one()
+    outs[0].three()
     slots[0].two()
     project_hop(1)
+    outs[1].two()
     wide.take(2)
     wide.send(3)
     feeds.take(1, inner)
@@ -774,7 +788,10 @@
     feeds.send(2, inner)
     thin.take(2)
     thin.send(3)
+    outs[2].one()
+    outs[1].three()
     project_hop(2)
+    outs[2].two()
     slots[0].three()
     wide.take(3)
     wide.left(3, (1, PLANES - 2))
@@ -783,8 +800,10 @@
     feeds.send(1, (1, PLANES - 2))
     second = feeds.plan(2, (1, PLANES - 2))
     thin.take(3)
-    outs.one()
+    outs[3].one()
+    outs[2].three()
     project_hop(3)
+    outs[3].two()
     store(n_ref, n_out)
     store(q_ref, q_out)
     store(k_ref, k_out)
@@ -850,7 +869,7 @@
     def pump_a():
         feeds.take(1, near)
         slots[1].one()
-        outs.two()
+        outs[3].three()
 
     def pump_b():
         slots[1].two()
@@ -862,16 +881,16 @@
     def pump_c():
         feeds.take(2, near)
         slots[2].one()
-        outs.three()
 
     pumps = ((0, pump_a), (1, pump_b), (2, pump_c))
 
     def flash(index, carried):
         step = PLANES - 1 - index
         flash_block(lax.rem(depth + step, PLANES))
-        pl.when(step > 0)(lambda: hand(step).start())
+        pl.when((step > 0) & (step < PLANES - 1))(lambda: hand(step).start())
         for when, pump in pumps:
             pl.when(index == when)(pump)
+        pl.when(index == 1)(lambda: hand(PLANES - 1).start())
         return carried
 
     lax.fori_loop(0, PLANES, flash, 0)
@@ -879,7 +898,8 @@
     own_rows = pl.ds(pl.multiple_of(depth * shard, shard), shard)
     attended_ref[:, columns_of(depth, 256)] = o_ref[own_rows, :]
     store(o_ref, o_out)
-    outs.end()
+    for part in outs:
+        part.end()
     store(out_ref, out_weight_out)
     slots[2].two()
     for step in range(1, PLANES):

time: 366 us -> 357 us (0.975)
  Pallas kernels: 348 us -> 339 us
    pallas_call x1, Pallas kernels: 149 us -> 139 us  [opening(): pl.pallas_call(open_kernel, in_specs=[any_spec] * 4 + [vmem] * 4, out_spe...]
where the time goes in v7:
time: 357 us; the launch traced here: 353 us
  Pallas kernels  339 us (95%)
  local copies, waits for them, and re-layouts  6.88 us (2%)
  other arithmetic  5.45 us (2%)
    pallas_call x1, Pallas kernels, closing(): pl.pallas_call(close_kernel, in_specs=[any_spec] * 15 + [vmem] * 4, out_s...  140 us
    pallas_call x1, Pallas kernels, opening(): pl.pallas_call(open_kernel, in_specs=[any_spec] * 4 + [vmem] * 4, out_spe...  139 us
    pallas_call x1, Pallas kernels, feed(): pl.pallas_call(feed_kernel, in_specs=[vmem, vmem, vmem, any_spec], out_sp...  45.5 us
    pallas_call x1, Pallas kernels, update(): pl.pallas_call(update_kernel, out_shape=[shape(dm.shape, full), shape((8,...  8.37 us

profile of v7, /device:TPU:0, one launch (start us, length us, event | category | flops | bytes accessed | tf_op | source)
XLA Modules:
  0.0 352.6 jit_solution(5843066729128603341)
XLA Ops:
  0.7 0.0 copy-start.1
  0.7 0.0 copy-start.4
  0.7 0.0 copy-start.3
  0.7 1.2 convert_element_type.18
  1.9 1.0 convert_element_type.19
  2.9 0.8 pad_maximum_fusion.refs_3_
  3.8 0.0 copy-done.1
  3.8 0.2 copy.41
  4.0 0.1 pad.8.clone
  4.0 0.0 copy-done.4
  4.0 0.9 maximum_maximum_fusion.refs_1_
  4.9 0.0 copy-done.3
  4.9 0.6 convert_element_type.17.refs_2_
  5.5 139.3 %opening.1 = (bf16[2048,256]{1,0:T(8,128)(2,1)}, bf16[2048,256]{1,0:T(8,128)(2,1)}, bf16[2048,256]{1,0:T(8,128)(2,1)}, bf16[2048,256]{1,0:T(8,128)(2,1)}, bf16[2...) custom-call(bf16[512,1024]{1,0:T(8,128)(2,1)} %bitcast.21, ...), custom_call_target="tpu_custom_call" | custom-call | tf_op jit(solution)/shard_map/opening/pallas_call | solution.py:935
  144.8 45.5 %feed.1 = (f32[512,1024]{1,0:T(8,128)}, bf16[512,1024]{1,0:T(8,128)(2,1)}, bf16[4,4,2112,128]{3,2,1,0:T(8,128)(2,1)}) custom-call(bf16[512,1024]{1,0:T(8,128)(2,1)} %get-tuple-element.69.refs_0_, bf16[512,1024]{1,0:T(8,128)(2,1)} %bitcast.23, f32[512,1024]{1,0:T(8,128)} %get-tuple-element.70.refs_2_.refs_0_, bf16[4,8,2112,128]{3,2,1,0:T(8,128)(2,1)} %get-tuple-element.71.refs_3_), custom_call_target="tpu_custom_call" | custom-call | tf_op jit(solution)/shard_map/feed/pallas_call | solution.py:1142
  190.3 6.5 %middle_back.1 = (bf16[512,1024]{1,0:T(8,128)(2,1)}, f32[512,1024]{1,0:T(8,128)}, f32[8,1024]{1,0:T(8,128)}, bf16[512,256]{1,0:T(8,128)(2,1)}, bf16[512,256]{1,0...) custom-call(f32[512,1024]{1,0:T(8,128)} %get-tuple-element.70.refs_2_.refs_0_, ...), custom_call_target="tpu_custom_call" | custom-call | flops 1073741824 | bytes 12582912 | tf_op jit(solution)/shard_map/middle_back/pallas_call | solution.py:1736
  196.8 0.8 slice.12
  197.6 0.8 slice_reduce_fusion
  198.4 0.1 pad.2.clone
  198.5 0.1 pad.3.clone
  198.6 0.1 maximum_maximum_fusion.1
  198.6 0.6 broadcast_in_dim.35.refs_18_
  199.3 139.6 %closing.1 = (f32[2048,256]{1,0:T(8,128)}, f32[512,1024]{1,0:T(8,128)}, f32[2112,128]{1,0:T(8,128)}, f32[256,128]{1,0:T(8,128)}, f32[768,128]{1,0:T(8,128)}, /*index=5*/f32[5,24,128]{2,1,0:T(8,128)}) custom-call(bf16[4,4,2112,128]{3,2,1,0:T(8,128)(2,1)} %get-tuple-element.77.refs_0_, bf16[512,1024]{1,0:T(8,128)(2,1)} %get-tuple-element.78.refs_1_, ...), custom_call_target="tpu_custom_call" | custom-call | tf_op jit(solution)/shard_map/closing/pallas_call | solution.py:1662
  338.9 1.3 slice_bitcast_fusion.refs_7_
  340.2 0.0 copy-start.2
  340.2 8.4 %update.1 = (f32[512,1024]{1,0:T(8,128)}, f32[8,128]{1,0:T(8,128)}, f32[3,128,256]{2,1,0:T(8,128)}, f32[256,128]{1,0:T(8,128)}, f32[2,704,128]{2,1,0:T(8,128)}, ...) custom-call(bf16[512,1024]{1,0:T(8,128)(2,1)} %bitcast.22, ...), custom_call_target="tpu_custom_call" | custom-call | bytes 16777216 | tf_op jit(solution)/shard_map/update/pallas_call | solution.py:1799
  348.6 0.0 copy-start
  348.6 1.5 slice_reduce_fusion.1
  350.1 0.0 copy-done.2
  350.1 1.0 copy.44
  351.0 0.0 copy-done
  351.0 1.3 copy.45
  (6 shorter events, 0.0 us)
Async XLA Ops:
  0.7 3.1 copy-start.1
  0.7 3.4 copy-start.4
  0.7 4.2 %copy-start.3 = (f32[256,128]{1,0:T(8,128)S(1)}, f32[256,128]{1,0:T(8,128)}, u32[]{:S(2)}) copy-start(f32[256,128]{1,0:T(8,128)} %refs_9_.1) | copy-start | bytes 393220
  340.2 9.8 %copy-start.2 = (bf16[512,1024]{1,0:T(8,128)(2,1)S(1)}, bf16[512,1024]{1,0:T(8,128)(2,1)}, u32[]{:S(2)}) copy-start(bf16[512,1024]{1,0:T(8,128)(2,1)} %get-tuple-element.72) | copy-start | bytes 3145732
  348.6 2.4 copy-start

commit v8 on v7

--- a/solution.py
+++ b/solution.py
@@ -1305,14 +1305,14 @@
 def close_kernel(*refs):
     (made, low_in, attended_in, q_in, k_in, v_in, o_in, n_in, weight_in, cos_in, sin_in) = refs[:11]
     incoming = refs[11:15]
-    log_ref, begin_ref, gain_ref, small_in = refs[15:19]
-    first_ref, back_ref, feed_total, out_total, attn_total, small_ref = refs[19:25]
+    log_ref, begin_ref, gain_ref, gain_two_ref, square_ref = refs[15:20]
+    first_ref, back_ref, feed_total, out_total, attn_total, small_ref = refs[20:26]
     (
         q_ref, k_ref, v_ref, o_ref, weight_ref, cos_ref, sin_ref, grad, inner, query_acc, key_acc, made_ref,
         stay, feed_first, feed_final, feed_held, out_made, out_core, out_first, out_final, out_held,
         attn_core, attn_first, attn_final, partial, partial_held, small_got,
         send, recv, local,
-    ) = refs[25:]
+    ) = refs[26:]
     links = Links(send, recv)
     place, depth = links.place, links.depth
     length = q_ref.shape[0]
@@ -1578,7 +1578,12 @@
     quarter_loads = [
         load(n_in.at[:, pl.ds(index * 256, 256)], quarter) for index, quarter in enumerate(quarters)
     ]
-    small_ref[...] = small_in[...]
+    small_ref[...] = jnp.zeros_like(small_ref)
+    for piece in range(8):
+        small_ref[0, 8 + piece : 9 + piece, :] = gain_two_ref[0:1, piece * PIECE : piece * PIECE + PIECE]
+    for which in range(2):
+        whole_sum = jnp.sum(square_ref[which : which + 1, :], axis=1, keepdims=True)
+        small_ref[0, 16 + which : 17 + which, :] = jnp.broadcast_to(whole_sum, (1, PIECE))
     line.take(1)
     line.forward(2)
     for copy in quarter_loads:
@@ -1652,7 +1657,7 @@
     links.drain()
 
 
-def closing(made, low_ref, attended_own, heads, normed, weight, tables, incoming, logs, begin_row, gains, small):
+def closing(made, low_ref, attended_own, heads, normed, weight, tables, incoming, logs, begin_row, gains, gain_two, squares):
     length, width = heads[0].shape
     rows = low_ref.shape[0]
     count = made.shape[2]
@@ -1661,7 +1666,7 @@
     shape = jax.ShapeDtypeStruct
     return pl.pallas_call(
         close_kernel,
-        in_specs=[any_spec] * 15 + [vmem] * 4,
+        in_specs=[any_spec] * 15 + [vmem] * 5,
         out_specs=[vmem] * 6,
         out_shape=[
             shape((length, width), full),
@@ -1704,7 +1709,7 @@
             vmem_limit_bytes=CLOSE_VMEM, collective_id=3, has_side_effects=True
         ),
         name="closing",
-    )(made, low_ref, attended_own, *heads, normed, weight, *tables, *incoming, logs, begin_row, gains, small)
+    )(made, low_ref, attended_own, *heads, normed, weight, *tables, *incoming, logs, begin_row, gains, gain_two, squares)
 
 
 def middle_back_kernel(*refs):
@@ -1763,7 +1768,7 @@
     factor = rms_factor(hidden)
     grad_ref[...] = dm_ref[...] + norm_back(hidden, factor, gain_ref[0:1, :], back_ref[...])[0]
     tokens = 8.0 * hidden_ref.shape[0] * PLANES
-    norm_ref[...] = jnp.sqrt(small_ref[16:24, :] / (tokens * D))
+    norm_ref[...] = jnp.sqrt(small_ref[4, 16:24, :] / (tokens * D))
     every = slice(None)
     rates = (D**-0.5, max(1, 8 * HEADS * HD // LEN) ** -0.5, D**-0.5, (FF // 3) ** -0.5)
 
@@ -1783,7 +1788,7 @@
         at = pl.ds(which, 1)
         stepped(
             masters[4],
-            small_ref[pl.ds(8 * which + place, 1), :],
+            small_ref[4, pl.ds(8 * which + place, 1), :],
             moments[4],
             squares[4],
             0.2,
@@ -1870,14 +1875,6 @@
     branch_low, middle_grad, gain_two, *out_grads = middle_back(
         middle, out_cotangent, normed_two_grad, out_weight, gains
     )
-    small = jnp.concatenate(
-        [
-            jnp.zeros((8, PIECE), jnp.float32),
-            gain_two[0].reshape(8, PIECE),
-            jnp.broadcast_to(jnp.sum(squares[:2], axis=1)[:, None], (2, PIECE)),
-            jnp.zeros((6, PIECE), jnp.float32),
-        ]
-    )
     values_grad, normed_grad, feed_total, out_total, attn_total, small = closing(
         made,
         branch_low,
@@ -1890,9 +1887,9 @@
         logs,
         begin_row,
         gains,
-        jnp.broadcast_to(small[None], (5, 24, PIECE)),
-    )
-    small = small[4]
+        gain_two,
+        squares,
+    )
     masters = [input_proj, output_proj, expand_proj, reduce_proj, norm_gains]
     moments = [
         old_moment_input,

time: 357 us -> 355 us (level)
  no operation moved by 1% of the time
where the time goes in v8:
time: 355 us; the launch traced here: 350 us
  Pallas kernels  339 us (95%)
  other arithmetic  6.05 us (2%)
  local copies, waits for them, and re-layouts  4.01 us (1%)
    pallas_call x1, Pallas kernels, closing(): pl.pallas_call(close_kernel, in_specs=[any_spec] * 15 + [vmem] * 5, out_s...  140 us
    pallas_call x1, Pallas kernels, opening(): pl.pallas_call(open_kernel, in_specs=[any_spec] * 4 + [vmem] * 4, out_spe...  139 us
    pallas_call x1, Pallas kernels, feed(): pl.pallas_call(feed_kernel, in_specs=[vmem, vmem, vmem, any_spec], out_sp...  45.6 us
    pallas_call x1, Pallas kernels, update(): pl.pallas_call(update_kernel, out_shape=[shape(dm.shape, full), shape((8,...  8.45 us

profile of v8, /device:TPU:0, one launch (start us, length us, event | category | flops | bytes accessed | tf_op | source)
XLA Modules:
  0.0 350.5 jit_solution(16978424225595519793)
XLA Ops:
  0.7 0.0 copy-start
  0.7 0.8 convert_element_type.16
  1.4 0.1 pad.4.clone
  1.5 1.5 convert_element_type.17.refs_2_
  3.0 1.0 convert_element_type.19
  4.0 1.0 convert_bitcast_fusion
  5.1 0.2 copy.41
  5.2 0.9 maximum_maximum_fusion.refs_1_
  6.1 0.0 copy-done
  6.1 0.8 pad_maximum_fusion.refs_3_
  7.0 139.2 %opening.1 = (bf16[2048,256]{1,0:T(8,128)(2,1)}, bf16[2048,256]{1,0:T(8,128)(2,1)}, bf16[2048,256]{1,0:T(8,128)(2,1)}, bf16[2048,256]{1,0:T(8,128)(2,1)}, bf16[2...) custom-call(bf16[512,1024]{1,0:T(8,128)(2,1)} %bitcast.18, ...), custom_call_target="tpu_custom_call" | custom-call | tf_op jit(solution)/shard_map/opening/pallas_call | solution.py:935
  146.2 45.6 %feed.1 = (f32[512,1024]{1,0:T(8,128)}, bf16[512,1024]{1,0:T(8,128)(2,1)}, bf16[4,4,2112,128]{3,2,1,0:T(8,128)(2,1)}) custom-call(bf16[512,1024]{1,0:T(8,128)(2,1)} %get-tuple-element.69.refs_0_, bf16[512,1024]{1,0:T(8,128)(2,1)} %bitcast.20, f32[512,1024]{1,0:T(8,128)} %get-tuple-element.70.refs_2_.refs_0_, bf16[4,8,2112,128]{3,2,1,0:T(8,128)(2,1)} %get-tuple-element.71.refs_3_), custom_call_target="tpu_custom_call" | custom-call | tf_op jit(solution)/shard_map/feed/pallas_call | solution.py:1142
  191.8 6.5 %middle_back.1 = (bf16[512,1024]{1,0:T(8,128)(2,1)}, f32[512,1024]{1,0:T(8,128)}, f32[8,1024]{1,0:T(8,128)}, bf16[512,256]{1,0:T(8,128)(2,1)}, bf16[512,256]{1,0...) custom-call(f32[512,1024]{1,0:T(8,128)} %get-tuple-element.70.refs_2_.refs_0_, ...), custom_call_target="tpu_custom_call" | custom-call | flops 1073741824 | bytes 12582912 | tf_op jit(solution)/shard_map/middle_back/pallas_call | solution.py:1741
  198.2 139.7 %closing.1 = (f32[2048,256]{1,0:T(8,128)}, f32[512,1024]{1,0:T(8,128)}, f32[2112,128]{1,0:T(8,128)}, f32[256,128]{1,0:T(8,128)}, f32[768,128]{1,0:T(8,128)}, /*index=5*/f32[5,24,128]{2,1,0:T(8,128)}) custom-call(bf16[4,4,2112,128]{3,2,1,0:T(8,128)(2,1)} %get-tuple-element.77.refs_0_, bf16[512,1024]{1,0:T(8,128)(2,1)} %get-tuple-element.78.refs_1_, ...), custom_call_target="tpu_custom_call" | custom-call | tf_op jit(solution)/shard_map/closing/pallas_call | solution.py:1667
  338.0 0.0 copy-start.2
  338.0 8.5 %update.1 = (f32[512,1024]{1,0:T(8,128)}, f32[8,128]{1,0:T(8,128)}, f32[3,128,256]{2,1,0:T(8,128)}, f32[256,128]{1,0:T(8,128)}, f32[2,704,128]{2,1,0:T(8,128)}, ...) custom-call(bf16[512,1024]{1,0:T(8,128)(2,1)} %bitcast.19, ...), custom_call_target="tpu_custom_call" | custom-call | bytes 16777216 | tf_op jit(solution)/shard_map/update/pallas_call | solution.py:1804
  346.4 0.0 copy-start.1
  346.4 1.5 slice_reduce_fusion
  347.9 0.0 copy-done.2
  347.9 1.0 copy.44
  348.9 0.0 copy-done.1
  348.9 1.3 copy.45
  (2 shorter events, 0.1 us)
Async XLA Ops:
  0.7 5.4 %copy-start = (f32[2,128,704]{1,2,0:T(8,128)S(1)}, f32[2,128,704]{1,2,0:T(8,128)}, u32[]{:S(2)}) copy-start(f32[2,128,704]{1,2,0:T(8,128)} %param.27) | copy-start | bytes 2162692
  338.0 9.9 %copy-start.2 = (bf16[512,1024]{1,0:T(8,128)(2,1)S(1)}, bf16[512,1024]{1,0:T(8,128)(2,1)}, u32[]{:S(2)}) copy-start(bf16[512,1024]{1,0:T(8,128)(2,1)} %get-tuple-element.72) | copy-start | bytes 3145732
  346.4 2.4 copy-start.1
